TPU v7x, 32 devices: a whole 2x2x4 slice. The times are simulated.
32 devices in a mesh: group: 1, image: 4 (over z), prow: 4 (over y, x), pcol: 2 (over core).
Axes of the slice: x: 2, y: 2, z: 4, core: 2. Of those that a mesh axis runs over, the one named last changes fastest.
Arguments:
- latent: bfloat16 [4, 32, 64, 640], P(('group', 'image'), 'prow', 'pcol'), may hold values from -6 to 6
- conv_weight: bfloat16 [3, 3, 640, 640], replicated, may hold values from -0.078125 to 0.078125
- w_query: bfloat16 [640, 640], replicated, may hold values from -2 to 2
- w_key: bfloat16 [640, 640], replicated, may hold values from -2 to 2
- w_value: bfloat16 [640, 640], replicated, may hold values from -0.25 to 0.25
- w_out: bfloat16 [640, 640], replicated, may hold values from -0.25 to 0.25
- anchor_index: int32 [4], P('group'), may hold values from 0 to 3, as said below
- block_order: int32 [4, 16], P('group'), may hold values from 0 to 15, each once within a row
- block_count: int32 [4], P('group'), may hold values from 1 to 4, as said below
Outputs:
- features: bfloat16 [4, 32, 64, 640], P(('group', 'image'), 'prow', 'pcol')
- attended: bfloat16 [4, 32, 64, 640], P(('group', 'image'), 'prow', 'pcol')
Inputs may be any that keep to these rules, and one draw needn't show every extreme that they name: `anchor_index`: 4 different images of the batch. `block_count`: some anchor has 4 subject blocks.
All inputs are finite; a program needn't handle non-finite values.
Results may differ from a plain program's by a relative error of at most 0.017.
Values may be sent and summed in bfloat16 or wider, within the bound.
No kernel may reach another device: no remote copies, remote signals or barrier semaphores. Data moves between devices by JAX's collectives and lax.ppermute only.
A program may use at most 128 MiB of HBM per device.

v0:
```python
import functools

import jax
import jax.numpy as jnp
from jax import lax
from jax.experimental import pallas as pl
from jax.experimental.pallas import tpu as pltpu
from jax.sharding import PartitionSpec as P

HEAD_DIM = 64
BLOCK = 128
NSEL = 4
LANES = 128
SUBLANES = 8
ONES = 16
F32 = jnp.float32
BF16 = jnp.bfloat16
MIB = 1 << 20


VMEM = pl.BlockSpec(memory_space=pltpu.VMEM)
SMEM = pl.BlockSpec(memory_space=pltpu.SMEM)
HBM = pl.BlockSpec(memory_space=pltpu.HBM)


def shape(*dims, dtype=BF16):
    return jax.ShapeDtypeStruct(dims, dtype)


def cost(flops, moved, exps=0):
    return pl.CostEstimate(flops=flops, bytes_accessed=moved, transcendentals=exps)


def grant(mib):
    return pltpu.CompilerParams(vmem_limit_bytes=mib * MIB)


def source_of(index, step, count):
    if count & (count - 1) == 0:
        return index ^ step
    return lax.rem(index + step, count) if not isinstance(index, int) else (index + step) % count


def target_of(index, step, count):
    if count & (count - 1) == 0:
        return index ^ step
    return lax.rem(index - step + count, count)


def step_of(index, source, count):
    if count & (count - 1) == 0:
        return index ^ source
    return lax.rem(source - index + count, count)


def exchange(block, axis, step):
    count = lax.axis_size(axis)
    return lax.ppermute(block, axis, [(source_of(i, step, count), i) for i in range(count)])


def shifted(block, axis, step):
    count = lax.axis_size(axis)
    return lax.ppermute(block, axis, [((i + step) % count, i) for i in range(count)])


def halo(cells):
    core, cores = lax.axis_index("pcol"), lax.axis_size("pcol")
    rows, cols = lax.axis_size("prow"), cells.shape[1]
    if cores == 2:
        inner = lax.dynamic_index_in_dim(cells, jnp.where(core == 0, cols - 1, 0), 1, keepdims=False)
        other = shifted(inner, "pcol", 1)
        zero = jnp.zeros_like(other)
        left = jnp.where(core == 1, other, zero)
        right = jnp.where(core == 0, other, zero)
    else:
        left = lax.ppermute(cells[:, -1], "pcol", [(i, i + 1) for i in range(cores - 1)])
        right = lax.ppermute(cells[:, 0], "pcol", [(i + 1, i) for i in range(cores - 1)])
    low = jnp.concatenate([cells[-1], left[-1:], right[-1:]], axis=0)
    high = jnp.concatenate([cells[0], left[:1], right[:1]], axis=0)
    odd = lax.rem(lax.axis_index("prow"), 2) == 1
    swaps = []
    for first in range(2):
        pairs = [(i, i + 1) for i in range(first, rows - 1, 2)]
        block = jnp.where(odd, high, low) if first == 0 else jnp.where(odd, low, high)
        swaps.append(lax.ppermute(block, "prow", pairs + [(j, i) for i, j in pairs]))
    above = jnp.where(odd, swaps[0], swaps[1])
    below = jnp.where(odd, swaps[1], swaps[0])
    return left, right, above, below


def conv_kernel(rows, cols, cores, x_ref, left_ref, right_ref, above_ref, below_ref, w_ref, *refs):
    features_ref, *half_refs, shift0, shift1, shift2, taps, sem = refs
    copies = [
        pltpu.make_async_copy(w_ref.at[n // 3, n % 3], taps.at[n], sem.at[n]) for n in range(9)
    ]
    for copy in copies:
        copy.start()

    def silu(v):
        v = v.astype(F32)
        return (v / (1.0 + jnp.exp(-v))).astype(BF16).astype(F32)

    side = lax.broadcasted_iota(jnp.int32, (cols, x_ref.shape[1]), 0)
    for r in range(rows + 2):
        if r == 0 or r == rows + 1:
            ref = above_ref if r == 0 else below_ref
            cells, lcell, rcell = ref[:cols], ref[cols:cols + 1], ref[cols + 1:cols + 2]
        else:
            cells = x_ref[(r - 1) * cols:r * cols]
            lcell, rcell = left_ref[r - 1:r], right_ref[r - 1:r]
        cells, lcell, rcell = silu(cells), silu(lcell), silu(rcell)
        at = slice(r * cols, (r + 1) * cols)
        shift1[at] = cells.astype(BF16)
        shift0[at] = jnp.where(side == 0, lcell, pltpu.roll(cells, 1, 0)).astype(BF16)
        shift2[at] = jnp.where(side == cols - 1, rcell, pltpu.roll(cells, cols - 1, 0)).astype(BF16)
    total = x_ref[...].astype(F32)
    for a in range(3):
        for b, shift in enumerate((shift0, shift1, shift2)):
            copies[3 * a + b].wait()
            total = total + jnp.dot(
                shift[a * cols:(a + rows) * cols], taps[3 * a + b], preferred_element_type=F32
            )
    features = total.astype(BF16)
    features_ref[...] = features
    values = features.astype(F32)
    centered = values - jnp.mean(values, axis=-1, keepdims=True)
    spread = jnp.mean(centered * centered, axis=-1, keepdims=True)
    normed = (centered * lax.rsqrt(spread + 1e-05)).astype(BF16)
    core = lax.axis_index("pcol")
    per = BLOCK // cores
    for b in range(rows * cols // BLOCK):
        for h in range(cores):
            rows_of = normed[b * BLOCK + h * per:b * BLOCK + (h + 1) * per]
            for s, ref in enumerate(half_refs):
                @pl.when(lax.rem(core + s, cores) == h)
                def _():
                    ref[b * per:(b + 1) * per] = rows_of


def conv_norm(cells, sides, conv_weight, cores):
    rows, cols, channels = cells.shape
    tokens = rows * cols
    return pl.pallas_call(
        functools.partial(conv_kernel, rows, cols, cores),
        out_shape=(shape(tokens, channels),) + (shape(tokens // cores, channels),) * cores,
        in_specs=[VMEM] * 5 + [HBM],
        out_specs=(VMEM,) * (1 + cores),
        scratch_shapes=[pltpu.VMEM(((rows + 2) * cols, channels), BF16)] * 3 + [
            pltpu.VMEM((9, channels, channels), BF16), pltpu.SemaphoreType.DMA((9,)),
        ],
        compiler_params=grant(58),
        cost_estimate=cost(18 * tokens * channels**2, 18 * channels**2, tokens * channels),
        name="conv_norm",
    )(cells.reshape(tokens, channels), *sides, conv_weight)


class Table:
    def __init__(self, ref, anchors, images):
        self.ref, self.anchors, self.images = ref, anchors, images
        self.every_image = anchors == images

    @staticmethod
    def build(anchor_index, block_count, order):
        return jnp.concatenate([anchor_index, block_count, order.reshape(-1)])

    def anchor_at(self, image):
        found = jnp.int32(0)
        for a in range(1, self.anchors):
            found = jnp.where(self.ref[a] == image, a, found)
        return found

    def count(self, anchor):
        return self.ref[self.anchors + anchor]

    def block(self, anchor, slot):
        return self.ref[2 * self.anchors + anchor * NSEL + slot]

    def own_times(self, step, group, cores, prows, per_patch):
        if not self.every_image:
            return jnp.float32(1.0)
        s, b = divmod(group, per_patch)
        patch = source_of(lax.axis_index("prow"), step, prows) * cores
        block = (patch + lax.rem(lax.axis_index("pcol") + s, cores)) * per_patch + b
        anchor = self.anchor_at(lax.axis_index("image"))
        times = jnp.float32(1.0)
        for slot in range(NSEL):
            hit = (slot < self.count(anchor)) & (self.block(anchor, slot) == block)
            times = jnp.where(hit, 2.0, times)
        return times

    def anchor_times(self, source, slot):
        if self.every_image:
            image = source_of(lax.axis_index("image"), source + 1, self.images)
            source = self.anchor_at(image)
        return jnp.where(slot < self.count(source), 1.0, 0.0).astype(F32)


def project(normed, times, wk_ref, wvt_ref, k_scr, v_scr):
    keys, channels = normed.shape
    k = jnp.dot(normed, wk_ref[...], preferred_element_type=F32).astype(BF16)
    for pair in range(channels // LANES):
        k_scr[pair] = k[:, pair * LANES:(pair + 1) * LANES]
    v = lax.dot_general(
        wvt_ref[...], normed, (((1,), (1,)), ((), ())), preferred_element_type=F32
    )
    per = keys // len(times)
    lane = lax.broadcasted_iota(jnp.int32, (1, keys), 1)
    mult = jnp.full((1, keys), times[0], F32)
    for g in range(1, len(times)):
        mult = jnp.where(lane >= g * per, times[g], mult)
    v = (v * mult).astype(BF16)
    ones = jnp.broadcast_to(mult, (ONES, keys)).astype(BF16)
    for head in range(channels // HEAD_DIM):
        v_scr[head, :HEAD_DIM] = v[head * HEAD_DIM:(head + 1) * HEAD_DIM]
        v_scr[head, HEAD_DIM:] = ones


def attend_heads(q_ref, k_scr, v_scr, out_ref, level_ref, width):
    zeros = jnp.zeros((HEAD_DIM, width), BF16)
    items = [
        (head, slice(at, at + width))
        for head in range(q_ref.shape[0] // HEAD_DIM)
        for at in range(0, q_ref.shape[1], width)
    ]

    def scores_of(head, cols):
        q = q_ref[head * HEAD_DIM:(head + 1) * HEAD_DIM, cols]
        q = jnp.concatenate([q, zeros] if head % 2 == 0 else [zeros, q], axis=0)
        return jnp.dot(k_scr[head // 2], q, preferred_element_type=F32)

    ahead = scores_of(*items[0])
    for n, (head, cols) in enumerate(items):
        scores = ahead
        if n + 1 < len(items):
            ahead = scores_of(*items[n + 1])
        peak = jnp.max(scores, axis=0, keepdims=True)
        probs = jnp.exp(scores - peak).astype(BF16)
        value = jnp.dot(v_scr[head], probs, preferred_element_type=F32)
        total = value[HEAD_DIM:HEAD_DIM + 1]
        out_ref[head * HEAD_DIM:(head + 1) * HEAD_DIM, cols] = (
            value[:HEAD_DIM] * (1.0 / total)
        ).astype(out_ref.dtype)
        level_ref[head, :, cols] = jnp.broadcast_to(peak + jnp.log(total), (SUBLANES, width))


def own_kernel(info, n_parts, table_ref, *refs):
    anchors, images, cores, prows, per_patch = info
    part_refs, key_ref = refs[:n_parts], refs[n_parts]
    wq_ref, wk_ref, wv_ref, q_ref, out_ref, level_ref, k_scr, v_scr = refs[n_parts + 1:]
    table = Table(table_ref, anchors, images)
    at = 0
    for ref in part_refs:
        q = lax.dot_general(
            wq_ref[...], ref[...], (((1,), (1,)), ((), ())), preferred_element_type=F32
        ).astype(BF16)
        q_ref[:, at:at + ref.shape[0]] = (q.astype(F32) * HEAD_DIM ** (-0.5)).astype(BF16)
        at += ref.shape[0]
    times = [table.own_times(0, g, cores, prows, per_patch) for g in range(cores * per_patch)]
    project(key_ref[...], times, wk_ref, wv_ref, k_scr, v_scr)
    attend_heads(q_ref, k_scr, v_scr, out_ref, level_ref, part_refs[0].shape[0] * cores)


def key_scratch(keys, channels):
    return [
        pltpu.VMEM((channels // LANES, keys, LANES), BF16),
        pltpu.VMEM((channels // HEAD_DIM, HEAD_DIM + ONES, keys), BF16),
    ]


def attend_cost(rows, keys, channels, extra=0):
    return cost(
        4 * keys * channels**2 + 16 * rows * keys * channels + extra,
        2 * channels * (2 * rows + keys),
        rows * keys * channels // HEAD_DIM,
    )


def attend_own(info, table, parts, key, w_query, w_key, w_value):
    size, channels = key.shape
    rows = sum(part.shape[0] for part in parts)
    return pl.pallas_call(
        functools.partial(own_kernel, info, len(parts)),
        out_shape=(
            shape(channels, rows), shape(channels, rows),
            shape(channels // HEAD_DIM, SUBLANES, rows, dtype=F32),
        ),
        in_specs=[SMEM] + [VMEM] * (len(parts) + 4),
        out_specs=(VMEM,) * 3,
        scratch_shapes=key_scratch(size, channels),
        compiler_params=grant(24),
        cost_estimate=attend_cost(rows, size, channels, 2 * rows * channels**2),
        name="attend_own",
    )(table, *parts, key, w_query, w_key, w_value)


def plane_kernel(info, tiles, table_ref, q_ref, *refs):
    anchors, images, cores, prows, per_patch = info
    key_refs = refs[:tiles]
    wk_ref, wv_ref, out_ref, level_ref, k_scr, v_scr = refs[tiles:]
    table = Table(table_ref, anchors, images)
    times = [
        table.own_times(t + 1, g, cores, prows, per_patch)
        for t in range(tiles) for g in range(cores * per_patch)
    ]
    normed = jnp.concatenate([ref[...] for ref in key_refs], axis=0)
    project(normed, times, wk_ref, wv_ref, k_scr, v_scr)
    attend_heads(q_ref, k_scr, v_scr, out_ref, level_ref, q_ref.shape[1] // cores)


def attend_plane(info, table, queries, keys, w_key, w_value):
    size, channels = keys[0].shape
    rows = queries.shape[1]
    return pl.pallas_call(
        functools.partial(plane_kernel, info, len(keys)),
        out_shape=(
            shape(channels, rows), shape(channels // HEAD_DIM, SUBLANES, rows, dtype=F32),
        ),
        in_specs=[SMEM] + [VMEM] * (len(keys) + 3),
        out_specs=(VMEM,) * 2,
        scratch_shapes=key_scratch(size * len(keys), channels),
        compiler_params=grant(24),
        cost_estimate=attend_cost(rows, size * len(keys), channels),
        name="attend_plane",
    )(table, queries, *keys, w_key, w_value)


def merge_head(parts, head, cols):
    rows = slice(head * HEAD_DIM, (head + 1) * HEAD_DIM)
    levels = [level(head, cols) for _, level in parts]
    peak = functools.reduce(jnp.maximum, levels)
    weights = [jnp.exp(level - peak) for level in levels]
    total = functools.reduce(jnp.add, weights)
    value = functools.reduce(
        jnp.add, [w * ref[rows, cols].astype(F32) for w, (ref, _) in zip(weights, parts)]
    )
    return value * (1.0 / total), peak + jnp.log(total)


def anchor_kernel(info, tiles, earlier, groups, table_ref, q_ref, *refs):
    anchors, images, _, prows, _ = info
    key_refs, refs = refs[:tiles], refs[tiles:]
    early_refs, refs = refs[:2 * earlier], refs[2 * earlier:]
    wk_ref, wv_ref, *out_refs = refs[:2 + groups + 1]
    out_scr, level_scr, k_scr, v_scr = refs[3 + groups:]
    own_ref, own_level_ref, *sent_refs = out_refs
    table = Table(table_ref, anchors, images)
    if table.every_image:
        each = NSEL // prows
        times = [
            table.anchor_times(s, source_of(lax.axis_index("prow"), t, prows) * each + slot)
            for t in range(tiles) for s in range(images - 1) for slot in range(each)
        ]
    else:
        times = [table.anchor_times(t, slot) for t in range(tiles) for slot in range(NSEL)]
    normed = jnp.concatenate([ref[...] for ref in key_refs], axis=0)
    project(normed, times, wk_ref, wv_ref, k_scr, v_scr)
    channels = q_ref.shape[0]
    width = q_ref.shape[1] // groups
    attend_heads(q_ref, k_scr, v_scr, out_scr, level_scr, width)
    pairs = list(zip(early_refs[::2], early_refs[1::2])) + [(out_scr, level_scr)]
    parts = [
        (ref, lambda head, cols, level=level: level[head, 0:1, cols]) for ref, level in pairs
    ]
    heads = channels // HEAD_DIM
    row = lax.broadcasted_iota(jnp.int32, (2 * SUBLANES, width), 0)
    for n in range(groups):
        cols = slice(n * width, (n + 1) * width)
        ref = own_ref if n == 0 else sent_refs[n - 1]
        levels = jnp.zeros((2 * SUBLANES, width), F32)
        for head in range(heads):
            value, level = merge_head(parts, head, cols)
            ref[head * HEAD_DIM:(head + 1) * HEAD_DIM] = value.astype(BF16)
            levels = jnp.where(row == head, level, levels)
        if n == 0:
            own_level_ref[...] = levels
        else:
            for term in range(3):
                high = levels.astype(BF16)
                at = channels + term * 2 * SUBLANES
                ref[at:at + 2 * SUBLANES] = high
                levels = levels - high.astype(F32)


def attend_anchors(info, table, queries, keys, earlier, w_key, w_value, groups):
    size, channels = keys[0].shape
    rows = queries.shape[1]
    width = rows // groups
    flat = [leaf for part in earlier for leaf in part]
    heads = channels // HEAD_DIM
    return pl.pallas_call(
        functools.partial(anchor_kernel, info, len(keys), len(earlier), groups),
        out_shape=(shape(channels, width), shape(2 * SUBLANES, width, dtype=F32))
        + (shape(channels + 6 * SUBLANES, width),) * (groups - 1),
        in_specs=[SMEM] + [VMEM] * (len(keys) + len(flat) + 3),
        out_specs=(VMEM,) * (1 + groups),
        scratch_shapes=[
            pltpu.VMEM((channels, rows), BF16), pltpu.VMEM((heads, SUBLANES, rows), F32),
        ] + key_scratch(size * len(keys), channels),
        compiler_params=grant(24),
        cost_estimate=attend_cost(rows, size * len(keys), channels),
        name="attend_anchors",
    )(table, queries, *keys, *flat, w_key, w_value)


def finish_kernel(cores, own_ref, level_ref, *refs):
    *received, w_ref, out_ref, merged = refs
    channels, tokens = own_ref.shape

    def row_of(ref, base, terms):
        def level(head, cols):
            return functools.reduce(jnp.add, [
                ref[base + t * 2 * SUBLANES:base + (t + 1) * 2 * SUBLANES].astype(F32)
                for t in range(terms)
            ])[head:head + 1]

        return level

    parts = [(own_ref, row_of(level_ref, 0, 1))]
    parts += [(ref, row_of(ref, channels, 3)) for ref in received]
    every = slice(0, tokens)
    for head in range(channels // HEAD_DIM):
        value, _ = merge_head(parts, head, every)
        merged[head * HEAD_DIM:(head + 1) * HEAD_DIM] = value.astype(BF16)
    out = lax.dot_general(
        merged[...], w_ref[...], (((0,), (0,)), ((), ())), preferred_element_type=F32
    ).astype(BF16)
    core = lax.axis_index("pcol")
    per = BLOCK // cores
    blocks = tokens // BLOCK
    for s in range(cores):
        for b in range(blocks):
            at = b * BLOCK + lax.rem(core + s, cores) * per
            out_ref[pl.ds(pl.multiple_of(at, per), per)] = out[
                (s * blocks + b) * per:(s * blocks + b + 1) * per
            ]


def finish(own, level, received, w_out, cores):
    channels, tokens = own.shape
    return pl.pallas_call(
        functools.partial(finish_kernel, cores),
        out_shape=shape(tokens, channels),
        in_specs=[VMEM] * (3 + len(received)),
        out_specs=VMEM,
        scratch_shapes=[pltpu.VMEM((channels, tokens), BF16)],
        compiler_params=grant(16),
        cost_estimate=cost(2 * tokens * channels**2, 2 * channels * (channels + 3 * tokens)),
        name="finish",
    )(own, level, *received, w_out)


def slot_place(table, anchor, slot, info):
    cores, per_patch = info[2], info[4]
    per = BLOCK // cores
    block = table.block(anchor, jnp.where(slot < table.count(anchor), slot, 0))
    patch, inner = lax.div(block, per_patch), lax.rem(block, per_patch)
    part = lax.rem(lax.rem(patch, cores) - lax.axis_index("pcol") + cores, cores)
    return lax.div(patch, cores), pl.multiple_of((part * per_patch + inner) * per, per)


def offer_kernel(info, table_ref, key_ref, *out_refs):
    anchors, images, cores, prows, _ = info
    table = Table(table_ref, anchors, images)
    anchor = table.anchor_at(lax.axis_index("image"))
    per, each = BLOCK // cores, NSEL // prows
    for step, ref in enumerate(out_refs):
        target = target_of(lax.axis_index("prow"), step, prows)
        for n in range(each):
            _, at = slot_place(table, anchor, target * each + n, info)
            ref[n * per:(n + 1) * per] = key_ref[pl.ds(at, per)]


def offer(info, table, key):
    rows = NSEL // info[3] * (BLOCK // info[2])
    return pl.pallas_call(
        functools.partial(offer_kernel, info),
        out_shape=(shape(rows, key.shape[1]),) * info[3],
        in_specs=[SMEM, VMEM],
        out_specs=(VMEM,) * info[3],
        compiler_params=grant(8),
        name="offer",
    )(table, key)


def accept_kernel(info, table_ref, *refs):
    anchors, images, cores, prows, _ = info
    *offers, out_ref = refs
    table = Table(table_ref, anchors, images)
    anchor = table.anchor_at(lax.axis_index("image"))
    prow = lax.axis_index("prow")
    per, each = BLOCK // cores, NSEL // prows
    for n in range(each):
        holder, _ = slot_place(table, anchor, prow * each + n, info)
        rows = slice(n * per, (n + 1) * per)
        for step, ref in enumerate(offers):
            @pl.when(step_of(prow, holder, prows) == step)
            def _():
                out_ref[rows] = ref[rows]


def accept(info, table, offers):
    return pl.pallas_call(
        functools.partial(accept_kernel, info),
        out_shape=shape(*offers[0].shape),
        in_specs=[SMEM] + [VMEM] * len(offers),
        out_specs=VMEM,
        compiler_params=grant(8),
        name="accept",
    )(table, *offers)


def anchor_rows(key, anchor_index, block_order, block_count, cores, per_patch):
    per = BLOCK // cores
    live = jnp.arange(NSEL) < block_count[:, None]
    block = jnp.where(live, block_order[:, :NSEL], block_order[:, :1])
    patch = block // per_patch
    part = (patch % cores - lax.axis_index("pcol")) % cores
    rows = key.reshape(-1, per, key.shape[1])[part * per_patch + block % per_patch]
    held = (patch // cores == lax.axis_index("prow")) & (
        anchor_index == lax.axis_index("image"))[:, None]
    rows = jnp.where(held[..., None, None], rows, jnp.zeros_like(rows))
    return lax.psum(rows.reshape(len(block), NSEL * per, -1), ("image", "prow"))


def shards(
    latent, conv_weight, w_query, w_key, w_value, w_out, anchor_index, block_order, block_count
):
    tile_rows, tile_cols, _ = latent.shape[1:]
    cores, prows, images = (lax.axis_size(a) for a in ("pcol", "prow", "image"))
    anchors = anchor_index.shape[0]
    per_patch = tile_rows * tile_cols // BLOCK
    info = (anchors, images, cores, prows, per_patch)
    table = Table.build(anchor_index, block_count, block_order[:, :NSEL])
    sides, wq, wv = lax.optimization_barrier((halo(latent[0]), w_query.T, w_value.T))
    features, *parts = conv_norm(latent[0], sides, conv_weight, cores)
    keys, queries = [parts[0]], list(parts)
    for s in range(1, cores):
        theirs = [None] * cores
        for t in [cores - s] + [t for t in range(cores) if t != cores - s]:
            theirs[t] = shifted(parts[t], "pcol", s)
        keys.append(theirs[cores - s])
        queries += theirs
    key = jnp.concatenate(keys, axis=0)
    every_image = anchors == images
    if every_image:
        mine, *offers = offer(info, table, key)
        offers = [mine] + [exchange(rows, "prow", s) for s, rows in enumerate(offers, 1)]
    plane = [exchange(key, "prow", s) for s in range(1, prows)]
    q, value, level = attend_own(info, table, queries, key, wq, w_key, wv)
    done = [(value, level)]
    if every_image:
        share = accept(info, table, offers)
        across = []
        for s in range(1, images):
            across.append(exchange(share, "image", s))
        local = jnp.concatenate(across, axis=0)
        sources = [local] + [exchange(local, "prow", s) for s in range(1, prows)]
    else:
        joined = anchor_rows(key, anchor_index, block_order, block_count, cores, per_patch)
        sources = [joined[anchor] for anchor in range(anchors)]
    if plane:
        done.append(attend_plane(info, table, q, plane, w_key, wv))
    own, level, *sent = attend_anchors(info, table, q, sources, done, w_key, wv, cores)
    received = [shifted(block, "pcol", cores - s) for s, block in enumerate(sent, 1)]
    attended = finish(own, level, received, w_out, cores)
    return features.reshape(latent.shape), attended.reshape(latent.shape)


def solution(mesh):
    tiled = P(("group", "image"), "prow", "pcol", None)
    return jax.shard_map(
        shards,
        mesh=mesh,
        in_specs=(tiled, P(), P(), P(), P(), P(), P("group"), P("group", None), P("group")),
        out_specs=(tiled, tiled),
        check_vma=False,
    )
```

profile of v0, /device:TPU:0, one launch (start us, length us, event | category | flops | bytes accessed | tf_op | source)
XLA Modules:
  0.0 74.1 jit_solution(4693021214278541242)
XLA Ops:
  0.7 1.0 %constant_dynamic-slice_fusion = bf16[1,8,1,640]{3,2,1,0:T(2,128)(2,1)S(1)} fusion(bf16[1,8,32,640]{3,2,1,0:T(8,128)(2,1)} %param.9, s32[]{:T(128)S(6)} %select_n.41), kind=kLoop, calls=%fused_computation.17 | loop fusion | bytes 20484 | tf_op jit(solution)/shard_map/jit(dynamic_index_in_dim)/dynamic_slice | solution.py:70
  2.2 0.8 %slice_bitcast_fusion.1 = (bf16[32,640]{1,0:T(8,128)(2,1)S(1)}, bf16[32,640]{1,0:T(8,128)(2,1)S(1)}) fusion(bf16[1,8,32,640]{3,2,1,0:T(8,128)(2,1)} %param.9), kind=kLoop, calls=%fused_computation.7 | loop fusion | bytes 163840 | tf_op jit(solution)/shard_map/squeeze | solution.py:79
  3.1 2.9 %collective-permute-start.1 = (bf16[34,640]{1,0:T(8,128)(2,1)S(1)}, bf16[34,640]{1,0:T(8,128)(2,1)S(1)}, u32[]{:S(2)}, u32[]{:S(2)}) collective-permute-start(bf16[34,640]{1,0:T(8,128)(2,1)S(1)} %get-tuple-element.49), channel_id=1, source_target_pairs={{0,2},{4,6},{2,0},{6,4},{1,3},{5,7},{3,1},{7,5},{8,10},{12,14},{10... | collective-permute-start | bytes 130568 | tf_op jit(solution)/shard_map/ppermute | solution.py:85
  6.7 1.8 %copy.14 = bf16[640,640]{0,1:T(8,128)(2,1)S(1)} copy(bf16[640,640]{1,0:T(8,128)(2,1)} %param.11) | data formatting | bytes 1638400 | tf_op args[2]
  8.5 1.8 %copy.15 = bf16[640,640]{0,1:T(8,128)(2,1)S(1)} copy(bf16[640,640]{1,0:T(8,128)(2,1)} %param.13) | data formatting | bytes 1638400 | tf_op args[4]
  11.8 7.5 %conv_norm.1 = (bf16[256,640]{1,0:T(8,128)(2,1)}, bf16[128,640]{1,0:T(8,128)(2,1)}, bf16[128,640]{1,0:T(8,128)(2,1)}) custom-call(bf16[256,640]{1,0:T(8,128)(2,1)} %bitcast.17, bf16[8,640]{1,0:T(8,128)(2,1)} %copy-done.5, bf16[8,640]{1,0:T(8,128)(2,1)} %copy-done.4, bf16[34,640]{1,0:T(8,128)(2,1)} %get-tuple-element.25.above_ref, ...), custom_call_target="tpu_custom_call" | custom-call | flops 1887436800 | bytes 7372800 | tf_op jit(solution)/shard_map/conv_norm/pallas_call | solution.py:143
  19.9 0.9 %constant_dynamic-update-slice_fusion.1 = bf16[256,640]{1,0:T(8,128)(2,1)S(1)} fusion(bf16[128,640]{1,0:T(8,128)(2,1)} %get-tuple-element.28.refs_0_), kind=kLoop, calls=%fused_computation.9 | loop fusion | bytes 327680
  21.6 4.3 %collective-permute-start.5 = (bf16[64,640]{1,0:T(8,128)(2,1)S(1)}, bf16[64,640]{1,0:T(8,128)(2,1)S(1)}, u32[]{:S(2)}, u32[]{:S(2)}) collective-permute-start(bf16[64,640]{1,0:T(8,128)(2,1)S(1)} %get-tuple-element.34), channel_id=1, source_target_pairs={{2,0},{0,2},{6,4},{4,6},{3,1},{1,3},{7,5},{5,7},{10,8},{8,10},{14,... | collective-permute-start | bytes 245768 | tf_op jit(solution)/shard_map/ppermute | solution.py:58
  25.9 1.5 %collective-permute-start.7 = (bf16[64,640]{1,0:T(8,128)(2,1)S(1)}, bf16[64,640]{1,0:T(8,128)(2,1)S(1)}, u32[]{:S(2)}, u32[]{:S(2)}) collective-permute-start(bf16[64,640]{1,0:T(8,128)(2,1)S(1)} %get-tuple-element.36), channel_id=1, source_target_pairs={{6,0},{4,2},{2,4},{0,6},{7,1},{5,3},{3,5},{1,7},{14,8},{12,10},{10... | collective-permute-start | bytes 245768 | tf_op jit(solution)/shard_map/ppermute | solution.py:58
  27.4 1.9 %collective-permute-start.14 = (bf16[256,640]{1,0:T(8,128)(2,1)S(1)}, bf16[256,640]{1,0:T(8,128)(2,1)S(1)}, u32[]{:S(2)}, u32[]{:S(2)}) collective-permute-start(bf16[256,640]{1,0:T(8,128)(2,1)S(1)} %constant_dynamic-update-slice_fusion.refs_4_.key_ref), channel_id=1, source_target_pairs={{2,0},{0,2},{6,4},{4,6},{3,1},{1,3},{7,5},{5,7},{10,8},{8,10},{14,... | collective-permute-start | bytes 983048 | tf_op jit(solution)/shard_map/ppermute | solution.py:58
  29.4 2.8 %collective-permute-done.6.refs_2_ = bf16[64,640]{1,0:T(8,128)(2,1)S(1)} collective-permute-done((bf16[64,640]{1,0:T(8,128)(2,1)S(1)}, bf16[64,640]{1,0:T(8,128)(2,1)S(1)}, u32[]{:S(2)}, u32[]{:S(2)}) %collective-permute-start.6) | collective-permute-done | bytes 81952 | tf_op jit(solution)/shard_map/ppermute | solution.py:58
  33.1 1.6 %collective-permute-start.8 = (bf16[64,640]{1,0:T(8,128)(2,1)S(1)}, bf16[64,640]{1,0:T(8,128)(2,1)S(1)}, u32[]{:S(2)}, u32[]{:S(2)}) collective-permute-start(bf16[64,640]{1,0:T(8,128)(2,1)S(1)} %accept.1), channel_id=1, source_target_pairs={{8,0},{0,8},{24,16},{16,24},{9,1},{1,9},{25,17},{17,25},{10,2},{2,... | collective-permute-start | bytes 245768 | tf_op jit(solution)/shard_map/ppermute | solution.py:58
  34.8 0.9 %copy-done.1 = bf16[128,640]{1,0:T(8,128)(2,1)S(1)} copy-done((bf16[128,640]{1,0:T(8,128)(2,1)S(1)}, bf16[128,640]{1,0:T(8,128)(2,1)}, u32[]{:S(2)}) %copy-start.1) | copy-done | bytes 163864
  35.7 0.9 %copy-done.3 = bf16[128,640]{1,0:T(8,128)(2,1)S(1)} copy-done((bf16[128,640]{1,0:T(8,128)(2,1)S(1)}, bf16[128,640]{1,0:T(8,128)(2,1)}, u32[]{:S(2)}) %copy-start.3) | copy-done | bytes 163864
  36.6 4.9 %attend_own.1 = (bf16[640,512]{1,0:T(8,128)(2,1)S(1)}, bf16[640,512]{1,0:T(8,128)(2,1)S(1)}, f32[10,8,512]{2,1,0:T(8,128)S(1)}) custom-call(s32[24]{0:T(128)S(1)} %pad_add_fusion.table_ref, bf16[128,640]{1,0:T(8,128)(2,1)S(1)} %copy-done.1, bf16[128,640]{1,0:T(8,128)(2,1)S(1)} %copy-done.3, bf16[128,640]{1,0:T(8,128)(2,1)S(1)} %collective-permute-done.3.refs_2_, ...), custom_call_target="tpu_custom_call" | custom-call | flops 2181038080 | bytes 1638400 | tf_op jit(solution)/shard_map/attend_own/pallas_call | solution.py:281
  41.5 2.7 %collective-permute-start.9 = (bf16[64,640]{1,0:T(8,128)(2,1)S(1)}, bf16[64,640]{1,0:T(8,128)(2,1)S(1)}, u32[]{:S(2)}, u32[]{:S(2)}) collective-permute-start(bf16[64,640]{1,0:T(8,128)(2,1)S(1)} %accept.1), channel_id=1, source_target_pairs={{16,0},{24,8},{0,16},{8,24},{17,1},{25,9},{1,17},{9,25},{18,2},{26... | collective-permute-start | bytes 245768 | tf_op jit(solution)/shard_map/ppermute | solution.py:58
  44.4 4.2 %collective-permute-done.9 = bf16[64,640]{1,0:T(8,128)(2,1)S(1)} collective-permute-done((bf16[64,640]{1,0:T(8,128)(2,1)S(1)}, bf16[64,640]{1,0:T(8,128)(2,1)S(1)}, u32[]{:S(2)}, u32[]{:S(2)}) %collective-permute-start.9) | collective-permute-done | bytes 81952 | tf_op jit(solution)/shard_map/ppermute | solution.py:58
  48.6 1.8 %collective-permute-done.10 = bf16[64,640]{1,0:T(8,128)(2,1)S(1)} collective-permute-done((bf16[64,640]{1,0:T(8,128)(2,1)S(1)}, bf16[64,640]{1,0:T(8,128)(2,1)S(1)}, u32[]{:S(2)}, u32[]{:S(2)}) %collective-permute-start.10) | collective-permute-done | bytes 81952 | tf_op jit(solution)/shard_map/ppermute | solution.py:58
  50.5 0.9 %collective-permute-start.11 = (bf16[192,640]{1,0:T(8,128)(2,1)S(1)}, bf16[192,640]{1,0:T(8,128)(2,1)S(1)}, u32[]{:S(2)}, u32[]{:S(2)}) collective-permute-start(bf16[192,640]{1,0:T(8,128)(2,1)S(1)} %constant_dynamic-update-slice_fusion.2.refs_0_), channel_id=1, source_target_pairs={{2,0},{0,2},{6,4},{4,6},{3,1},{1,3},{7,5},{5,7},{10,8},{8,10},{14,... | collective-permute-start | bytes 737288 | tf_op jit(solution)/shard_map/ppermute | solution.py:58
  51.4 2.5 %collective-permute-start.12 = (bf16[192,640]{1,0:T(8,128)(2,1)S(1)}, bf16[192,640]{1,0:T(8,128)(2,1)S(1)}, u32[]{:S(2)}, u32[]{:S(2)}) collective-permute-start(bf16[192,640]{1,0:T(8,128)(2,1)S(1)} %constant_dynamic-update-slice_fusion.2.refs_0_), channel_id=1, source_target_pairs={{4,0},{6,2},{0,4},{2,6},{5,1},{7,3},{1,5},{3,7},{12,8},{14,10},{8,... | collective-permute-start | bytes 737288 | tf_op jit(solution)/shard_map/ppermute | solution.py:58
  54.0 8.2 %attend_plane.1 = (bf16[640,512]{1,0:T(8,128)(2,1)S(1)}, f32[10,8,512]{2,1,0:T(8,128)S(1)}) custom-call(s32[24]{0:T(128)S(1)} %pad_add_fusion.table_ref, bf16[640,512]{1,0:T(8,128)(2,1)S(1)} %get-tuple-element.32.q_ref, bf16[256,640]{1,0:T(8,128)(2,1)S(1)} %collective-permute-done.14.refs_0_, bf16[256,640]{1,0:T(8,128)(2,1)S(1)} %collective-permute-done.15.refs_1_, ...), custom_call_target="tpu_custom_call" | custom-call | flops 5284823040 | bytes 2293760 | tf_op jit(solution)/shard_map/attend_plane/pallas_call | solution.py:313
  62.3 8.8 %attend_anchors.1 = (bf16[640,256]{1,0:T(8,128)(2,1)S(1)}, f32[16,256]{1,0:T(8,128)S(1)}, bf16[688,256]{1,0:T(8,128)(2,1)S(1)}) custom-call(s32[24]{0:T(128)S(1)} %pad_add_fusion.table_ref, bf16[640,512]{1,0:T(8,128)(2,1)S(1)} %get-tuple-element.32.q_ref, bf16[192,640]{1,0:T(8,128)(2,1)S(1)} %constant_dynamic-update-slice_fusion.2.refs_0_, ...), custom_call_target="tpu_custom_call" | custom-call | flops 5284823040 | bytes 2293760 | tf_op jit(solution)/shard_map/attend_anchors/pallas_call | solution.py:390
  71.1 1.7 %collective-permute-done.17.refs_0_ = bf16[688,256]{1,0:T(8,128)(2,1)S(1)} collective-permute-done((bf16[688,256]{1,0:T(8,128)(2,1)S(1)}, bf16[688,256]{1,0:T(8,128)(2,1)S(1)}, u32[]{:S(2)}, u32[]{:S(2)}) %collective-permute-start.17) | collective-permute-done | bytes 352288 | tf_op jit(solution)/shard_map/ppermute | solution.py:63
  72.8 1.3 %finish.1 = bf16[256,640]{1,0:T(8,128)(2,1)} custom-call(bf16[640,256]{1,0:T(8,128)(2,1)S(1)} %get-tuple-element.41.own_ref, f32[16,256]{1,0:T(8,128)S(1)} %get-tuple-element.42.level_ref, bf16[688,256]{1,0:T(8,128)(2,1)S(1)} %collective-permute-done.17.refs_0_, bf16[640,640]{1,0:T(8,128)(2,1)S(1)} %copy-done), custom_call_target="tpu_custom_call" | custom-call | flops 209715200 | bytes 1802240 | tf_op jit(solution)/shard_map/finish/pallas_call | solution.py:440
  (51 shorter events, 5.6 us)
Async XLA Ops:
  0.6 18.7 %copy-start.7 = (s32[4]{0:T(128)S(1)}, s32[4]{0:T(128)}, u32[]{:S(2)}) copy-start(s32[4]{0:T(128)} %param.15) | copy-start | bytes 52
  0.6 18.7 %copy-start.6 = (s32[4]{0:T(128)S(1)}, s32[4]{0:T(128)}, u32[]{:S(2)}) copy-start(s32[4]{0:T(128)} %param.17) | copy-start | bytes 52
  0.7 34.1 %copy-start.2 = (bf16[640,640]{1,0:T(8,128)(2,1)S(1)}, bf16[640,640]{1,0:T(8,128)(2,1)}, u32[]{:S(2)}) copy-start(bf16[640,640]{1,0:T(8,128)(2,1)} %refs_8_.1) | copy-start | bytes 2457604
  1.7 1.4 %collective-permute-start = (bf16[8,640]{1,0:T(8,128)(2,1)S(1)}, bf16[8,640]{1,0:T(8,128)(2,1)S(1)}, u32[]{:S(2)}, u32[]{:S(2)}) collective-permute-start(bf16[8,640]{1,0:T(8,128)(2,1)S(1)} %bitcast.19), channel_id=1, source_target_pairs={{1,0},{0,1},{3,2},{2,3},{5,4},{4,5},{7,6},{6,7},{9,8},{8,9},{11,10... | collective-permute-start | bytes 30728 | tf_op jit(solution)/shard_map/ppermute | solution.py:63
  3.1 8.7 %copy-start.4 = (bf16[8,640]{1,0:T(8,128)(2,1)}, bf16[8,640]{1,0:T(8,128)(2,1)S(1)}, u32[]{:S(2)}) copy-start(bf16[8,640]{1,0:T(8,128)(2,1)S(1)} %get-tuple-element.24.right_ref) | copy-start | bytes 30724
  3.1 8.7 %copy-start.5 = (bf16[8,640]{1,0:T(8,128)(2,1)}, bf16[8,640]{1,0:T(8,128)(2,1)S(1)}, u32[]{:S(2)}) copy-start(bf16[8,640]{1,0:T(8,128)(2,1)S(1)} %get-tuple-element.23.left_ref) | copy-start | bytes 30724
  3.1 8.0 %collective-permute-start.1 = (bf16[34,640]{1,0:T(8,128)(2,1)S(1)}, bf16[34,640]{1,0:T(8,128)(2,1)S(1)}, u32[]{:S(2)}, u32[]{:S(2)}) collective-permute-start(bf16[34,640]{1,0:T(8,128)(2,1)S(1)} %get-tuple-element.49), channel_id=1, source_target_pairs={{0,2},{4,6},{2,0},{6,4},{1,3},{5,7},{3,1},{7,5},{8,10},{12,14},{10... | collective-permute-start | bytes 130568 | tf_op jit(solution)/shard_map/ppermute | solution.py:85
  6.0 5.1 %collective-permute-start.2 = (bf16[34,640]{1,0:T(8,128)(2,1)S(1)}, bf16[34,640]{1,0:T(8,128)(2,1)S(1)}, u32[]{:S(2)}, u32[]{:S(2)}) collective-permute-start(bf16[34,640]{1,0:T(8,128)(2,1)S(1)} %get-tuple-element.48), channel_id=1, source_target_pairs={{2,4},{4,2},{3,5},{5,3},{10,12},{12,10},{11,13},{13,11},{18,20},{2... | collective-permute-start | bytes 130568 | tf_op jit(solution)/shard_map/ppermute | solution.py:85
  19.3 1.7 %collective-permute-start.4 = (bf16[128,640]{1,0:T(8,128)(2,1)}, bf16[128,640]{1,0:T(8,128)(2,1)S(1)}, u32[]{:S(2)}, u32[]{:S(2)}) collective-permute-start(bf16[128,640]{1,0:T(8,128)(2,1)} %get-tuple-element.29.refs_1_), channel_id=1, source_target_pairs={{1,0},{0,1},{3,2},{2,3},{5,4},{4,5},{7,6},{6,7},{9,8},{8,9},{11,10... | collective-permute-start | bytes 491528 | tf_op jit(solution)/shard_map/ppermute | solution.py:63
  19.5 15.3 %collective-permute-start.3 = (bf16[128,640]{1,0:T(8,128)(2,1)}, bf16[128,640]{1,0:T(8,128)(2,1)S(1)}, u32[]{:S(2)}, u32[]{:S(2)}) collective-permute-start(bf16[128,640]{1,0:T(8,128)(2,1)} %get-tuple-element.28.refs_0_), channel_id=1, source_target_pairs={{1,0},{0,1},{3,2},{2,3},{5,4},{4,5},{7,6},{6,7},{9,8},{8,9},{11,10... | collective-permute-start | bytes 491528 | tf_op jit(solution)/shard_map/ppermute | solution.py:63
  21.6 7.8 %collective-permute-start.5 = (bf16[64,640]{1,0:T(8,128)(2,1)S(1)}, bf16[64,640]{1,0:T(8,128)(2,1)S(1)}, u32[]{:S(2)}, u32[]{:S(2)}) collective-permute-start(bf16[64,640]{1,0:T(8,128)(2,1)S(1)} %get-tuple-element.34), channel_id=1, source_target_pairs={{2,0},{0,2},{6,4},{4,6},{3,1},{1,3},{7,5},{5,7},{10,8},{8,10},{14,... | collective-permute-start | bytes 245768 | tf_op jit(solution)/shard_map/ppermute | solution.py:58
  25.9 6.3 %collective-permute-start.6 = (bf16[64,640]{1,0:T(8,128)(2,1)S(1)}, bf16[64,640]{1,0:T(8,128)(2,1)S(1)}, u32[]{:S(2)}, u32[]{:S(2)}) collective-permute-start(bf16[64,640]{1,0:T(8,128)(2,1)S(1)} %get-tuple-element.35), channel_id=1, source_target_pairs={{4,0},{6,2},{0,4},{2,6},{5,1},{7,3},{1,5},{3,7},{12,8},{14,10},{8,... | collective-permute-start | bytes 245768 | tf_op jit(solution)/shard_map/ppermute | solution.py:58
  25.9 6.5 %collective-permute-start.7 = (bf16[64,640]{1,0:T(8,128)(2,1)S(1)}, bf16[64,640]{1,0:T(8,128)(2,1)S(1)}, u32[]{:S(2)}, u32[]{:S(2)}) collective-permute-start(bf16[64,640]{1,0:T(8,128)(2,1)S(1)} %get-tuple-element.36), channel_id=1, source_target_pairs={{6,0},{4,2},{2,4},{0,6},{7,1},{5,3},{3,5},{1,7},{14,8},{12,10},{10... | collective-permute-start | bytes 245768 | tf_op jit(solution)/shard_map/ppermute | solution.py:58
  27.4 26.4 %collective-permute-start.14 = (bf16[256,640]{1,0:T(8,128)(2,1)S(1)}, bf16[256,640]{1,0:T(8,128)(2,1)S(1)}, u32[]{:S(2)}, u32[]{:S(2)}) collective-permute-start(bf16[256,640]{1,0:T(8,128)(2,1)S(1)} %constant_dynamic-update-slice_fusion.refs_4_.key_ref), channel_id=1, source_target_pairs={{2,0},{0,2},{6,4},{4,6},{3,1},{1,3},{7,5},{5,7},{10,8},{8,10},{14,... | collective-permute-start | bytes 983048 | tf_op jit(solution)/shard_map/ppermute | solution.py:58
  29.4 24.6 %collective-permute-start.15 = (bf16[256,640]{1,0:T(8,128)(2,1)S(1)}, bf16[256,640]{1,0:T(8,128)(2,1)S(1)}, u32[]{:S(2)}, u32[]{:S(2)}) collective-permute-start(bf16[256,640]{1,0:T(8,128)(2,1)S(1)} %constant_dynamic-update-slice_fusion.refs_4_.key_ref), channel_id=1, source_target_pairs={{4,0},{6,2},{0,4},{2,6},{5,1},{7,3},{1,5},{3,7},{12,8},{14,10},{8,... | collective-permute-start | bytes 983048 | tf_op jit(solution)/shard_map/ppermute | solution.py:58
  32.2 21.8 %collective-permute-start.16 = (bf16[256,640]{1,0:T(8,128)(2,1)S(1)}, bf16[256,640]{1,0:T(8,128)(2,1)S(1)}, u32[]{:S(2)}, u32[]{:S(2)}) collective-permute-start(bf16[256,640]{1,0:T(8,128)(2,1)S(1)} %constant_dynamic-update-slice_fusion.refs_4_.key_ref), channel_id=1, source_target_pairs={{6,0},{4,2},{2,4},{0,6},{7,1},{5,3},{3,5},{1,7},{14,8},{12,10},{10... | collective-permute-start | bytes 983048 | tf_op jit(solution)/shard_map/ppermute | solution.py:58
  33.1 11.1 %collective-permute-start.8 = (bf16[64,640]{1,0:T(8,128)(2,1)S(1)}, bf16[64,640]{1,0:T(8,128)(2,1)S(1)}, u32[]{:S(2)}, u32[]{:S(2)}) collective-permute-start(bf16[64,640]{1,0:T(8,128)(2,1)S(1)} %accept.1), channel_id=1, source_target_pairs={{8,0},{0,8},{24,16},{16,24},{9,1},{1,9},{25,17},{17,25},{10,2},{2,... | collective-permute-start | bytes 245768 | tf_op jit(solution)/shard_map/ppermute | solution.py:58
  41.5 7.0 %collective-permute-start.9 = (bf16[64,640]{1,0:T(8,128)(2,1)S(1)}, bf16[64,640]{1,0:T(8,128)(2,1)S(1)}, u32[]{:S(2)}, u32[]{:S(2)}) collective-permute-start(bf16[64,640]{1,0:T(8,128)(2,1)S(1)} %accept.1), channel_id=1, source_target_pairs={{16,0},{24,8},{0,16},{8,24},{17,1},{25,9},{1,17},{9,25},{18,2},{26... | collective-permute-start | bytes 245768 | tf_op jit(solution)/shard_map/ppermute | solution.py:58
  44.2 6.2 %collective-permute-start.10 = (bf16[64,640]{1,0:T(8,128)(2,1)S(1)}, bf16[64,640]{1,0:T(8,128)(2,1)S(1)}, u32[]{:S(2)}, u32[]{:S(2)}) collective-permute-start(bf16[64,640]{1,0:T(8,128)(2,1)S(1)} %accept.1), channel_id=1, source_target_pairs={{24,0},{16,8},{8,16},{0,24},{25,1},{17,9},{9,17},{1,25},{26,2},{18... | collective-permute-start | bytes 245768 | tf_op jit(solution)/shard_map/ppermute | solution.py:58
  50.5 11.8 %collective-permute-start.11 = (bf16[192,640]{1,0:T(8,128)(2,1)S(1)}, bf16[192,640]{1,0:T(8,128)(2,1)S(1)}, u32[]{:S(2)}, u32[]{:S(2)}) collective-permute-start(bf16[192,640]{1,0:T(8,128)(2,1)S(1)} %constant_dynamic-update-slice_fusion.2.refs_0_), channel_id=1, source_target_pairs={{2,0},{0,2},{6,4},{4,6},{3,1},{1,3},{7,5},{5,7},{10,8},{8,10},{14,... | collective-permute-start | bytes 737288 | tf_op jit(solution)/shard_map/ppermute | solution.py:58
  51.4 10.9 %collective-permute-start.12 = (bf16[192,640]{1,0:T(8,128)(2,1)S(1)}, bf16[192,640]{1,0:T(8,128)(2,1)S(1)}, u32[]{:S(2)}, u32[]{:S(2)}) collective-permute-start(bf16[192,640]{1,0:T(8,128)(2,1)S(1)} %constant_dynamic-update-slice_fusion.2.refs_0_), channel_id=1, source_target_pairs={{4,0},{6,2},{0,4},{2,6},{5,1},{7,3},{1,5},{3,7},{12,8},{14,10},{8,... | collective-permute-start | bytes 737288 | tf_op jit(solution)/shard_map/ppermute | solution.py:58
  53.9 8.4 %collective-permute-start.13 = (bf16[192,640]{1,0:T(8,128)(2,1)S(1)}, bf16[192,640]{1,0:T(8,128)(2,1)S(1)}, u32[]{:S(2)}, u32[]{:S(2)}) collective-permute-start(bf16[192,640]{1,0:T(8,128)(2,1)S(1)} %constant_dynamic-update-slice_fusion.2.refs_0_), channel_id=1, source_target_pairs={{6,0},{4,2},{2,4},{0,6},{7,1},{5,3},{3,5},{1,7},{14,8},{12,10},{10... | collective-permute-start | bytes 737288 | tf_op jit(solution)/shard_map/ppermute | solution.py:58
  62.3 10.5 %copy-start = (bf16[640,640]{1,0:T(8,128)(2,1)S(1)}, bf16[640,640]{1,0:T(8,128)(2,1)}, u32[]{:S(2)}) copy-start(bf16[640,640]{1,0:T(8,128)(2,1)} %refs_1_.1) | copy-start | bytes 2457604
  71.1 1.7 %collective-permute-start.17 = (bf16[688,256]{1,0:T(8,128)(2,1)S(1)}, bf16[688,256]{1,0:T(8,128)(2,1)S(1)}, u32[]{:S(2)}, u32[]{:S(2)}) collective-permute-start(bf16[688,256]{1,0:T(8,128)(2,1)S(1)} %get-tuple-element.43), channel_id=1, source_target_pairs={{1,0},{0,1},{3,2},{2,3},{5,4},{4,5},{7,6},{6,7},{9,8},{8,9},{11,10... | collective-permute-start | bytes 1056776 | tf_op jit(solution)/shard_map/ppermute | solution.py:63
  (2 other events, 1.8 us)
where the time goes:
time: 74.4 us; the launch traced here: 74.1 us
  Pallas kernels  32 us (43%)
  starting transfers between devices  20.8 us (28%)
  waiting for transfers between devices  10.5 us (14%)
  local copies, waits for them, and re-layouts  9.09 us (12%)
  between operations  0.86 us (1%)
  other arithmetic  0.78 us (1%)
    ppermute x12, starting transfers between devices, exchange(): lax.ppermute(block, axis, [(source_of(i, step, count), i) for i in range(...  16.1 us
    ppermute x12, waiting for transfers between devices, exchange(): lax.ppermute(block, axis, [(source_of(i, step, count), i) for i in range(...  8.77 us
    pallas_call x1, Pallas kernels, attend_anchors(): pl.pallas_call(functools.partial(anchor_kernel, info, len(keys), len(earl...  8.76 us
    pallas_call x1, Pallas kernels, attend_plane(): pl.pallas_call(functools.partial(plane_kernel, info, len(keys)), out_shap...  8.23 us
    pallas_call x1, Pallas kernels, conv_norm(): pl.pallas_call(functools.partial(conv_kernel, rows, cols, cores), out_sha...  7.46 us
    unnamed x22, local copies, waits for them, and re-layouts  6.48 us
    pallas_call x1, Pallas kernels, attend_own(): pl.pallas_call(functools.partial(own_kernel, info, len(parts)), out_shape...  4.93 us
    ppermute x2, starting transfers between devices, halo(): lax.ppermute(block, 'prow', pairs + [(j, i) for i, j in pairs])  3.54 us
  transfers between devices with their start and end apart: 18, of which 5 were waited for; matrix products, arithmetic and copies ran while one was open for 9% of the time, Pallas kernels for 20%

commit v1 on v0

--- a/solution.py
+++ b/solution.py
@@ -13,14 +13,17 @@
 LANES = 128
 SUBLANES = 8
 ONES = 16
+AHEAD = 2
+EDGE_FLOPS = 4 * 10**9
+CONV_MIB = 52
 F32 = jnp.float32
 BF16 = jnp.bfloat16
 MIB = 1 << 20
 
 
 VMEM = pl.BlockSpec(memory_space=pltpu.VMEM)
+HBM = pl.BlockSpec(memory_space=pltpu.HBM)
 SMEM = pl.BlockSpec(memory_space=pltpu.SMEM)
-HBM = pl.BlockSpec(memory_space=pltpu.HBM)
 
 
 def shape(*dims, dtype=BF16):
@@ -63,20 +66,42 @@
     return lax.ppermute(block, axis, [((i + step) % count, i) for i in range(count)])
 
 
+def edges_kernel(x_ref, first_ref, last_ref, top_ref, bottom_ref):
+    rows, cols, _ = x_ref.shape
+    part = 2 * SUBLANES
+    first_ref[...] = x_ref[:, :part].astype(F32)[:, 0].astype(BF16)
+    last_ref[...] = x_ref[:, cols - part:].astype(F32)[:, part - 1].astype(BF16)
+    top_ref[...] = x_ref[0]
+    bottom_ref[...] = x_ref[rows - 1]
+
+
+def edges(cells):
+    rows, cols, channels = cells.shape
+    return pl.pallas_call(
+        edges_kernel,
+        out_shape=(shape(rows, channels),) * 2 + (shape(cols, channels),) * 2,
+        in_specs=[VMEM],
+        out_specs=(VMEM,) * 4,
+        compiler_params=grant(8),
+        cost_estimate=cost(EDGE_FLOPS, cells.nbytes),
+        name="edges",
+    )(cells)
+
+
 def halo(cells):
+    first, last, top, bottom = edges(cells)
     core, cores = lax.axis_index("pcol"), lax.axis_size("pcol")
-    rows, cols = lax.axis_size("prow"), cells.shape[1]
+    rows = lax.axis_size("prow")
     if cores == 2:
-        inner = lax.dynamic_index_in_dim(cells, jnp.where(core == 0, cols - 1, 0), 1, keepdims=False)
-        other = shifted(inner, "pcol", 1)
+        other = shifted(jnp.where(core == 0, last, first), "pcol", 1)
         zero = jnp.zeros_like(other)
         left = jnp.where(core == 1, other, zero)
         right = jnp.where(core == 0, other, zero)
     else:
-        left = lax.ppermute(cells[:, -1], "pcol", [(i, i + 1) for i in range(cores - 1)])
-        right = lax.ppermute(cells[:, 0], "pcol", [(i + 1, i) for i in range(cores - 1)])
-    low = jnp.concatenate([cells[-1], left[-1:], right[-1:]], axis=0)
-    high = jnp.concatenate([cells[0], left[:1], right[:1]], axis=0)
+        left = lax.ppermute(last, "pcol", [(i, i + 1) for i in range(cores - 1)])
+        right = lax.ppermute(first, "pcol", [(i + 1, i) for i in range(cores - 1)])
+    low = jnp.concatenate([bottom, left[-1:], right[-1:]], axis=0)
+    high = jnp.concatenate([top, left[:1], right[:1]], axis=0)
     odd = lax.rem(lax.axis_index("prow"), 2) == 1
     swaps = []
     for first in range(2):
@@ -91,7 +116,8 @@
 def conv_kernel(rows, cols, cores, x_ref, left_ref, right_ref, above_ref, below_ref, w_ref, *refs):
     features_ref, *half_refs, shift0, shift1, shift2, taps, sem = refs
     copies = [
-        pltpu.make_async_copy(w_ref.at[n // 3, n % 3], taps.at[n], sem.at[n]) for n in range(9)
+        pltpu.make_async_copy(w_ref.at[rows_of], taps.at[rows_of], sem.at[n])
+        for n, rows_of in enumerate((slice(0, 1), slice(1, 3)))
     ]
     for copy in copies:
         copy.start()
@@ -115,10 +141,11 @@
         shift2[at] = jnp.where(side == cols - 1, rcell, pltpu.roll(cells, cols - 1, 0)).astype(BF16)
     total = x_ref[...].astype(F32)
     for a in range(3):
+        if a < 2:
+            copies[a].wait()
         for b, shift in enumerate((shift0, shift1, shift2)):
-            copies[3 * a + b].wait()
             total = total + jnp.dot(
-                shift[a * cols:(a + rows) * cols], taps[3 * a + b], preferred_element_type=F32
+                shift[a * cols:(a + rows) * cols], taps[a, b], preferred_element_type=F32
             )
     features = total.astype(BF16)
     features_ref[...] = features
@@ -146,9 +173,9 @@
         in_specs=[VMEM] * 5 + [HBM],
         out_specs=(VMEM,) * (1 + cores),
         scratch_shapes=[pltpu.VMEM(((rows + 2) * cols, channels), BF16)] * 3 + [
-            pltpu.VMEM((9, channels, channels), BF16), pltpu.SemaphoreType.DMA((9,)),
+            pltpu.VMEM((3, 3, channels, channels), BF16), pltpu.SemaphoreType.DMA((2,)),
         ],
-        compiler_params=grant(58),
+        compiler_params=grant(CONV_MIB),
         cost_estimate=cost(18 * tokens * channels**2, 18 * channels**2, tokens * channels),
         name="conv_norm",
     )(cells.reshape(tokens, channels), *sides, conv_weight)
@@ -195,20 +222,18 @@
         return jnp.where(slot < self.count(source), 1.0, 0.0).astype(F32)
 
 
-def project(normed, times, wk_ref, wvt_ref, k_scr, v_scr):
+def project(normed, times, wk_ref, wv_ref, k_scr, v_scr):
     keys, channels = normed.shape
     k = jnp.dot(normed, wk_ref[...], preferred_element_type=F32).astype(BF16)
     for pair in range(channels // LANES):
         k_scr[pair] = k[:, pair * LANES:(pair + 1) * LANES]
-    v = lax.dot_general(
-        wvt_ref[...], normed, (((1,), (1,)), ((), ())), preferred_element_type=F32
-    )
+    v = jnp.dot(normed, wv_ref[...], preferred_element_type=F32).astype(BF16).T
     per = keys // len(times)
     lane = lax.broadcasted_iota(jnp.int32, (1, keys), 1)
     mult = jnp.full((1, keys), times[0], F32)
     for g in range(1, len(times)):
         mult = jnp.where(lane >= g * per, times[g], mult)
-    v = (v * mult).astype(BF16)
+    v = v * mult.astype(BF16)
     ones = jnp.broadcast_to(mult, (ONES, keys)).astype(BF16)
     for head in range(channels // HEAD_DIM):
         v_scr[head, :HEAD_DIM] = v[head * HEAD_DIM:(head + 1) * HEAD_DIM]
@@ -228,11 +253,11 @@
         q = jnp.concatenate([q, zeros] if head % 2 == 0 else [zeros, q], axis=0)
         return jnp.dot(k_scr[head // 2], q, preferred_element_type=F32)
 
-    ahead = scores_of(*items[0])
+    ahead = [scores_of(*item) for item in items[:AHEAD]]
     for n, (head, cols) in enumerate(items):
-        scores = ahead
-        if n + 1 < len(items):
-            ahead = scores_of(*items[n + 1])
+        scores = ahead.pop(0)
+        if n + AHEAD < len(items):
+            ahead.append(scores_of(*items[n + AHEAD]))
         peak = jnp.max(scores, axis=0, keepdims=True)
         probs = jnp.exp(scores - peak).astype(BF16)
         value = jnp.dot(v_scr[head], probs, preferred_element_type=F32)
@@ -250,10 +275,8 @@
     table = Table(table_ref, anchors, images)
     at = 0
     for ref in part_refs:
-        q = lax.dot_general(
-            wq_ref[...], ref[...], (((1,), (1,)), ((), ())), preferred_element_type=F32
-        ).astype(BF16)
-        q_ref[:, at:at + ref.shape[0]] = (q.astype(F32) * HEAD_DIM ** (-0.5)).astype(BF16)
+        q = jnp.dot(ref[...], wq_ref[...], preferred_element_type=F32).astype(BF16)
+        q_ref[:, at:at + ref.shape[0]] = q.T * BF16(HEAD_DIM ** (-0.5))
         at += ref.shape[0]
     times = [table.own_times(0, g, cores, prows, per_patch) for g in range(cores * per_patch)]
     project(key_ref[...], times, wk_ref, wv_ref, k_scr, v_scr)
@@ -531,8 +554,7 @@
     per_patch = tile_rows * tile_cols // BLOCK
     info = (anchors, images, cores, prows, per_patch)
     table = Table.build(anchor_index, block_count, block_order[:, :NSEL])
-    sides, wq, wv = lax.optimization_barrier((halo(latent[0]), w_query.T, w_value.T))
-    features, *parts = conv_norm(latent[0], sides, conv_weight, cores)
+    features, *parts = conv_norm(latent[0], halo(latent[0]), conv_weight, cores)
     keys, queries = [parts[0]], list(parts)
     for s in range(1, cores):
         theirs = [None] * cores
@@ -546,7 +568,7 @@
         mine, *offers = offer(info, table, key)
         offers = [mine] + [exchange(rows, "prow", s) for s, rows in enumerate(offers, 1)]
     plane = [exchange(key, "prow", s) for s in range(1, prows)]
-    q, value, level = attend_own(info, table, queries, key, wq, w_key, wv)
+    q, value, level = attend_own(info, table, queries, key, w_query, w_key, w_value)
     done = [(value, level)]
     if every_image:
         share = accept(info, table, offers)
@@ -559,8 +581,8 @@
         joined = anchor_rows(key, anchor_index, block_order, block_count, cores, per_patch)
         sources = [joined[anchor] for anchor in range(anchors)]
     if plane:
-        done.append(attend_plane(info, table, q, plane, w_key, wv))
-    own, level, *sent = attend_anchors(info, table, q, sources, done, w_key, wv, cores)
+        done.append(attend_plane(info, table, q, plane, w_key, w_value))
+    own, level, *sent = attend_anchors(info, table, q, sources, done, w_key, w_value, cores)
     received = [shifted(block, "pcol", cores - s) for s, block in enumerate(sent, 1)]
     attended = finish(own, level, received, w_out, cores)
     return features.reshape(latent.shape), attended.reshape(latent.shape)

time: 74.4 us -> 67.5 us (0.907)
  local copies, waits for them, and re-layouts: 9.09 us -> 1.18 us
  starting transfers between devices: 20.8 us -> 26.9 us
  Pallas kernels: 32 us -> 27.6 us
    ppermute x12, starting transfers between devices: 16.1 us -> 22.2 us  [exchange(): lax.ppermute(block, axis, [(source_of(i, step, count), i) for i in range(...]
    unnamed x22 -> x21, local copies, waits for them, and re-layouts: 6.48 us -> 1.05 us
    ppermute x12, waiting for transfers between devices: 8.77 us -> 6.02 us  [exchange(): lax.ppermute(block, axis, [(source_of(i, step, count), i) for i in range(...]
    ppermute x4, waiting for transfers between devices: 1.76 us -> 3.27 us  [shifted(): lax.ppermute(block, axis, [((i + step) % count, i) for i in range(count)])]
    pallas_call x1, Pallas kernels: 7.46 us -> 6.06 us  [conv_norm(): pl.pallas_call(functools.partial(conv_kernel, rows, cols, cores), out_sha...]
    ppermute x2, waiting for transfers between devices: 0.01 us -> 1.37 us  [halo(): lax.ppermute(block, 'prow', pairs + [(j, i) for i, j in pairs])]
    pallas_call x1, Pallas kernels: 8.23 us -> 7.03 us  [attend_plane(): pl.pallas_call(functools.partial(plane_kernel, info, len(keys)), out_shap...]
    pallas_call x1, Pallas kernels: 8.76 us -> 7.6 us  [attend_anchors(): pl.pallas_call(functools.partial(anchor_kernel, info, len(keys), len(earl...]
  transfers between devices with their start and end apart: 18 -> 18, of which waited for: 5 -> 6; matrix products, arithmetic and copies ran while one was open for 9% -> 0% of each run, Pallas kernels for 20% -> 19%
where the time goes in v1:
time: 67.5 us; the launch traced here: 67.4 us
  Pallas kernels  27.6 us (41%)
  starting transfers between devices  26.9 us (40%)
  waiting for transfers between devices  10.7 us (16%)
  local copies, waits for them, and re-layouts  1.18 us (2%)
  between operations  0.88 us (1%)
    ppermute x12, starting transfers between devices, exchange(): lax.ppermute(block, axis, [(source_of(i, step, count), i) for i in range(...  22.2 us
    pallas_call x1, Pallas kernels, attend_anchors(): pl.pallas_call(functools.partial(anchor_kernel, info, len(keys), len(earl...  7.6 us
    pallas_call x1, Pallas kernels, attend_plane(): pl.pallas_call(functools.partial(plane_kernel, info, len(keys)), out_shap...  7.03 us
    pallas_call x1, Pallas kernels, conv_norm(): pl.pallas_call(functools.partial(conv_kernel, rows, cols, cores), out_sha...  6.06 us
    ppermute x12, waiting for transfers between devices, exchange(): lax.ppermute(block, axis, [(source_of(i, step, count), i) for i in range(...  6.02 us
    pallas_call x1, Pallas kernels, attend_own(): pl.pallas_call(functools.partial(own_kernel, info, len(parts)), out_shape...  4.21 us
    ppermute x2, starting transfers between devices, halo(): lax.ppermute(block, 'prow', pairs + [(j, i) for i, j in pairs])  3.54 us
    ppermute x4, waiting for transfers between devices, shifted(): lax.ppermute(block, axis, [((i + step) % count, i) for i in range(count)])  3.27 us
  transfers between devices with their start and end apart: 18, of which 6 were waited for; matrix products, arithmetic and copies ran while one was open for 0% of the time, Pallas kernels for 19%

profile of v1, /device:TPU:0, one launch (start us, length us, event | category | flops | bytes accessed | tf_op | source)
XLA Modules:
  0.0 67.4 jit_solution(10766194292312722276)
XLA Ops:
  0.6 1.0 %copy-done.1 = bf16[1,8,32,640]{3,2,1,0:T(8,128)(2,1)S(1)} copy-done((bf16[1,8,32,640]{3,2,1,0:T(8,128)(2,1)S(1)}, bf16[1,8,32,640]{3,2,1,0:T(8,128)(2,1)}, u32[]{:S(2)}) %copy-start.1) | copy-done | bytes 327704
  2.3 0.8 %collective-permute-done = bf16[8,640]{1,0:T(8,128)(2,1)S(1)} collective-permute-done((bf16[8,640]{1,0:T(8,128)(2,1)S(1)}, bf16[8,640]{1,0:T(8,128)(2,1)S(1)}, u32[]{:S(2)}, u32[]{:S(2)}) %collective-permute-start) | collective-permute-done | bytes 10272 | tf_op jit(solution)/shard_map/ppermute | solution.py:66
  3.2 2.9 %collective-permute-start.1 = (bf16[34,640]{1,0:T(8,128)(2,1)S(1)}, bf16[34,640]{1,0:T(8,128)(2,1)S(1)}, u32[]{:S(2)}, u32[]{:S(2)}) collective-permute-start(bf16[34,640]{1,0:T(8,128)(2,1)S(1)} %get-tuple-element.43), channel_id=1, source_target_pairs={{0,2},{4,6},{2,0},{6,4},{1,3},{5,7},{3,1},{7,5},{8,10},{12,14},{10... | collective-permute-start | bytes 130568 | tf_op jit(solution)/shard_map/ppermute | solution.py:110
  6.1 0.7 collective-permute-start.2
  6.8 1.4 %collective-permute-done.1 = bf16[34,640]{1,0:T(8,128)(2,1)S(1)} collective-permute-done((bf16[34,640]{1,0:T(8,128)(2,1)S(1)}, bf16[34,640]{1,0:T(8,128)(2,1)S(1)}, u32[]{:S(2)}, u32[]{:S(2)}) %collective-permute-start.1) | collective-permute-done | bytes 43552 | tf_op jit(solution)/shard_map/ppermute | solution.py:110
  8.2 6.1 %conv_norm.1 = (bf16[256,640]{1,0:T(8,128)(2,1)}, bf16[128,640]{1,0:T(8,128)(2,1)S(1)}, bf16[128,640]{1,0:T(8,128)(2,1)S(1)}) custom-call(bf16[256,640]{1,0:T(8,128)(2,1)S(1)} %bitcast.6, bf16[8,640]{1,0:T(8,128)(2,1)S(1)} %get-tuple-element.49.left_ref, bf16[8,640]{1,0:T(8,128)(2,1)S(1)} %get-tuple-element.48.right_ref, ...), custom_call_target="tpu_custom_call" | custom-call | flops 1887436800 | bytes 7372800 | tf_op jit(solution)/shard_map/conv_norm/pallas_call | solution.py:170
  15.0 0.8 %collective-permute-done.4.refs_3_ = bf16[128,640]{1,0:T(8,128)(2,1)S(1)} collective-permute-done((bf16[128,640]{1,0:T(8,128)(2,1)S(1)}, bf16[128,640]{1,0:T(8,128)(2,1)S(1)}, u32[]{:S(2)}, u32[]{:S(2)}) %collective-permute-start.4) | collective-permute-done | bytes 163872 | tf_op jit(solution)/shard_map/ppermute | solution.py:66
  15.8 0.6 offer.1
  16.4 4.9 %collective-permute-start.5 = (bf16[64,640]{1,0:T(8,128)(2,1)S(1)}, bf16[64,640]{1,0:T(8,128)(2,1)S(1)}, u32[]{:S(2)}, u32[]{:S(2)}) collective-permute-start(bf16[64,640]{1,0:T(8,128)(2,1)S(1)} %get-tuple-element.30), channel_id=1, source_target_pairs={{2,0},{0,2},{6,4},{4,6},{3,1},{1,3},{7,5},{5,7},{10,8},{8,10},{14,... | collective-permute-start | bytes 245768 | tf_op jit(solution)/shard_map/ppermute | solution.py:61
  21.3 1.5 %collective-permute-start.6 = (bf16[64,640]{1,0:T(8,128)(2,1)S(1)}, bf16[64,640]{1,0:T(8,128)(2,1)S(1)}, u32[]{:S(2)}, u32[]{:S(2)}) collective-permute-start(bf16[64,640]{1,0:T(8,128)(2,1)S(1)} %get-tuple-element.31), channel_id=1, source_target_pairs={{4,0},{6,2},{0,4},{2,6},{5,1},{7,3},{1,5},{3,7},{12,8},{14,10},{8,... | collective-permute-start | bytes 245768 | tf_op jit(solution)/shard_map/ppermute | solution.py:61
  22.8 1.4 %collective-permute-start.7 = (bf16[64,640]{1,0:T(8,128)(2,1)S(1)}, bf16[64,640]{1,0:T(8,128)(2,1)S(1)}, u32[]{:S(2)}, u32[]{:S(2)}) collective-permute-start(bf16[64,640]{1,0:T(8,128)(2,1)S(1)} %get-tuple-element.32), channel_id=1, source_target_pairs={{6,0},{4,2},{2,4},{0,6},{7,1},{5,3},{3,5},{1,7},{14,8},{12,10},{10... | collective-permute-start | bytes 245768 | tf_op jit(solution)/shard_map/ppermute | solution.py:61
  24.8 2.9 %collective-permute-start.15 = (bf16[256,640]{1,0:T(8,128)(2,1)S(1)}, bf16[256,640]{1,0:T(8,128)(2,1)S(1)}, u32[]{:S(2)}, u32[]{:S(2)}) collective-permute-start(bf16[256,640]{1,0:T(8,128)(2,1)S(1)} %constant_dynamic-update-slice_fusion.refs_4_.key_ref), channel_id=1, source_target_pairs={{4,0},{6,2},{0,4},{2,6},{5,1},{7,3},{1,5},{3,7},{12,8},{14,10},{8,... | collective-permute-start | bytes 983048 | tf_op jit(solution)/shard_map/ppermute | solution.py:61
  27.7 2.8 %collective-permute-start.16 = (bf16[256,640]{1,0:T(8,128)(2,1)S(1)}, bf16[256,640]{1,0:T(8,128)(2,1)S(1)}, u32[]{:S(2)}, u32[]{:S(2)}) collective-permute-start(bf16[256,640]{1,0:T(8,128)(2,1)S(1)} %constant_dynamic-update-slice_fusion.refs_4_.key_ref), channel_id=1, source_target_pairs={{6,0},{4,2},{2,4},{0,6},{7,1},{5,3},{3,5},{1,7},{14,8},{12,10},{10... | collective-permute-start | bytes 983048 | tf_op jit(solution)/shard_map/ppermute | solution.py:61
  30.5 0.8 %accept.1 = bf16[64,640]{1,0:T(8,128)(2,1)S(1)} custom-call(s32[24]{0:T(128)S(1)} %pad_add_fusion.table_ref, bf16[64,640]{1,0:T(8,128)(2,1)S(1)} %get-tuple-element.29.refs_0_, bf16[64,640]{1,0:T(8,128)(2,1)S(1)} %collective-permute-done.5.refs_1_, bf16[64,640]{1,0:T(8,128)(2,1)S(1)} %collective-permute-done.6.refs_2_, ...), custom_call_target="tpu_custom_call" | custom-call | tf_op jit(solution)/shard_map/accept/pallas_call | solution.py:525
  31.3 1.6 %collective-permute-start.8 = (bf16[64,640]{1,0:T(8,128)(2,1)S(1)}, bf16[64,640]{1,0:T(8,128)(2,1)S(1)}, u32[]{:S(2)}, u32[]{:S(2)}) collective-permute-start(bf16[64,640]{1,0:T(8,128)(2,1)S(1)} %accept.1), channel_id=1, source_target_pairs={{8,0},{0,8},{24,16},{16,24},{9,1},{1,9},{25,17},{17,25},{10,2},{2,... | collective-permute-start | bytes 245768 | tf_op jit(solution)/shard_map/ppermute | solution.py:61
  33.0 4.2 %attend_own.1 = (bf16[640,512]{1,0:T(8,128)(2,1)S(1)}, bf16[640,512]{1,0:T(8,128)(2,1)S(1)}, f32[10,8,512]{2,1,0:T(8,128)S(1)}) custom-call(s32[24]{0:T(128)S(1)} %pad_add_fusion.table_ref, bf16[128,640]{1,0:T(8,128)(2,1)S(1)} %get-tuple-element.26.refs_0_, bf16[128,640]{1,0:T(8,128)(2,1)S(1)} %get-tuple-element.27.refs_1_, ...), custom_call_target="tpu_custom_call" | custom-call | flops 2181038080 | bytes 1638400 | tf_op jit(solution)/shard_map/attend_own/pallas_call | solution.py:304
  37.2 2.7 %collective-permute-start.9 = (bf16[64,640]{1,0:T(8,128)(2,1)S(1)}, bf16[64,640]{1,0:T(8,128)(2,1)S(1)}, u32[]{:S(2)}, u32[]{:S(2)}) collective-permute-start(bf16[64,640]{1,0:T(8,128)(2,1)S(1)} %accept.1), channel_id=1, source_target_pairs={{16,0},{24,8},{0,16},{8,24},{17,1},{25,9},{1,17},{9,25},{18,2},{26... | collective-permute-start | bytes 245768 | tf_op jit(solution)/shard_map/ppermute | solution.py:61
  40.1 3.6 %collective-permute-done.9 = bf16[64,640]{1,0:T(8,128)(2,1)S(1)} collective-permute-done((bf16[64,640]{1,0:T(8,128)(2,1)S(1)}, bf16[64,640]{1,0:T(8,128)(2,1)S(1)}, u32[]{:S(2)}, u32[]{:S(2)}) %collective-permute-start.9) | collective-permute-done | bytes 81952 | tf_op jit(solution)/shard_map/ppermute | solution.py:61
  43.7 2.4 %collective-permute-done.10 = bf16[64,640]{1,0:T(8,128)(2,1)S(1)} collective-permute-done((bf16[64,640]{1,0:T(8,128)(2,1)S(1)}, bf16[64,640]{1,0:T(8,128)(2,1)S(1)}, u32[]{:S(2)}, u32[]{:S(2)}) %collective-permute-start.10) | collective-permute-done | bytes 81952 | tf_op jit(solution)/shard_map/ppermute | solution.py:61
  46.9 2.8 %collective-permute-start.13 = (bf16[192,640]{1,0:T(8,128)(2,1)S(1)}, bf16[192,640]{1,0:T(8,128)(2,1)S(1)}, u32[]{:S(2)}, u32[]{:S(2)}) collective-permute-start(bf16[192,640]{1,0:T(8,128)(2,1)S(1)} %constant_dynamic-update-slice_fusion.2.refs_0_), channel_id=1, source_target_pairs={{6,0},{4,2},{2,4},{0,6},{7,1},{5,3},{3,5},{1,7},{14,8},{12,10},{10... | collective-permute-start | bytes 737288 | tf_op jit(solution)/shard_map/ppermute | solution.py:61
  49.7 7.0 %attend_plane.1 = (bf16[640,512]{1,0:T(8,128)(2,1)S(1)}, f32[10,8,512]{2,1,0:T(8,128)S(1)}) custom-call(s32[24]{0:T(128)S(1)} %pad_add_fusion.table_ref, bf16[640,512]{1,0:T(8,128)(2,1)S(1)} %get-tuple-element.28.q_ref, bf16[256,640]{1,0:T(8,128)(2,1)S(1)} %collective-permute-done.14.refs_0_, bf16[256,640]{1,0:T(8,128)(2,1)S(1)} %collective-permute-done.15.refs_1_, ...), custom_call_target="tpu_custom_call" | custom-call | flops 5284823040 | bytes 2293760 | tf_op jit(solution)/shard_map/attend_plane/pallas_call | solution.py:336
  56.8 7.6 %attend_anchors.1 = (bf16[640,256]{1,0:T(8,128)(2,1)S(1)}, f32[16,256]{1,0:T(8,128)S(1)}, bf16[688,256]{1,0:T(8,128)(2,1)S(1)}) custom-call(s32[24]{0:T(128)S(1)} %pad_add_fusion.table_ref, bf16[640,512]{1,0:T(8,128)(2,1)S(1)} %get-tuple-element.28.q_ref, bf16[192,640]{1,0:T(8,128)(2,1)S(1)} %constant_dynamic-update-slice_fusion.2.refs_0_, ...), custom_call_target="tpu_custom_call" | custom-call | flops 5284823040 | bytes 2293760 | tf_op jit(solution)/shard_map/attend_anchors/pallas_call | solution.py:413
  64.4 1.7 %collective-permute-done.17.refs_0_ = bf16[688,256]{1,0:T(8,128)(2,1)S(1)} collective-permute-done((bf16[688,256]{1,0:T(8,128)(2,1)S(1)}, bf16[688,256]{1,0:T(8,128)(2,1)S(1)}, u32[]{:S(2)}, u32[]{:S(2)}) %collective-permute-start.17) | collective-permute-done | bytes 352288 | tf_op jit(solution)/shard_map/ppermute | solution.py:66
  66.1 1.3 %finish.1 = bf16[256,640]{1,0:T(8,128)(2,1)} custom-call(bf16[640,256]{1,0:T(8,128)(2,1)S(1)} %get-tuple-element.37.own_ref, f32[16,256]{1,0:T(8,128)S(1)} %get-tuple-element.38.level_ref, bf16[688,256]{1,0:T(8,128)(2,1)S(1)} %collective-permute-done.17.refs_0_, bf16[640,640]{1,0:T(8,128)(2,1)S(1)} %copy-done), custom_call_target="tpu_custom_call" | custom-call | flops 209715200 | bytes 1802240 | tf_op jit(solution)/shard_map/finish/pallas_call | solution.py:463
  (50 shorter events, 3.2 us)
Async XLA Ops:
  1.7 12.7 %copy-start.7 = (s32[4]{0:T(128)S(1)}, s32[4]{0:T(128)}, u32[]{:S(2)}) copy-start(s32[4]{0:T(128)} %param.17) | copy-start | bytes 52
  1.7 12.7 %copy-start.8 = (s32[4]{0:T(128)S(1)}, s32[4]{0:T(128)}, u32[]{:S(2)}) copy-start(s32[4]{0:T(128)} %param.15) | copy-start | bytes 52
  1.7 31.3 %copy-start.3 = (bf16[640,640]{1,0:T(8,128)(2,1)S(1)}, bf16[640,640]{1,0:T(8,128)(2,1)}, u32[]{:S(2)}) copy-start(bf16[640,640]{1,0:T(8,128)(2,1)} %refs_5_.1) | copy-start | bytes 2457604
  1.7 31.3 %copy-start.4 = (bf16[640,640]{1,0:T(8,128)(2,1)S(1)}, bf16[640,640]{1,0:T(8,128)(2,1)}, u32[]{:S(2)}) copy-start(bf16[640,640]{1,0:T(8,128)(2,1)} %refs_8_.1) | copy-start | bytes 2457604
  1.7 31.3 %copy-start.5 = (bf16[640,640]{1,0:T(8,128)(2,1)S(1)}, bf16[640,640]{1,0:T(8,128)(2,1)}, u32[]{:S(2)}) copy-start(bf16[640,640]{1,0:T(8,128)(2,1)} %refs_9_.1) | copy-start | bytes 2457604
  1.7 1.4 %collective-permute-start = (bf16[8,640]{1,0:T(8,128)(2,1)S(1)}, bf16[8,640]{1,0:T(8,128)(2,1)S(1)}, u32[]{:S(2)}, u32[]{:S(2)}) collective-permute-start(bf16[8,640]{1,0:T(8,128)(2,1)S(1)} %broadcast_select_fusion.5), channel_id=1, source_target_pairs={{1,0},{0,1},{3,2},{2,3},{5,4},{4,5},{7,6},{6,7},{9,8},{8,9},{11,10... | collective-permute-start | bytes 30728 | tf_op jit(solution)/shard_map/ppermute | solution.py:66
  3.2 5.0 %collective-permute-start.1 = (bf16[34,640]{1,0:T(8,128)(2,1)S(1)}, bf16[34,640]{1,0:T(8,128)(2,1)S(1)}, u32[]{:S(2)}, u32[]{:S(2)}) collective-permute-start(bf16[34,640]{1,0:T(8,128)(2,1)S(1)} %get-tuple-element.43), channel_id=1, source_target_pairs={{0,2},{4,6},{2,0},{6,4},{1,3},{5,7},{3,1},{7,5},{8,10},{12,14},{10... | collective-permute-start | bytes 130568 | tf_op jit(solution)/shard_map/ppermute | solution.py:110
  6.1 2.1 %collective-permute-start.2 = (bf16[34,640]{1,0:T(8,128)(2,1)S(1)}, bf16[34,640]{1,0:T(8,128)(2,1)S(1)}, u32[]{:S(2)}, u32[]{:S(2)}) collective-permute-start(bf16[34,640]{1,0:T(8,128)(2,1)S(1)} %get-tuple-element.42), channel_id=1, source_target_pairs={{2,4},{4,2},{3,5},{5,3},{10,12},{12,10},{11,13},{13,11},{18,20},{2... | collective-permute-start | bytes 130568 | tf_op jit(solution)/shard_map/ppermute | solution.py:110
  14.3 1.5 %collective-permute-start.4 = (bf16[128,640]{1,0:T(8,128)(2,1)S(1)}, bf16[128,640]{1,0:T(8,128)(2,1)S(1)}, u32[]{:S(2)}, u32[]{:S(2)}) collective-permute-start(bf16[128,640]{1,0:T(8,128)(2,1)S(1)} %get-tuple-element.27.refs_1_), channel_id=1, source_target_pairs={{1,0},{0,1},{3,2},{2,3},{5,4},{4,5},{7,6},{6,7},{9,8},{8,9},{11,10... | collective-permute-start | bytes 491528 | tf_op jit(solution)/shard_map/ppermute | solution.py:66
  14.5 18.5 %collective-permute-start.3 = (bf16[128,640]{1,0:T(8,128)(2,1)S(1)}, bf16[128,640]{1,0:T(8,128)(2,1)S(1)}, u32[]{:S(2)}, u32[]{:S(2)}) collective-permute-start(bf16[128,640]{1,0:T(8,128)(2,1)S(1)} %get-tuple-element.26.refs_0_), channel_id=1, source_target_pairs={{1,0},{0,1},{3,2},{2,3},{5,4},{4,5},{7,6},{6,7},{9,8},{8,9},{11,10... | collective-permute-start | bytes 491528 | tf_op jit(solution)/shard_map/ppermute | solution.py:66
  16.4 8.4 %collective-permute-start.5 = (bf16[64,640]{1,0:T(8,128)(2,1)S(1)}, bf16[64,640]{1,0:T(8,128)(2,1)S(1)}, u32[]{:S(2)}, u32[]{:S(2)}) collective-permute-start(bf16[64,640]{1,0:T(8,128)(2,1)S(1)} %get-tuple-element.30), channel_id=1, source_target_pairs={{2,0},{0,2},{6,4},{4,6},{3,1},{1,3},{7,5},{5,7},{10,8},{8,10},{14,... | collective-permute-start | bytes 245768 | tf_op jit(solution)/shard_map/ppermute | solution.py:61
  21.3 6.4 %collective-permute-start.6 = (bf16[64,640]{1,0:T(8,128)(2,1)S(1)}, bf16[64,640]{1,0:T(8,128)(2,1)S(1)}, u32[]{:S(2)}, u32[]{:S(2)}) collective-permute-start(bf16[64,640]{1,0:T(8,128)(2,1)S(1)} %get-tuple-element.31), channel_id=1, source_target_pairs={{4,0},{6,2},{0,4},{2,6},{5,1},{7,3},{1,5},{3,7},{12,8},{14,10},{8,... | collective-permute-start | bytes 245768 | tf_op jit(solution)/shard_map/ppermute | solution.py:61
  22.8 7.7 %collective-permute-start.7 = (bf16[64,640]{1,0:T(8,128)(2,1)S(1)}, bf16[64,640]{1,0:T(8,128)(2,1)S(1)}, u32[]{:S(2)}, u32[]{:S(2)}) collective-permute-start(bf16[64,640]{1,0:T(8,128)(2,1)S(1)} %get-tuple-element.32), channel_id=1, source_target_pairs={{6,0},{4,2},{2,4},{0,6},{7,1},{5,3},{3,5},{1,7},{14,8},{12,10},{10... | collective-permute-start | bytes 245768 | tf_op jit(solution)/shard_map/ppermute | solution.py:61
  24.2 22.6 %collective-permute-start.14 = (bf16[256,640]{1,0:T(8,128)(2,1)S(1)}, bf16[256,640]{1,0:T(8,128)(2,1)S(1)}, u32[]{:S(2)}, u32[]{:S(2)}) collective-permute-start(bf16[256,640]{1,0:T(8,128)(2,1)S(1)} %constant_dynamic-update-slice_fusion.refs_4_.key_ref), channel_id=1, source_target_pairs={{2,0},{0,2},{6,4},{4,6},{3,1},{1,3},{7,5},{5,7},{10,8},{8,10},{14,... | collective-permute-start | bytes 983048 | tf_op jit(solution)/shard_map/ppermute | solution.py:61
  24.8 24.9 %collective-permute-start.15 = (bf16[256,640]{1,0:T(8,128)(2,1)S(1)}, bf16[256,640]{1,0:T(8,128)(2,1)S(1)}, u32[]{:S(2)}, u32[]{:S(2)}) collective-permute-start(bf16[256,640]{1,0:T(8,128)(2,1)S(1)} %constant_dynamic-update-slice_fusion.refs_4_.key_ref), channel_id=1, source_target_pairs={{4,0},{6,2},{0,4},{2,6},{5,1},{7,3},{1,5},{3,7},{12,8},{14,10},{8,... | collective-permute-start | bytes 983048 | tf_op jit(solution)/shard_map/ppermute | solution.py:61
  27.7 21.9 %collective-permute-start.16 = (bf16[256,640]{1,0:T(8,128)(2,1)S(1)}, bf16[256,640]{1,0:T(8,128)(2,1)S(1)}, u32[]{:S(2)}, u32[]{:S(2)}) collective-permute-start(bf16[256,640]{1,0:T(8,128)(2,1)S(1)} %constant_dynamic-update-slice_fusion.refs_4_.key_ref), channel_id=1, source_target_pairs={{6,0},{4,2},{2,4},{0,6},{7,1},{5,3},{3,5},{1,7},{14,8},{12,10},{10... | collective-permute-start | bytes 983048 | tf_op jit(solution)/shard_map/ppermute | solution.py:61
  31.3 8.5 %collective-permute-start.8 = (bf16[64,640]{1,0:T(8,128)(2,1)S(1)}, bf16[64,640]{1,0:T(8,128)(2,1)S(1)}, u32[]{:S(2)}, u32[]{:S(2)}) collective-permute-start(bf16[64,640]{1,0:T(8,128)(2,1)S(1)} %accept.1), channel_id=1, source_target_pairs={{8,0},{0,8},{24,16},{16,24},{9,1},{1,9},{25,17},{17,25},{10,2},{2,... | collective-permute-start | bytes 245768 | tf_op jit(solution)/shard_map/ppermute | solution.py:61
  37.2 6.5 %collective-permute-start.9 = (bf16[64,640]{1,0:T(8,128)(2,1)S(1)}, bf16[64,640]{1,0:T(8,128)(2,1)S(1)}, u32[]{:S(2)}, u32[]{:S(2)}) collective-permute-start(bf16[64,640]{1,0:T(8,128)(2,1)S(1)} %accept.1), channel_id=1, source_target_pairs={{16,0},{24,8},{0,16},{8,24},{17,1},{25,9},{1,17},{9,25},{18,2},{26... | collective-permute-start | bytes 245768 | tf_op jit(solution)/shard_map/ppermute | solution.py:61
  39.9 6.2 %collective-permute-start.10 = (bf16[64,640]{1,0:T(8,128)(2,1)S(1)}, bf16[64,640]{1,0:T(8,128)(2,1)S(1)}, u32[]{:S(2)}, u32[]{:S(2)}) collective-permute-start(bf16[64,640]{1,0:T(8,128)(2,1)S(1)} %accept.1), channel_id=1, source_target_pairs={{24,0},{16,8},{8,16},{0,24},{25,1},{17,9},{9,17},{1,25},{26,2},{18... | collective-permute-start | bytes 245768 | tf_op jit(solution)/shard_map/ppermute | solution.py:61
  46.1 10.6 %collective-permute-start.11 = (bf16[192,640]{1,0:T(8,128)(2,1)S(1)}, bf16[192,640]{1,0:T(8,128)(2,1)S(1)}, u32[]{:S(2)}, u32[]{:S(2)}) collective-permute-start(bf16[192,640]{1,0:T(8,128)(2,1)S(1)} %constant_dynamic-update-slice_fusion.2.refs_0_), channel_id=1, source_target_pairs={{2,0},{0,2},{6,4},{4,6},{3,1},{1,3},{7,5},{5,7},{10,8},{8,10},{14,... | collective-permute-start | bytes 737288 | tf_op jit(solution)/shard_map/ppermute | solution.py:61
  46.6 10.1 %collective-permute-start.12 = (bf16[192,640]{1,0:T(8,128)(2,1)S(1)}, bf16[192,640]{1,0:T(8,128)(2,1)S(1)}, u32[]{:S(2)}, u32[]{:S(2)}) collective-permute-start(bf16[192,640]{1,0:T(8,128)(2,1)S(1)} %constant_dynamic-update-slice_fusion.2.refs_0_), channel_id=1, source_target_pairs={{4,0},{6,2},{0,4},{2,6},{5,1},{7,3},{1,5},{3,7},{12,8},{14,10},{8,... | collective-permute-start | bytes 737288 | tf_op jit(solution)/shard_map/ppermute | solution.py:61
  46.9 9.9 %collective-permute-start.13 = (bf16[192,640]{1,0:T(8,128)(2,1)S(1)}, bf16[192,640]{1,0:T(8,128)(2,1)S(1)}, u32[]{:S(2)}, u32[]{:S(2)}) collective-permute-start(bf16[192,640]{1,0:T(8,128)(2,1)S(1)} %constant_dynamic-update-slice_fusion.2.refs_0_), channel_id=1, source_target_pairs={{6,0},{4,2},{2,4},{0,6},{7,1},{5,3},{3,5},{1,7},{14,8},{12,10},{10... | collective-permute-start | bytes 737288 | tf_op jit(solution)/shard_map/ppermute | solution.py:61
  56.7 9.3 %copy-start = (bf16[640,640]{1,0:T(8,128)(2,1)S(1)}, bf16[640,640]{1,0:T(8,128)(2,1)}, u32[]{:S(2)}) copy-start(bf16[640,640]{1,0:T(8,128)(2,1)} %refs_1_.1) | copy-start | bytes 2457604
  64.4 1.7 %collective-permute-start.17 = (bf16[688,256]{1,0:T(8,128)(2,1)S(1)}, bf16[688,256]{1,0:T(8,128)(2,1)S(1)}, u32[]{:S(2)}, u32[]{:S(2)}) collective-permute-start(bf16[688,256]{1,0:T(8,128)(2,1)S(1)} %get-tuple-element.39), channel_id=1, source_target_pairs={{1,0},{0,1},{3,2},{2,3},{5,4},{4,5},{7,6},{6,7},{9,8},{8,9},{11,10... | collective-permute-start | bytes 1056776 | tf_op jit(solution)/shard_map/ppermute | solution.py:66
  (3 other events, 12.7 us)

commit v2 on v1

--- a/solution.py
+++ b/solution.py
@@ -15,14 +15,14 @@
 ONES = 16
 AHEAD = 2
 EDGE_FLOPS = 4 * 10**9
-CONV_MIB = 52
+STAGE_MIB = 46
 F32 = jnp.float32
 BF16 = jnp.bfloat16
 MIB = 1 << 20
 
 
 VMEM = pl.BlockSpec(memory_space=pltpu.VMEM)
-HBM = pl.BlockSpec(memory_space=pltpu.HBM)
+ANY = pl.BlockSpec(memory_space=pl.ANY)
 SMEM = pl.BlockSpec(memory_space=pltpu.SMEM)
 
 
@@ -113,14 +113,27 @@
     return left, right, above, below
 
 
+def stage_kernel(in_ref, out_ref, sem):
+    copy = pltpu.make_async_copy(in_ref, out_ref, sem)
+    copy.start()
+    copy.wait()
+
+
+def stage(array):
+    return pl.pallas_call(
+        stage_kernel,
+        out_shape=shape(*array.shape),
+        in_specs=[ANY],
+        out_specs=VMEM,
+        scratch_shapes=[pltpu.SemaphoreType.DMA],
+        compiler_params=grant(STAGE_MIB),
+        cost_estimate=cost(0, 2 * array.nbytes),
+        name="stage",
+    )(array)
+
+
 def conv_kernel(rows, cols, cores, x_ref, left_ref, right_ref, above_ref, below_ref, w_ref, *refs):
-    features_ref, *half_refs, shift0, shift1, shift2, taps, sem = refs
-    copies = [
-        pltpu.make_async_copy(w_ref.at[rows_of], taps.at[rows_of], sem.at[n])
-        for n, rows_of in enumerate((slice(0, 1), slice(1, 3)))
-    ]
-    for copy in copies:
-        copy.start()
+    features_ref, *half_refs, shift0, shift1, shift2 = refs
 
     def silu(v):
         v = v.astype(F32)
@@ -141,11 +154,9 @@
         shift2[at] = jnp.where(side == cols - 1, rcell, pltpu.roll(cells, cols - 1, 0)).astype(BF16)
     total = x_ref[...].astype(F32)
     for a in range(3):
-        if a < 2:
-            copies[a].wait()
         for b, shift in enumerate((shift0, shift1, shift2)):
             total = total + jnp.dot(
-                shift[a * cols:(a + rows) * cols], taps[a, b], preferred_element_type=F32
+                shift[a * cols:(a + rows) * cols], w_ref[a, b], preferred_element_type=F32
             )
     features = total.astype(BF16)
     features_ref[...] = features
@@ -170,12 +181,10 @@
     return pl.pallas_call(
         functools.partial(conv_kernel, rows, cols, cores),
         out_shape=(shape(tokens, channels),) + (shape(tokens // cores, channels),) * cores,
-        in_specs=[VMEM] * 5 + [HBM],
+        in_specs=[VMEM] * 6,
         out_specs=(VMEM,) * (1 + cores),
-        scratch_shapes=[pltpu.VMEM(((rows + 2) * cols, channels), BF16)] * 3 + [
-            pltpu.VMEM((3, 3, channels, channels), BF16), pltpu.SemaphoreType.DMA((2,)),
-        ],
-        compiler_params=grant(CONV_MIB),
+        scratch_shapes=[pltpu.VMEM(((rows + 2) * cols, channels), BF16)] * 3,
+        compiler_params=grant(24),
         cost_estimate=cost(18 * tokens * channels**2, 18 * channels**2, tokens * channels),
         name="conv_norm",
     )(cells.reshape(tokens, channels), *sides, conv_weight)
@@ -553,8 +562,10 @@
     anchors = anchor_index.shape[0]
     per_patch = tile_rows * tile_cols // BLOCK
     info = (anchors, images, cores, prows, per_patch)
+    features, *parts = conv_norm(latent[0], halo(latent[0]), stage(conv_weight), cores)
+    parts, *anchoring = lax.optimization_barrier((parts, anchor_index, block_count, block_order))
+    anchor_index, block_count, block_order = anchoring
     table = Table.build(anchor_index, block_count, block_order[:, :NSEL])
-    features, *parts = conv_norm(latent[0], halo(latent[0]), conv_weight, cores)
     keys, queries = [parts[0]], list(parts)
     for s in range(1, cores):
         theirs = [None] * cores

time: 67.5 us -> 70.4 us (1.043)
  starting transfers between devices: 26.9 us -> 29.7 us
  waiting for transfers between devices: 10.7 us -> 9.68 us
  Pallas kernels: 27.6 us -> 28.5 us
    pallas_call x0 -> x1, Pallas kernels: none -> 3.1 us  [stage(): pl.pallas_call(stage_kernel, out_shape=shape(*array.shape), in_specs=[ANY...]
    ppermute x2, starting transfers between devices: 3.54 us -> 6.28 us  [halo(): lax.ppermute(block, 'prow', pairs + [(j, i) for i, j in pairs])]
    pallas_call x1, Pallas kernels: 6.06 us -> 3.93 us  [conv_norm(): pl.pallas_call(functools.partial(conv_kernel, rows, cols, cores), out_sha...]
    ppermute x2, waiting for transfers between devices: 1.37 us -> 0.01 us  [halo(): lax.ppermute(block, 'prow', pairs + [(j, i) for i, j in pairs])]
  transfers between devices with their start and end apart: 18 -> 18, of which waited for: 6 -> 5; matrix products, arithmetic and copies ran while one was open for 0% -> 0% of each run, Pallas kernels for 19% -> 22%
where the time goes in v2:
time: 70.4 us; the launch traced here: 70.2 us
  starting transfers between devices  29.7 us (42%)
  Pallas kernels  28.5 us (40%)
  waiting for transfers between devices  9.68 us (14%)
  local copies, waits for them, and re-layouts  1.19 us (2%)
  between operations  0.9 us (1%)
    ppermute x12, starting transfers between devices, exchange(): lax.ppermute(block, axis, [(source_of(i, step, count), i) for i in range(...  22.3 us
    pallas_call x1, Pallas kernels, attend_anchors(): pl.pallas_call(functools.partial(anchor_kernel, info, len(keys), len(earl...  7.58 us
    pallas_call x1, Pallas kernels, attend_plane(): pl.pallas_call(functools.partial(plane_kernel, info, len(keys)), out_shap...  7.05 us
    ppermute x12, waiting for transfers between devices, exchange(): lax.ppermute(block, axis, [(source_of(i, step, count), i) for i in range(...  6.41 us
    ppermute x2, starting transfers between devices, halo(): lax.ppermute(block, 'prow', pairs + [(j, i) for i, j in pairs])  6.28 us
    pallas_call x1, Pallas kernels, attend_own(): pl.pallas_call(functools.partial(own_kernel, info, len(parts)), out_shape...  4.19 us
    pallas_call x1, Pallas kernels, conv_norm(): pl.pallas_call(functools.partial(conv_kernel, rows, cols, cores), out_sha...  3.93 us
    ppermute x4, waiting for transfers between devices, shifted(): lax.ppermute(block, axis, [((i + step) % count, i) for i in range(count)])  3.27 us
  transfers between devices with their start and end apart: 18, of which 5 were waited for; matrix products, arithmetic and copies ran while one was open for 0% of the time, Pallas kernels for 22%

profile of v2, /device:TPU:0, one launch (start us, length us, event | category | flops | bytes accessed | tf_op | source)
XLA Modules:
  0.0 70.2 jit_solution(5904851260478119026)
XLA Ops:
  0.6 1.0 %copy-done.1 = bf16[1,8,32,640]{3,2,1,0:T(8,128)(2,1)S(1)} copy-done((bf16[1,8,32,640]{3,2,1,0:T(8,128)(2,1)S(1)}, bf16[1,8,32,640]{3,2,1,0:T(8,128)(2,1)}, u32[]{:S(2)}) %copy-start.1) | copy-done | bytes 327704
  2.2 0.8 %collective-permute-done = bf16[8,640]{1,0:T(8,128)(2,1)S(1)} collective-permute-done((bf16[8,640]{1,0:T(8,128)(2,1)S(1)}, bf16[8,640]{1,0:T(8,128)(2,1)S(1)}, u32[]{:S(2)}, u32[]{:S(2)}) %collective-permute-start) | collective-permute-done | bytes 10272 | tf_op jit(solution)/shard_map/ppermute | solution.py:66
  3.1 0.7 collective-permute-start.2
  3.8 5.6 %collective-permute-start.1 = (bf16[34,640]{1,0:T(8,128)(2,1)S(1)}, bf16[34,640]{1,0:T(8,128)(2,1)S(1)}, u32[]{:S(2)}, u32[]{:S(2)}) collective-permute-start(bf16[34,640]{1,0:T(8,128)(2,1)S(1)} %get-tuple-element.53), channel_id=1, source_target_pairs={{0,2},{4,6},{2,0},{6,4},{1,3},{5,7},{3,1},{7,5},{8,10},{12,14},{10... | collective-permute-start | bytes 130568 | tf_op jit(solution)/shard_map/ppermute | solution.py:110
  9.4 3.1 %stage.1.w_ref = bf16[3,3,640,640]{3,2,1,0:T(8,128)(2,1)S(1)} custom-call(bf16[3,3,640,640]{3,2,1,0:T(8,128)(2,1)} %in_ref.1), custom_call_target="tpu_custom_call" | custom-call | bytes 14745600 | tf_op jit(solution)/shard_map/stage/pallas_call | solution.py:123
  12.7 3.9 %conv_norm.1 = (bf16[256,640]{1,0:T(8,128)(2,1)}, bf16[128,640]{1,0:T(8,128)(2,1)S(1)}, bf16[128,640]{1,0:T(8,128)(2,1)S(1)}) custom-call(bf16[256,640]{1,0:T(8,128)(2,1)S(1)} %bitcast.6, bf16[8,640]{1,0:T(8,128)(2,1)S(1)} %get-tuple-element.59.left_ref, bf16[8,640]{1,0:T(8,128)(2,1)S(1)} %get-tuple-element.58.right_ref, ...), custom_call_target="tpu_custom_call" | custom-call | flops 1887436800 | bytes 7372800 | tf_op jit(solution)/shard_map/conv_norm/pallas_call | solution.py:181
  17.3 0.8 %collective-permute-done.4.refs_3_ = bf16[128,640]{1,0:T(8,128)(2,1)S(1)} collective-permute-done((bf16[128,640]{1,0:T(8,128)(2,1)S(1)}, bf16[128,640]{1,0:T(8,128)(2,1)S(1)}, u32[]{:S(2)}, u32[]{:S(2)}) %collective-permute-start.4) | collective-permute-done | bytes 163872 | tf_op jit(solution)/shard_map/ppermute | solution.py:66
  18.7 1.0 %collective-permute-start.5 = (bf16[64,640]{1,0:T(8,128)(2,1)S(1)}, bf16[64,640]{1,0:T(8,128)(2,1)S(1)}, u32[]{:S(2)}, u32[]{:S(2)}) collective-permute-start(bf16[64,640]{1,0:T(8,128)(2,1)S(1)} %get-tuple-element.40), channel_id=1, source_target_pairs={{2,0},{0,2},{6,4},{4,6},{3,1},{1,3},{7,5},{5,7},{10,8},{8,10},{14,... | collective-permute-start | bytes 245768 | tf_op jit(solution)/shard_map/ppermute | solution.py:61
  19.7 1.1 %collective-permute-start.6 = (bf16[64,640]{1,0:T(8,128)(2,1)S(1)}, bf16[64,640]{1,0:T(8,128)(2,1)S(1)}, u32[]{:S(2)}, u32[]{:S(2)}) collective-permute-start(bf16[64,640]{1,0:T(8,128)(2,1)S(1)} %get-tuple-element.41), channel_id=1, source_target_pairs={{4,0},{6,2},{0,4},{2,6},{5,1},{7,3},{1,5},{3,7},{12,8},{14,10},{8,... | collective-permute-start | bytes 245768 | tf_op jit(solution)/shard_map/ppermute | solution.py:61
  20.8 1.5 %collective-permute-start.7 = (bf16[64,640]{1,0:T(8,128)(2,1)S(1)}, bf16[64,640]{1,0:T(8,128)(2,1)S(1)}, u32[]{:S(2)}, u32[]{:S(2)}) collective-permute-start(bf16[64,640]{1,0:T(8,128)(2,1)S(1)} %get-tuple-element.42), channel_id=1, source_target_pairs={{6,0},{4,2},{2,4},{0,6},{7,1},{5,3},{3,5},{1,7},{14,8},{12,10},{10... | collective-permute-start | bytes 245768 | tf_op jit(solution)/shard_map/ppermute | solution.py:61
  22.3 1.4 %collective-permute-start.16 = (bf16[256,640]{1,0:T(8,128)(2,1)S(1)}, bf16[256,640]{1,0:T(8,128)(2,1)S(1)}, u32[]{:S(2)}, u32[]{:S(2)}) collective-permute-start(bf16[256,640]{1,0:T(8,128)(2,1)S(1)} %constant_dynamic-update-slice_fusion.refs_4_.key_ref), channel_id=1, source_target_pairs={{6,0},{4,2},{2,4},{0,6},{7,1},{5,3},{3,5},{1,7},{14,8},{12,10},{10... | collective-permute-start | bytes 983048 | tf_op jit(solution)/shard_map/ppermute | solution.py:61
  23.7 0.9 %collective-permute-start.15 = (bf16[256,640]{1,0:T(8,128)(2,1)S(1)}, bf16[256,640]{1,0:T(8,128)(2,1)S(1)}, u32[]{:S(2)}, u32[]{:S(2)}) collective-permute-start(bf16[256,640]{1,0:T(8,128)(2,1)S(1)} %constant_dynamic-update-slice_fusion.refs_4_.key_ref), channel_id=1, source_target_pairs={{4,0},{6,2},{0,4},{2,6},{5,1},{7,3},{1,5},{3,7},{12,8},{14,10},{8,... | collective-permute-start | bytes 983048 | tf_op jit(solution)/shard_map/ppermute | solution.py:61
  25.0 8.4 %collective-permute-start.14 = (bf16[256,640]{1,0:T(8,128)(2,1)S(1)}, bf16[256,640]{1,0:T(8,128)(2,1)S(1)}, u32[]{:S(2)}, u32[]{:S(2)}) collective-permute-start(bf16[256,640]{1,0:T(8,128)(2,1)S(1)} %constant_dynamic-update-slice_fusion.refs_4_.key_ref), channel_id=1, source_target_pairs={{2,0},{0,2},{6,4},{4,6},{3,1},{1,3},{7,5},{5,7},{10,8},{8,10},{14,... | collective-permute-start | bytes 983048 | tf_op jit(solution)/shard_map/ppermute | solution.py:61
  33.4 0.8 %accept.1 = bf16[64,640]{1,0:T(8,128)(2,1)S(1)} custom-call(s32[24]{0:T(128)S(1)} %pad_add_fusion.table_ref, bf16[64,640]{1,0:T(8,128)(2,1)S(1)} %get-tuple-element.39.refs_0_, bf16[64,640]{1,0:T(8,128)(2,1)S(1)} %collective-permute-done.5.refs_1_, bf16[64,640]{1,0:T(8,128)(2,1)S(1)} %collective-permute-done.6.refs_2_, ...), custom_call_target="tpu_custom_call" | custom-call | tf_op jit(solution)/shard_map/accept/pallas_call | solution.py:534
  34.2 1.7 %collective-permute-start.8 = (bf16[64,640]{1,0:T(8,128)(2,1)S(1)}, bf16[64,640]{1,0:T(8,128)(2,1)S(1)}, u32[]{:S(2)}, u32[]{:S(2)}) collective-permute-start(bf16[64,640]{1,0:T(8,128)(2,1)S(1)} %accept.1), channel_id=1, source_target_pairs={{8,0},{0,8},{24,16},{16,24},{9,1},{1,9},{25,17},{17,25},{10,2},{2,... | collective-permute-start | bytes 245768 | tf_op jit(solution)/shard_map/ppermute | solution.py:61
  35.9 4.2 %attend_own.1 = (bf16[640,512]{1,0:T(8,128)(2,1)S(1)}, bf16[640,512]{1,0:T(8,128)(2,1)S(1)}, f32[10,8,512]{2,1,0:T(8,128)S(1)}) custom-call(s32[24]{0:T(128)S(1)} %pad_add_fusion.table_ref, bf16[128,640]{1,0:T(8,128)(2,1)S(1)} %get-tuple-element.36.refs_0_, bf16[128,640]{1,0:T(8,128)(2,1)S(1)} %get-tuple-element.37.refs_1_, ...), custom_call_target="tpu_custom_call" | custom-call | flops 2181038080 | bytes 1638400 | tf_op jit(solution)/shard_map/attend_own/pallas_call | solution.py:313
  40.1 2.5 %collective-permute-start.10 = (bf16[64,640]{1,0:T(8,128)(2,1)S(1)}, bf16[64,640]{1,0:T(8,128)(2,1)S(1)}, u32[]{:S(2)}, u32[]{:S(2)}) collective-permute-start(bf16[64,640]{1,0:T(8,128)(2,1)S(1)} %accept.1), channel_id=1, source_target_pairs={{24,0},{16,8},{8,16},{0,24},{25,1},{17,9},{9,17},{1,25},{26,2},{18... | collective-permute-start | bytes 245768 | tf_op jit(solution)/shard_map/ppermute | solution.py:61
  42.8 6.0 %collective-permute-done.9 = bf16[64,640]{1,0:T(8,128)(2,1)S(1)} collective-permute-done((bf16[64,640]{1,0:T(8,128)(2,1)S(1)}, bf16[64,640]{1,0:T(8,128)(2,1)S(1)}, u32[]{:S(2)}, u32[]{:S(2)}) %collective-permute-start.9) | collective-permute-done | bytes 81952 | tf_op jit(solution)/shard_map/ppermute | solution.py:61
  48.9 1.4 %collective-permute-start.13 = (bf16[192,640]{1,0:T(8,128)(2,1)S(1)}, bf16[192,640]{1,0:T(8,128)(2,1)S(1)}, u32[]{:S(2)}, u32[]{:S(2)}) collective-permute-start(bf16[192,640]{1,0:T(8,128)(2,1)S(1)} %constant_dynamic-update-slice_fusion.2.refs_0_), channel_id=1, source_target_pairs={{6,0},{4,2},{2,4},{0,6},{7,1},{5,3},{3,5},{1,7},{14,8},{12,10},{10... | collective-permute-start | bytes 737288 | tf_op jit(solution)/shard_map/ppermute | solution.py:61
  50.4 2.0 %collective-permute-start.11 = (bf16[192,640]{1,0:T(8,128)(2,1)S(1)}, bf16[192,640]{1,0:T(8,128)(2,1)S(1)}, u32[]{:S(2)}, u32[]{:S(2)}) collective-permute-start(bf16[192,640]{1,0:T(8,128)(2,1)S(1)} %constant_dynamic-update-slice_fusion.2.refs_0_), channel_id=1, source_target_pairs={{2,0},{0,2},{6,4},{4,6},{3,1},{1,3},{7,5},{5,7},{10,8},{8,10},{14,... | collective-permute-start | bytes 737288 | tf_op jit(solution)/shard_map/ppermute | solution.py:61
  52.5 7.0 %attend_plane.1 = (bf16[640,512]{1,0:T(8,128)(2,1)S(1)}, f32[10,8,512]{2,1,0:T(8,128)S(1)}) custom-call(s32[24]{0:T(128)S(1)} %pad_add_fusion.table_ref, bf16[640,512]{1,0:T(8,128)(2,1)S(1)} %get-tuple-element.38.q_ref, bf16[256,640]{1,0:T(8,128)(2,1)S(1)} %collective-permute-done.14.refs_0_, bf16[256,640]{1,0:T(8,128)(2,1)S(1)} %collective-permute-done.15.refs_1_, ...), custom_call_target="tpu_custom_call" | custom-call | flops 5284823040 | bytes 2293760 | tf_op jit(solution)/shard_map/attend_plane/pallas_call | solution.py:345
  59.6 7.6 %attend_anchors.1 = (bf16[640,256]{1,0:T(8,128)(2,1)S(1)}, f32[16,256]{1,0:T(8,128)S(1)}, bf16[688,256]{1,0:T(8,128)(2,1)S(1)}) custom-call(s32[24]{0:T(128)S(1)} %pad_add_fusion.table_ref, bf16[640,512]{1,0:T(8,128)(2,1)S(1)} %get-tuple-element.38.q_ref, bf16[192,640]{1,0:T(8,128)(2,1)S(1)} %constant_dynamic-update-slice_fusion.2.refs_0_, ...), custom_call_target="tpu_custom_call" | custom-call | flops 5284823040 | bytes 2293760 | tf_op jit(solution)/shard_map/attend_anchors/pallas_call | solution.py:422
  67.2 1.7 %collective-permute-done.17.refs_0_ = bf16[688,256]{1,0:T(8,128)(2,1)S(1)} collective-permute-done((bf16[688,256]{1,0:T(8,128)(2,1)S(1)}, bf16[688,256]{1,0:T(8,128)(2,1)S(1)}, u32[]{:S(2)}, u32[]{:S(2)}) %collective-permute-start.17) | collective-permute-done | bytes 352288 | tf_op jit(solution)/shard_map/ppermute | solution.py:66
  68.9 1.3 %finish.1 = bf16[256,640]{1,0:T(8,128)(2,1)} custom-call(bf16[640,256]{1,0:T(8,128)(2,1)S(1)} %get-tuple-element.47.own_ref, f32[16,256]{1,0:T(8,128)S(1)} %get-tuple-element.48.level_ref, bf16[688,256]{1,0:T(8,128)(2,1)S(1)} %collective-permute-done.17.refs_0_, bf16[640,640]{1,0:T(8,128)(2,1)S(1)} %copy-done), custom_call_target="tpu_custom_call" | custom-call | flops 209715200 | bytes 1802240 | tf_op jit(solution)/shard_map/finish/pallas_call | solution.py:472
  (51 shorter events, 2.8 us)
Async XLA Ops:
  1.7 1.4 %collective-permute-start = (bf16[8,640]{1,0:T(8,128)(2,1)S(1)}, bf16[8,640]{1,0:T(8,128)(2,1)S(1)}, u32[]{:S(2)}, u32[]{:S(2)}) collective-permute-start(bf16[8,640]{1,0:T(8,128)(2,1)S(1)} %broadcast_select_fusion.5), channel_id=1, source_target_pairs={{1,0},{0,1},{3,2},{2,3},{5,4},{4,5},{7,6},{6,7},{9,8},{8,9},{11,10... | collective-permute-start | bytes 30728 | tf_op jit(solution)/shard_map/ppermute | solution.py:66
  3.1 9.5 %collective-permute-start.2 = (bf16[34,640]{1,0:T(8,128)(2,1)S(1)}, bf16[34,640]{1,0:T(8,128)(2,1)S(1)}, u32[]{:S(2)}, u32[]{:S(2)}) collective-permute-start(bf16[34,640]{1,0:T(8,128)(2,1)S(1)} %get-tuple-element.52), channel_id=1, source_target_pairs={{2,4},{4,2},{3,5},{5,3},{10,12},{12,10},{11,13},{13,11},{18,20},{2... | collective-permute-start | bytes 130568 | tf_op jit(solution)/shard_map/ppermute | solution.py:110
  3.8 8.9 %copy-start.2 = (bf16[1,8,32,640]{3,2,1,0:T(8,128)(2,1)S(1)}, bf16[1,8,32,640]{3,2,1,0:T(8,128)(2,1)}, u32[]{:S(2)}) copy-start(bf16[1,8,32,640]{3,2,1,0:T(8,128)(2,1)} %param.9) | copy-start | bytes 983044
  3.8 8.8 %collective-permute-start.1 = (bf16[34,640]{1,0:T(8,128)(2,1)S(1)}, bf16[34,640]{1,0:T(8,128)(2,1)S(1)}, u32[]{:S(2)}, u32[]{:S(2)}) collective-permute-start(bf16[34,640]{1,0:T(8,128)(2,1)S(1)} %get-tuple-element.53), channel_id=1, source_target_pairs={{0,2},{4,6},{2,0},{6,4},{1,3},{5,7},{3,1},{7,5},{8,10},{12,14},{10... | collective-permute-start | bytes 130568 | tf_op jit(solution)/shard_map/ppermute | solution.py:110
  12.6 4.6 %copy-start.7 = (s32[4]{0:T(128)S(1)}, s32[4]{0:T(128)}, u32[]{:S(2)}) copy-start(s32[4]{0:T(128)} %param.17) | copy-start | bytes 52
  12.6 23.3 %copy-start.3 = (bf16[640,640]{1,0:T(8,128)(2,1)S(1)}, bf16[640,640]{1,0:T(8,128)(2,1)}, u32[]{:S(2)}) copy-start(bf16[640,640]{1,0:T(8,128)(2,1)} %refs_5_.1) | copy-start | bytes 2457604
  12.6 23.3 %copy-start.4 = (bf16[640,640]{1,0:T(8,128)(2,1)S(1)}, bf16[640,640]{1,0:T(8,128)(2,1)}, u32[]{:S(2)}) copy-start(bf16[640,640]{1,0:T(8,128)(2,1)} %refs_8_.1) | copy-start | bytes 2457604
  12.6 23.3 %copy-start.5 = (bf16[640,640]{1,0:T(8,128)(2,1)S(1)}, bf16[640,640]{1,0:T(8,128)(2,1)}, u32[]{:S(2)}) copy-start(bf16[640,640]{1,0:T(8,128)(2,1)} %refs_9_.1) | copy-start | bytes 2457604
  16.7 1.4 %collective-permute-start.4 = (bf16[128,640]{1,0:T(8,128)(2,1)S(1)}, bf16[128,640]{1,0:T(8,128)(2,1)S(1)}, u32[]{:S(2)}, u32[]{:S(2)}) collective-permute-start(bf16[128,640]{1,0:T(8,128)(2,1)S(1)} %get-tuple-element.37.refs_1_), channel_id=1, source_target_pairs={{1,0},{0,1},{3,2},{2,3},{5,4},{4,5},{7,6},{6,7},{9,8},{8,9},{11,10... | collective-permute-start | bytes 491528 | tf_op jit(solution)/shard_map/ppermute | solution.py:66
  16.7 19.2 %collective-permute-start.3 = (bf16[128,640]{1,0:T(8,128)(2,1)S(1)}, bf16[128,640]{1,0:T(8,128)(2,1)S(1)}, u32[]{:S(2)}, u32[]{:S(2)}) collective-permute-start(bf16[128,640]{1,0:T(8,128)(2,1)S(1)} %get-tuple-element.36.refs_0_), channel_id=1, source_target_pairs={{1,0},{0,1},{3,2},{2,3},{5,4},{4,5},{7,6},{6,7},{9,8},{8,9},{11,10... | collective-permute-start | bytes 491528 | tf_op jit(solution)/shard_map/ppermute | solution.py:66
  18.7 5.0 %collective-permute-start.5 = (bf16[64,640]{1,0:T(8,128)(2,1)S(1)}, bf16[64,640]{1,0:T(8,128)(2,1)S(1)}, u32[]{:S(2)}, u32[]{:S(2)}) collective-permute-start(bf16[64,640]{1,0:T(8,128)(2,1)S(1)} %get-tuple-element.40), channel_id=1, source_target_pairs={{2,0},{0,2},{6,4},{4,6},{3,1},{1,3},{7,5},{5,7},{10,8},{8,10},{14,... | collective-permute-start | bytes 245768 | tf_op jit(solution)/shard_map/ppermute | solution.py:61
  19.7 5.3 %collective-permute-start.6 = (bf16[64,640]{1,0:T(8,128)(2,1)S(1)}, bf16[64,640]{1,0:T(8,128)(2,1)S(1)}, u32[]{:S(2)}, u32[]{:S(2)}) collective-permute-start(bf16[64,640]{1,0:T(8,128)(2,1)S(1)} %get-tuple-element.41), channel_id=1, source_target_pairs={{4,0},{6,2},{0,4},{2,6},{5,1},{7,3},{1,5},{3,7},{12,8},{14,10},{8,... | collective-permute-start | bytes 245768 | tf_op jit(solution)/shard_map/ppermute | solution.py:61
  20.8 12.7 %collective-permute-start.7 = (bf16[64,640]{1,0:T(8,128)(2,1)S(1)}, bf16[64,640]{1,0:T(8,128)(2,1)S(1)}, u32[]{:S(2)}, u32[]{:S(2)}) collective-permute-start(bf16[64,640]{1,0:T(8,128)(2,1)S(1)} %get-tuple-element.42), channel_id=1, source_target_pairs={{6,0},{4,2},{2,4},{0,6},{7,1},{5,3},{3,5},{1,7},{14,8},{12,10},{10... | collective-permute-start | bytes 245768 | tf_op jit(solution)/shard_map/ppermute | solution.py:61
  22.3 28.2 %collective-permute-start.16 = (bf16[256,640]{1,0:T(8,128)(2,1)S(1)}, bf16[256,640]{1,0:T(8,128)(2,1)S(1)}, u32[]{:S(2)}, u32[]{:S(2)}) collective-permute-start(bf16[256,640]{1,0:T(8,128)(2,1)S(1)} %constant_dynamic-update-slice_fusion.refs_4_.key_ref), channel_id=1, source_target_pairs={{6,0},{4,2},{2,4},{0,6},{7,1},{5,3},{3,5},{1,7},{14,8},{12,10},{10... | collective-permute-start | bytes 983048 | tf_op jit(solution)/shard_map/ppermute | solution.py:61
  23.7 28.8 %collective-permute-start.15 = (bf16[256,640]{1,0:T(8,128)(2,1)S(1)}, bf16[256,640]{1,0:T(8,128)(2,1)S(1)}, u32[]{:S(2)}, u32[]{:S(2)}) collective-permute-start(bf16[256,640]{1,0:T(8,128)(2,1)S(1)} %constant_dynamic-update-slice_fusion.refs_4_.key_ref), channel_id=1, source_target_pairs={{4,0},{6,2},{0,4},{2,6},{5,1},{7,3},{1,5},{3,7},{12,8},{14,10},{8,... | collective-permute-start | bytes 983048 | tf_op jit(solution)/shard_map/ppermute | solution.py:61
  25.0 27.5 %collective-permute-start.14 = (bf16[256,640]{1,0:T(8,128)(2,1)S(1)}, bf16[256,640]{1,0:T(8,128)(2,1)S(1)}, u32[]{:S(2)}, u32[]{:S(2)}) collective-permute-start(bf16[256,640]{1,0:T(8,128)(2,1)S(1)} %constant_dynamic-update-slice_fusion.refs_4_.key_ref), channel_id=1, source_target_pairs={{2,0},{0,2},{6,4},{4,6},{3,1},{1,3},{7,5},{5,7},{10,8},{8,10},{14,... | collective-permute-start | bytes 983048 | tf_op jit(solution)/shard_map/ppermute | solution.py:61
  34.2 8.4 %collective-permute-start.8 = (bf16[64,640]{1,0:T(8,128)(2,1)S(1)}, bf16[64,640]{1,0:T(8,128)(2,1)S(1)}, u32[]{:S(2)}, u32[]{:S(2)}) collective-permute-start(bf16[64,640]{1,0:T(8,128)(2,1)S(1)} %accept.1), channel_id=1, source_target_pairs={{8,0},{0,8},{24,16},{16,24},{9,1},{1,9},{25,17},{17,25},{10,2},{2,... | collective-permute-start | bytes 245768 | tf_op jit(solution)/shard_map/ppermute | solution.py:61
  40.1 8.8 %collective-permute-start.10 = (bf16[64,640]{1,0:T(8,128)(2,1)S(1)}, bf16[64,640]{1,0:T(8,128)(2,1)S(1)}, u32[]{:S(2)}, u32[]{:S(2)}) collective-permute-start(bf16[64,640]{1,0:T(8,128)(2,1)S(1)} %accept.1), channel_id=1, source_target_pairs={{24,0},{16,8},{8,16},{0,24},{25,1},{17,9},{9,17},{1,25},{26,2},{18... | collective-permute-start | bytes 245768 | tf_op jit(solution)/shard_map/ppermute | solution.py:61
  42.6 6.2 %collective-permute-start.9 = (bf16[64,640]{1,0:T(8,128)(2,1)S(1)}, bf16[64,640]{1,0:T(8,128)(2,1)S(1)}, u32[]{:S(2)}, u32[]{:S(2)}) collective-permute-start(bf16[64,640]{1,0:T(8,128)(2,1)S(1)} %accept.1), channel_id=1, source_target_pairs={{16,0},{24,8},{0,16},{8,24},{17,1},{25,9},{1,17},{9,25},{18,2},{26... | collective-permute-start | bytes 245768 | tf_op jit(solution)/shard_map/ppermute | solution.py:61
  48.9 10.6 %collective-permute-start.13 = (bf16[192,640]{1,0:T(8,128)(2,1)S(1)}, bf16[192,640]{1,0:T(8,128)(2,1)S(1)}, u32[]{:S(2)}, u32[]{:S(2)}) collective-permute-start(bf16[192,640]{1,0:T(8,128)(2,1)S(1)} %constant_dynamic-update-slice_fusion.2.refs_0_), channel_id=1, source_target_pairs={{6,0},{4,2},{2,4},{0,6},{7,1},{5,3},{3,5},{1,7},{14,8},{12,10},{10... | collective-permute-start | bytes 737288 | tf_op jit(solution)/shard_map/ppermute | solution.py:61
  50.3 9.2 %collective-permute-start.12 = (bf16[192,640]{1,0:T(8,128)(2,1)S(1)}, bf16[192,640]{1,0:T(8,128)(2,1)S(1)}, u32[]{:S(2)}, u32[]{:S(2)}) collective-permute-start(bf16[192,640]{1,0:T(8,128)(2,1)S(1)} %constant_dynamic-update-slice_fusion.2.refs_0_), channel_id=1, source_target_pairs={{4,0},{6,2},{0,4},{2,6},{5,1},{7,3},{1,5},{3,7},{12,8},{14,10},{8,... | collective-permute-start | bytes 737288 | tf_op jit(solution)/shard_map/ppermute | solution.py:61
  50.4 9.1 %collective-permute-start.11 = (bf16[192,640]{1,0:T(8,128)(2,1)S(1)}, bf16[192,640]{1,0:T(8,128)(2,1)S(1)}, u32[]{:S(2)}, u32[]{:S(2)}) collective-permute-start(bf16[192,640]{1,0:T(8,128)(2,1)S(1)} %constant_dynamic-update-slice_fusion.2.refs_0_), channel_id=1, source_target_pairs={{2,0},{0,2},{6,4},{4,6},{3,1},{1,3},{7,5},{5,7},{10,8},{8,10},{14,... | collective-permute-start | bytes 737288 | tf_op jit(solution)/shard_map/ppermute | solution.py:61
  59.6 9.3 %copy-start = (bf16[640,640]{1,0:T(8,128)(2,1)S(1)}, bf16[640,640]{1,0:T(8,128)(2,1)}, u32[]{:S(2)}) copy-start(bf16[640,640]{1,0:T(8,128)(2,1)} %refs_1_.1) | copy-start | bytes 2457604
  67.2 1.7 %collective-permute-start.17 = (bf16[688,256]{1,0:T(8,128)(2,1)S(1)}, bf16[688,256]{1,0:T(8,128)(2,1)S(1)}, u32[]{:S(2)}, u32[]{:S(2)}) collective-permute-start(bf16[688,256]{1,0:T(8,128)(2,1)S(1)} %get-tuple-element.49), channel_id=1, source_target_pairs={{1,0},{0,1},{3,2},{2,3},{5,4},{4,5},{7,6},{6,7},{9,8},{8,9},{11,10... | collective-permute-start | bytes 1056776 | tf_op jit(solution)/shard_map/ppermute | solution.py:66
  (3 other events, 9.7 us)

commit v3 on v2

--- a/solution.py
+++ b/solution.py
@@ -64,6 +64,27 @@
 def shifted(block, axis, step):
     count = lax.axis_size(axis)
     return lax.ppermute(block, axis, [((i + step) % count, i) for i in range(count)])
+
+
+def crossed(core, entry, prows):
+    if prows != 4 or entry not in (1, 2):
+        return entry
+    return jnp.where(lax.rem(core, 2) == 1, 3 - entry, entry)
+
+
+def gathered(block):
+    prows, cores = lax.axis_size("prow"), lax.axis_size("pcol")
+    if prows != 4:
+        return [exchange(block, "prow", s) for s in range(1, prows)]
+
+    def hop(rows, entry):
+        return lax.ppermute(rows, ("prow", "pcol"), [
+            ((p ^ (entry if c % 2 == 0 else 3 - entry)) * cores + c, p * cores + c)
+            for p in range(prows) for c in range(cores)
+        ])
+
+    near, side = hop(block, 1), hop(block, 2)
+    return [near, side, hop(near, 2)]
 
 
 def edges_kernel(x_ref, first_ref, last_ref, top_ref, bottom_ref):
@@ -215,8 +236,9 @@
         if not self.every_image:
             return jnp.float32(1.0)
         s, b = divmod(group, per_patch)
-        patch = source_of(lax.axis_index("prow"), step, prows) * cores
-        block = (patch + lax.rem(lax.axis_index("pcol") + s, cores)) * per_patch + b
+        core = lax.axis_index("pcol")
+        patch = source_of(lax.axis_index("prow"), crossed(core, step, prows), prows) * cores
+        block = (patch + lax.rem(core + s, cores)) * per_patch + b
         anchor = self.anchor_at(lax.axis_index("image"))
         times = jnp.float32(1.0)
         for slot in range(NSEL):
@@ -577,17 +599,21 @@
     every_image = anchors == images
     if every_image:
         mine, *offers = offer(info, table, key)
-        offers = [mine] + [exchange(rows, "prow", s) for s, rows in enumerate(offers, 1)]
-    plane = [exchange(key, "prow", s) for s in range(1, prows)]
+        received = [mine]
+        for s, rows in enumerate(offers, 1):
+            received.append(exchange(rows, "prow", s))
+    plane = gathered(key)
     q, value, level = attend_own(info, table, queries, key, w_query, w_key, w_value)
     done = [(value, level)]
     if every_image:
-        share = accept(info, table, offers)
+        share = accept(info, table, received)
         across = []
         for s in range(1, images):
             across.append(exchange(share, "image", s))
         local = jnp.concatenate(across, axis=0)
-        sources = [local] + [exchange(local, "prow", s) for s in range(1, prows)]
+        sources = [local]
+        for s in range(1, prows):
+            sources.append(exchange(local, "prow", s))
     else:
         joined = anchor_rows(key, anchor_index, block_order, block_count, cores, per_patch)
         sources = [joined[anchor] for anchor in range(anchors)]

time: 70.4 us -> 73 us (1.037)
  waiting for transfers between devices: 9.68 us -> 20.1 us
  starting transfers between devices: 29.7 us -> 21.9 us
    ppermute x12 -> x9, starting transfers between devices: 22.3 us -> 11.5 us  [exchange(): lax.ppermute(block, axis, [(source_of(i, step, count), i) for i in range(...]
    ppermute x0 -> x3, waiting for transfers between devices: none -> 5.35 us  [hop(): lax.ppermute(rows, ('prow', 'pcol'), [((p ^ (entry if c % 2 == 0 else 3 -...]
    ppermute x12 -> x9, waiting for transfers between devices: 6.41 us -> 11.5 us  [exchange(): lax.ppermute(block, axis, [(source_of(i, step, count), i) for i in range(...]
    ppermute x0 -> x3, starting transfers between devices: none -> 3 us  [hop(): lax.ppermute(rows, ('prow', 'pcol'), [((p ^ (entry if c % 2 == 0 else 3 -...]
  transfers between devices with their start and end apart: 18 -> 18, of which waited for: 5 -> 7; matrix products, arithmetic and copies ran while one was open for 0% -> 0% of each run, Pallas kernels for 22% -> 22%
where the time goes in v3:
time: 73 us; the launch traced here: 72.8 us
  Pallas kernels  28.6 us (39%)
  starting transfers between devices  21.9 us (30%)
  waiting for transfers between devices  20.1 us (28%)
  local copies, waits for them, and re-layouts  1.19 us (2%)
  between operations  0.89 us (1%)
    ppermute x9, starting transfers between devices, exchange(): lax.ppermute(block, axis, [(source_of(i, step, count), i) for i in range(...  11.5 us
    ppermute x9, waiting for transfers between devices, exchange(): lax.ppermute(block, axis, [(source_of(i, step, count), i) for i in range(...  11.5 us
    pallas_call x1, Pallas kernels, attend_anchors(): pl.pallas_call(functools.partial(anchor_kernel, info, len(keys), len(earl...  7.61 us
    pallas_call x1, Pallas kernels, attend_plane(): pl.pallas_call(functools.partial(plane_kernel, info, len(keys)), out_shap...  7.06 us
    ppermute x2, starting transfers between devices, halo(): lax.ppermute(block, 'prow', pairs + [(j, i) for i, j in pairs])  6.28 us
    ppermute x3, waiting for transfers between devices, hop(): lax.ppermute(rows, ('prow', 'pcol'), [((p ^ (entry if c % 2 == 0 else 3 -...  5.35 us
    pallas_call x1, Pallas kernels, attend_own(): pl.pallas_call(functools.partial(own_kernel, info, len(parts)), out_shape...  4.18 us
    pallas_call x1, Pallas kernels, conv_norm(): pl.pallas_call(functools.partial(conv_kernel, rows, cols, cores), out_sha...  3.93 us
  transfers between devices with their start and end apart: 18, of which 7 were waited for; matrix products, arithmetic and copies ran while one was open for 0% of the time, Pallas kernels for 22%

profile of v3, /device:TPU:0, one launch (start us, length us, event | category | flops | bytes accessed | tf_op | source)
XLA Modules:
  0.0 72.8 jit_solution(3145358173153851048)
XLA Ops:
  0.6 1.0 %copy-done.1 = bf16[1,8,32,640]{3,2,1,0:T(8,128)(2,1)S(1)} copy-done((bf16[1,8,32,640]{3,2,1,0:T(8,128)(2,1)S(1)}, bf16[1,8,32,640]{3,2,1,0:T(8,128)(2,1)}, u32[]{:S(2)}) %copy-start.1) | copy-done | bytes 327704
  2.2 0.8 %collective-permute-done = bf16[8,640]{1,0:T(8,128)(2,1)S(1)} collective-permute-done((bf16[8,640]{1,0:T(8,128)(2,1)S(1)}, bf16[8,640]{1,0:T(8,128)(2,1)S(1)}, u32[]{:S(2)}, u32[]{:S(2)}) %collective-permute-start) | collective-permute-done | bytes 10272 | tf_op jit(solution)/shard_map/ppermute | solution.py:66
  3.8 5.6 %collective-permute-start.1 = (bf16[34,640]{1,0:T(8,128)(2,1)S(1)}, bf16[34,640]{1,0:T(8,128)(2,1)S(1)}, u32[]{:S(2)}, u32[]{:S(2)}) collective-permute-start(bf16[34,640]{1,0:T(8,128)(2,1)S(1)} %get-tuple-element.53), channel_id=1, source_target_pairs={{0,2},{4,6},{2,0},{6,4},{1,3},{5,7},{3,1},{7,5},{8,10},{12,14},{10... | collective-permute-start | bytes 130568 | tf_op jit(solution)/shard_map/ppermute | solution.py:131
  9.4 3.1 %stage.1.w_ref = bf16[3,3,640,640]{3,2,1,0:T(8,128)(2,1)S(1)} custom-call(bf16[3,3,640,640]{3,2,1,0:T(8,128)(2,1)} %in_ref.1), custom_call_target="tpu_custom_call" | custom-call | bytes 14745600 | tf_op jit(solution)/shard_map/stage/pallas_call | solution.py:144
  12.7 3.9 %conv_norm.1 = (bf16[256,640]{1,0:T(8,128)(2,1)}, bf16[128,640]{1,0:T(8,128)(2,1)S(1)}, bf16[128,640]{1,0:T(8,128)(2,1)S(1)}) custom-call(bf16[256,640]{1,0:T(8,128)(2,1)S(1)} %bitcast.6, bf16[8,640]{1,0:T(8,128)(2,1)S(1)} %get-tuple-element.59.left_ref, bf16[8,640]{1,0:T(8,128)(2,1)S(1)} %get-tuple-element.58.right_ref, ...), custom_call_target="tpu_custom_call" | custom-call | flops 1887436800 | bytes 7372800 | tf_op jit(solution)/shard_map/conv_norm/pallas_call | solution.py:202
  17.2 0.8 %collective-permute-done.4.refs_3_ = bf16[128,640]{1,0:T(8,128)(2,1)S(1)} collective-permute-done((bf16[128,640]{1,0:T(8,128)(2,1)S(1)}, bf16[128,640]{1,0:T(8,128)(2,1)S(1)}, u32[]{:S(2)}, u32[]{:S(2)}) %collective-permute-start.4) | collective-permute-done | bytes 163872 | tf_op jit(solution)/shard_map/ppermute | solution.py:66
  18.0 1.0 %collective-permute-start.14 = (bf16[256,640]{1,0:T(8,128)(2,1)S(1)}, bf16[256,640]{1,0:T(8,128)(2,1)S(1)}, u32[]{:S(2)}, u32[]{:S(2)}) collective-permute-start(bf16[256,640]{1,0:T(8,128)(2,1)S(1)} %constant_dynamic-update-slice_fusion.refs_4_.key_ref), channel_id=1, source_target_pairs={{2,0},{5,1},{0,2},{7,3},{6,4},{1,5},{4,6},{3,7},{10,8},{13,9},{8,1... | collective-permute-start | bytes 983048 | tf_op jit(solution)/shard_map/ppermute | solution.py:81
  19.7 1.2 %collective-permute-start.5 = (bf16[64,640]{1,0:T(8,128)(2,1)S(1)}, bf16[64,640]{1,0:T(8,128)(2,1)S(1)}, u32[]{:S(2)}, u32[]{:S(2)}) collective-permute-start(bf16[64,640]{1,0:T(8,128)(2,1)S(1)} %get-tuple-element.40), channel_id=1, source_target_pairs={{2,0},{0,2},{6,4},{4,6},{3,1},{1,3},{7,5},{5,7},{10,8},{8,10},{14,... | collective-permute-start | bytes 245768 | tf_op jit(solution)/shard_map/ppermute | solution.py:61
  20.9 0.9 %collective-permute-start.6 = (bf16[64,640]{1,0:T(8,128)(2,1)S(1)}, bf16[64,640]{1,0:T(8,128)(2,1)S(1)}, u32[]{:S(2)}, u32[]{:S(2)}) collective-permute-start(bf16[64,640]{1,0:T(8,128)(2,1)S(1)} %get-tuple-element.41), channel_id=1, source_target_pairs={{4,0},{6,2},{0,4},{2,6},{5,1},{7,3},{1,5},{3,7},{12,8},{14,10},{8,... | collective-permute-start | bytes 245768 | tf_op jit(solution)/shard_map/ppermute | solution.py:61
  21.8 1.5 %collective-permute-start.7 = (bf16[64,640]{1,0:T(8,128)(2,1)S(1)}, bf16[64,640]{1,0:T(8,128)(2,1)S(1)}, u32[]{:S(2)}, u32[]{:S(2)}) collective-permute-start(bf16[64,640]{1,0:T(8,128)(2,1)S(1)} %get-tuple-element.42), channel_id=1, source_target_pairs={{6,0},{4,2},{2,4},{0,6},{7,1},{5,3},{3,5},{1,7},{14,8},{12,10},{10... | collective-permute-start | bytes 245768 | tf_op jit(solution)/shard_map/ppermute | solution.py:61
  23.2 5.7 %collective-permute-done.5.refs_1_ = bf16[64,640]{1,0:T(8,128)(2,1)S(1)} collective-permute-done((bf16[64,640]{1,0:T(8,128)(2,1)S(1)}, bf16[64,640]{1,0:T(8,128)(2,1)S(1)}, u32[]{:S(2)}, u32[]{:S(2)}) %collective-permute-start.5) | collective-permute-done | bytes 81952 | tf_op jit(solution)/shard_map/ppermute | solution.py:61
  29.5 1.2 %collective-permute-done.7.refs_3_ = bf16[64,640]{1,0:T(8,128)(2,1)S(1)} collective-permute-done((bf16[64,640]{1,0:T(8,128)(2,1)S(1)}, bf16[64,640]{1,0:T(8,128)(2,1)S(1)}, u32[]{:S(2)}, u32[]{:S(2)}) %collective-permute-start.7) | collective-permute-done | bytes 81952 | tf_op jit(solution)/shard_map/ppermute | solution.py:61
  31.5 1.6 %collective-permute-start.8 = (bf16[64,640]{1,0:T(8,128)(2,1)S(1)}, bf16[64,640]{1,0:T(8,128)(2,1)S(1)}, u32[]{:S(2)}, u32[]{:S(2)}) collective-permute-start(bf16[64,640]{1,0:T(8,128)(2,1)S(1)} %accept.1), channel_id=1, source_target_pairs={{8,0},{0,8},{24,16},{16,24},{9,1},{1,9},{25,17},{17,25},{10,2},{2,... | collective-permute-start | bytes 245768 | tf_op jit(solution)/shard_map/ppermute | solution.py:61
  33.2 4.2 %attend_own.1 = (bf16[640,512]{1,0:T(8,128)(2,1)S(1)}, bf16[640,512]{1,0:T(8,128)(2,1)S(1)}, f32[10,8,512]{2,1,0:T(8,128)S(1)}) custom-call(s32[24]{0:T(128)S(1)} %pad_add_fusion.table_ref, bf16[128,640]{1,0:T(8,128)(2,1)S(1)} %get-tuple-element.36.refs_0_, bf16[128,640]{1,0:T(8,128)(2,1)S(1)} %get-tuple-element.37.refs_1_, ...), custom_call_target="tpu_custom_call" | custom-call | flops 2181038080 | bytes 1638400 | tf_op jit(solution)/shard_map/attend_own/pallas_call | solution.py:335
  37.4 2.5 %collective-permute-start.10 = (bf16[64,640]{1,0:T(8,128)(2,1)S(1)}, bf16[64,640]{1,0:T(8,128)(2,1)S(1)}, u32[]{:S(2)}, u32[]{:S(2)}) collective-permute-start(bf16[64,640]{1,0:T(8,128)(2,1)S(1)} %accept.1), channel_id=1, source_target_pairs={{24,0},{16,8},{8,16},{0,24},{25,1},{17,9},{9,17},{1,25},{26,2},{18... | collective-permute-start | bytes 245768 | tf_op jit(solution)/shard_map/ppermute | solution.py:61
  40.1 1.4 %collective-permute-start.16 = (bf16[256,640]{1,0:T(8,128)(2,1)S(1)}, bf16[256,640]{1,0:T(8,128)(2,1)S(1)}, u32[]{:S(2)}, u32[]{:S(2)}) collective-permute-start(bf16[256,640]{1,0:T(8,128)(2,1)S(1)} %collective-permute-done.14.refs_0_), channel_id=1, source_target_pairs={{4,0},{3,1},{6,2},{1,3},{0,4},{7,5},{2,6},{5,7},{12,8},{11,9},{14,... | collective-permute-start | bytes 983048 | tf_op jit(solution)/shard_map/ppermute | solution.py:81
  41.5 4.6 %collective-permute-done.9 = bf16[64,640]{1,0:T(8,128)(2,1)S(1)} collective-permute-done((bf16[64,640]{1,0:T(8,128)(2,1)S(1)}, bf16[64,640]{1,0:T(8,128)(2,1)S(1)}, u32[]{:S(2)}, u32[]{:S(2)}) %collective-permute-start.9) | collective-permute-done | bytes 81952 | tf_op jit(solution)/shard_map/ppermute | solution.py:61
  46.2 1.6 %collective-permute-start.13 = (bf16[192,640]{1,0:T(8,128)(2,1)S(1)}, bf16[192,640]{1,0:T(8,128)(2,1)S(1)}, u32[]{:S(2)}, u32[]{:S(2)}) collective-permute-start(bf16[192,640]{1,0:T(8,128)(2,1)S(1)} %constant_dynamic-update-slice_fusion.2.refs_0_), channel_id=1, source_target_pairs={{6,0},{4,2},{2,4},{0,6},{7,1},{5,3},{3,5},{1,7},{14,8},{12,10},{10... | collective-permute-start | bytes 737288 | tf_op jit(solution)/shard_map/ppermute | solution.py:61
  47.8 1.3 %collective-permute-start.12 = (bf16[192,640]{1,0:T(8,128)(2,1)S(1)}, bf16[192,640]{1,0:T(8,128)(2,1)S(1)}, u32[]{:S(2)}, u32[]{:S(2)}) collective-permute-start(bf16[192,640]{1,0:T(8,128)(2,1)S(1)} %constant_dynamic-update-slice_fusion.2.refs_0_), channel_id=1, source_target_pairs={{4,0},{6,2},{0,4},{2,6},{5,1},{7,3},{1,5},{3,7},{12,8},{14,10},{8,... | collective-permute-start | bytes 737288 | tf_op jit(solution)/shard_map/ppermute | solution.py:61
  49.7 5.3 %collective-permute-done.16.refs_2_ = bf16[256,640]{1,0:T(8,128)(2,1)S(1)} collective-permute-done((bf16[256,640]{1,0:T(8,128)(2,1)S(1)}, bf16[256,640]{1,0:T(8,128)(2,1)S(1)}, u32[]{:S(2)}, u32[]{:S(2)}) %collective-permute-start.16) | collective-permute-done | bytes 327712 | tf_op jit(solution)/shard_map/ppermute | solution.py:81
  55.1 7.1 %attend_plane.1 = (bf16[640,512]{1,0:T(8,128)(2,1)S(1)}, f32[10,8,512]{2,1,0:T(8,128)S(1)}) custom-call(s32[24]{0:T(128)S(1)} %pad_add_fusion.table_ref, bf16[640,512]{1,0:T(8,128)(2,1)S(1)} %get-tuple-element.38.q_ref, bf16[256,640]{1,0:T(8,128)(2,1)S(1)} %collective-permute-done.14.refs_0_, bf16[256,640]{1,0:T(8,128)(2,1)S(1)} %collective-permute-done.15.refs_1_, ...), custom_call_target="tpu_custom_call" | custom-call | flops 5284823040 | bytes 2293760 | tf_op jit(solution)/shard_map/attend_plane/pallas_call | solution.py:367
  62.2 7.6 %attend_anchors.1 = (bf16[640,256]{1,0:T(8,128)(2,1)S(1)}, f32[16,256]{1,0:T(8,128)S(1)}, bf16[688,256]{1,0:T(8,128)(2,1)S(1)}) custom-call(s32[24]{0:T(128)S(1)} %pad_add_fusion.table_ref, bf16[640,512]{1,0:T(8,128)(2,1)S(1)} %get-tuple-element.38.q_ref, bf16[192,640]{1,0:T(8,128)(2,1)S(1)} %constant_dynamic-update-slice_fusion.2.refs_0_, ...), custom_call_target="tpu_custom_call" | custom-call | flops 5284823040 | bytes 2293760 | tf_op jit(solution)/shard_map/attend_anchors/pallas_call | solution.py:444
  69.9 1.7 %collective-permute-done.17.refs_0_ = bf16[688,256]{1,0:T(8,128)(2,1)S(1)} collective-permute-done((bf16[688,256]{1,0:T(8,128)(2,1)S(1)}, bf16[688,256]{1,0:T(8,128)(2,1)S(1)}, u32[]{:S(2)}, u32[]{:S(2)}) %collective-permute-start.17) | collective-permute-done | bytes 352288 | tf_op jit(solution)/shard_map/ppermute | solution.py:66
  71.5 1.3 %finish.1 = bf16[256,640]{1,0:T(8,128)(2,1)} custom-call(bf16[640,256]{1,0:T(8,128)(2,1)S(1)} %get-tuple-element.47.own_ref, f32[16,256]{1,0:T(8,128)S(1)} %get-tuple-element.48.level_ref, bf16[688,256]{1,0:T(8,128)(2,1)S(1)} %collective-permute-done.17.refs_0_, bf16[640,640]{1,0:T(8,128)(2,1)S(1)} %copy-done), custom_call_target="tpu_custom_call" | custom-call | flops 209715200 | bytes 1802240 | tf_op jit(solution)/shard_map/finish/pallas_call | solution.py:494
  (51 shorter events, 5.1 us)
Async XLA Ops:
  1.7 1.4 %collective-permute-start = (bf16[8,640]{1,0:T(8,128)(2,1)S(1)}, bf16[8,640]{1,0:T(8,128)(2,1)S(1)}, u32[]{:S(2)}, u32[]{:S(2)}) collective-permute-start(bf16[8,640]{1,0:T(8,128)(2,1)S(1)} %broadcast_select_fusion.5), channel_id=1, source_target_pairs={{1,0},{0,1},{3,2},{2,3},{5,4},{4,5},{7,6},{6,7},{9,8},{8,9},{11,10... | collective-permute-start | bytes 30728 | tf_op jit(solution)/shard_map/ppermute | solution.py:66
  3.1 9.5 %collective-permute-start.2 = (bf16[34,640]{1,0:T(8,128)(2,1)S(1)}, bf16[34,640]{1,0:T(8,128)(2,1)S(1)}, u32[]{:S(2)}, u32[]{:S(2)}) collective-permute-start(bf16[34,640]{1,0:T(8,128)(2,1)S(1)} %get-tuple-element.52), channel_id=1, source_target_pairs={{2,4},{4,2},{3,5},{5,3},{10,12},{12,10},{11,13},{13,11},{18,20},{2... | collective-permute-start | bytes 130568 | tf_op jit(solution)/shard_map/ppermute | solution.py:131
  3.8 8.9 %copy-start.2 = (bf16[1,8,32,640]{3,2,1,0:T(8,128)(2,1)S(1)}, bf16[1,8,32,640]{3,2,1,0:T(8,128)(2,1)}, u32[]{:S(2)}) copy-start(bf16[1,8,32,640]{3,2,1,0:T(8,128)(2,1)} %param.9) | copy-start | bytes 983044
  3.8 8.8 %collective-permute-start.1 = (bf16[34,640]{1,0:T(8,128)(2,1)S(1)}, bf16[34,640]{1,0:T(8,128)(2,1)S(1)}, u32[]{:S(2)}, u32[]{:S(2)}) collective-permute-start(bf16[34,640]{1,0:T(8,128)(2,1)S(1)} %get-tuple-element.53), channel_id=1, source_target_pairs={{0,2},{4,6},{2,0},{6,4},{1,3},{5,7},{3,1},{7,5},{8,10},{12,14},{10... | collective-permute-start | bytes 130568 | tf_op jit(solution)/shard_map/ppermute | solution.py:131
  12.6 6.4 %copy-start.7 = (s32[4]{0:T(128)S(1)}, s32[4]{0:T(128)}, u32[]{:S(2)}) copy-start(s32[4]{0:T(128)} %param.17) | copy-start | bytes 52
  12.6 20.6 %copy-start.3 = (bf16[640,640]{1,0:T(8,128)(2,1)S(1)}, bf16[640,640]{1,0:T(8,128)(2,1)}, u32[]{:S(2)}) copy-start(bf16[640,640]{1,0:T(8,128)(2,1)} %refs_5_.1) | copy-start | bytes 2457604
  12.6 20.6 %copy-start.4 = (bf16[640,640]{1,0:T(8,128)(2,1)S(1)}, bf16[640,640]{1,0:T(8,128)(2,1)}, u32[]{:S(2)}) copy-start(bf16[640,640]{1,0:T(8,128)(2,1)} %refs_8_.1) | copy-start | bytes 2457604
  12.6 20.6 %copy-start.5 = (bf16[640,640]{1,0:T(8,128)(2,1)S(1)}, bf16[640,640]{1,0:T(8,128)(2,1)}, u32[]{:S(2)}) copy-start(bf16[640,640]{1,0:T(8,128)(2,1)} %refs_9_.1) | copy-start | bytes 2457604
  16.6 1.4 %collective-permute-start.4 = (bf16[128,640]{1,0:T(8,128)(2,1)S(1)}, bf16[128,640]{1,0:T(8,128)(2,1)S(1)}, u32[]{:S(2)}, u32[]{:S(2)}) collective-permute-start(bf16[128,640]{1,0:T(8,128)(2,1)S(1)} %get-tuple-element.37.refs_1_), channel_id=1, source_target_pairs={{1,0},{0,1},{3,2},{2,3},{5,4},{4,5},{7,6},{6,7},{9,8},{8,9},{11,10... | collective-permute-start | bytes 491528 | tf_op jit(solution)/shard_map/ppermute | solution.py:66
  16.7 16.5 %collective-permute-start.3 = (bf16[128,640]{1,0:T(8,128)(2,1)S(1)}, bf16[128,640]{1,0:T(8,128)(2,1)S(1)}, u32[]{:S(2)}, u32[]{:S(2)}) collective-permute-start(bf16[128,640]{1,0:T(8,128)(2,1)S(1)} %get-tuple-element.36.refs_0_), channel_id=1, source_target_pairs={{1,0},{0,1},{3,2},{2,3},{5,4},{4,5},{7,6},{6,7},{9,8},{8,9},{11,10... | collective-permute-start | bytes 491528 | tf_op jit(solution)/shard_map/ppermute | solution.py:66
  18.0 22.1 %collective-permute-start.14 = (bf16[256,640]{1,0:T(8,128)(2,1)S(1)}, bf16[256,640]{1,0:T(8,128)(2,1)S(1)}, u32[]{:S(2)}, u32[]{:S(2)}) collective-permute-start(bf16[256,640]{1,0:T(8,128)(2,1)S(1)} %constant_dynamic-update-slice_fusion.refs_4_.key_ref), channel_id=1, source_target_pairs={{2,0},{5,1},{0,2},{7,3},{6,4},{1,5},{4,6},{3,7},{10,8},{13,9},{8,1... | collective-permute-start | bytes 983048 | tf_op jit(solution)/shard_map/ppermute | solution.py:81
  19.7 9.3 %collective-permute-start.5 = (bf16[64,640]{1,0:T(8,128)(2,1)S(1)}, bf16[64,640]{1,0:T(8,128)(2,1)S(1)}, u32[]{:S(2)}, u32[]{:S(2)}) collective-permute-start(bf16[64,640]{1,0:T(8,128)(2,1)S(1)} %get-tuple-element.40), channel_id=1, source_target_pairs={{2,0},{0,2},{6,4},{4,6},{3,1},{1,3},{7,5},{5,7},{10,8},{8,10},{14,... | collective-permute-start | bytes 245768 | tf_op jit(solution)/shard_map/ppermute | solution.py:61
  20.9 8.7 %collective-permute-start.6 = (bf16[64,640]{1,0:T(8,128)(2,1)S(1)}, bf16[64,640]{1,0:T(8,128)(2,1)S(1)}, u32[]{:S(2)}, u32[]{:S(2)}) collective-permute-start(bf16[64,640]{1,0:T(8,128)(2,1)S(1)} %get-tuple-element.41), channel_id=1, source_target_pairs={{4,0},{6,2},{0,4},{2,6},{5,1},{7,3},{1,5},{3,7},{12,8},{14,10},{8,... | collective-permute-start | bytes 245768 | tf_op jit(solution)/shard_map/ppermute | solution.py:61
  21.8 9.0 %collective-permute-start.7 = (bf16[64,640]{1,0:T(8,128)(2,1)S(1)}, bf16[64,640]{1,0:T(8,128)(2,1)S(1)}, u32[]{:S(2)}, u32[]{:S(2)}) collective-permute-start(bf16[64,640]{1,0:T(8,128)(2,1)S(1)} %get-tuple-element.42), channel_id=1, source_target_pairs={{6,0},{4,2},{2,4},{0,6},{7,1},{5,3},{3,5},{1,7},{14,8},{12,10},{10... | collective-permute-start | bytes 245768 | tf_op jit(solution)/shard_map/ppermute | solution.py:61
  28.9 20.8 %collective-permute-start.15 = (bf16[256,640]{1,0:T(8,128)(2,1)S(1)}, bf16[256,640]{1,0:T(8,128)(2,1)S(1)}, u32[]{:S(2)}, u32[]{:S(2)}) collective-permute-start(bf16[256,640]{1,0:T(8,128)(2,1)S(1)} %constant_dynamic-update-slice_fusion.refs_4_.key_ref), channel_id=1, source_target_pairs={{4,0},{3,1},{6,2},{1,3},{0,4},{7,5},{2,6},{5,7},{12,8},{11,9},{14,... | collective-permute-start | bytes 983048 | tf_op jit(solution)/shard_map/ppermute | solution.py:81
  31.5 10.0 %collective-permute-start.8 = (bf16[64,640]{1,0:T(8,128)(2,1)S(1)}, bf16[64,640]{1,0:T(8,128)(2,1)S(1)}, u32[]{:S(2)}, u32[]{:S(2)}) collective-permute-start(bf16[64,640]{1,0:T(8,128)(2,1)S(1)} %accept.1), channel_id=1, source_target_pairs={{8,0},{0,8},{24,16},{16,24},{9,1},{1,9},{25,17},{17,25},{10,2},{2,... | collective-permute-start | bytes 245768 | tf_op jit(solution)/shard_map/ppermute | solution.py:61
  37.4 8.8 %collective-permute-start.10 = (bf16[64,640]{1,0:T(8,128)(2,1)S(1)}, bf16[64,640]{1,0:T(8,128)(2,1)S(1)}, u32[]{:S(2)}, u32[]{:S(2)}) collective-permute-start(bf16[64,640]{1,0:T(8,128)(2,1)S(1)} %accept.1), channel_id=1, source_target_pairs={{24,0},{16,8},{8,16},{0,24},{25,1},{17,9},{9,17},{1,25},{26,2},{18... | collective-permute-start | bytes 245768 | tf_op jit(solution)/shard_map/ppermute | solution.py:61
  39.9 6.2 %collective-permute-start.9 = (bf16[64,640]{1,0:T(8,128)(2,1)S(1)}, bf16[64,640]{1,0:T(8,128)(2,1)S(1)}, u32[]{:S(2)}, u32[]{:S(2)}) collective-permute-start(bf16[64,640]{1,0:T(8,128)(2,1)S(1)} %accept.1), channel_id=1, source_target_pairs={{16,0},{24,8},{0,16},{8,24},{17,1},{25,9},{1,17},{9,25},{18,2},{26... | collective-permute-start | bytes 245768 | tf_op jit(solution)/shard_map/ppermute | solution.py:61
  40.1 15.0 %collective-permute-start.16 = (bf16[256,640]{1,0:T(8,128)(2,1)S(1)}, bf16[256,640]{1,0:T(8,128)(2,1)S(1)}, u32[]{:S(2)}, u32[]{:S(2)}) collective-permute-start(bf16[256,640]{1,0:T(8,128)(2,1)S(1)} %collective-permute-done.14.refs_0_), channel_id=1, source_target_pairs={{4,0},{3,1},{6,2},{1,3},{0,4},{7,5},{2,6},{5,7},{12,8},{11,9},{14,... | collective-permute-start | bytes 983048 | tf_op jit(solution)/shard_map/ppermute | solution.py:81
  46.2 16.0 %collective-permute-start.13 = (bf16[192,640]{1,0:T(8,128)(2,1)S(1)}, bf16[192,640]{1,0:T(8,128)(2,1)S(1)}, u32[]{:S(2)}, u32[]{:S(2)}) collective-permute-start(bf16[192,640]{1,0:T(8,128)(2,1)S(1)} %constant_dynamic-update-slice_fusion.2.refs_0_), channel_id=1, source_target_pairs={{6,0},{4,2},{2,4},{0,6},{7,1},{5,3},{3,5},{1,7},{14,8},{12,10},{10... | collective-permute-start | bytes 737288 | tf_op jit(solution)/shard_map/ppermute | solution.py:61
  47.8 14.4 %collective-permute-start.12 = (bf16[192,640]{1,0:T(8,128)(2,1)S(1)}, bf16[192,640]{1,0:T(8,128)(2,1)S(1)}, u32[]{:S(2)}, u32[]{:S(2)}) collective-permute-start(bf16[192,640]{1,0:T(8,128)(2,1)S(1)} %constant_dynamic-update-slice_fusion.2.refs_0_), channel_id=1, source_target_pairs={{4,0},{6,2},{0,4},{2,6},{5,1},{7,3},{1,5},{3,7},{12,8},{14,10},{8,... | collective-permute-start | bytes 737288 | tf_op jit(solution)/shard_map/ppermute | solution.py:61
  49.0 13.1 %collective-permute-start.11 = (bf16[192,640]{1,0:T(8,128)(2,1)S(1)}, bf16[192,640]{1,0:T(8,128)(2,1)S(1)}, u32[]{:S(2)}, u32[]{:S(2)}) collective-permute-start(bf16[192,640]{1,0:T(8,128)(2,1)S(1)} %constant_dynamic-update-slice_fusion.2.refs_0_), channel_id=1, source_target_pairs={{2,0},{0,2},{6,4},{4,6},{3,1},{1,3},{7,5},{5,7},{10,8},{8,10},{14,... | collective-permute-start | bytes 737288 | tf_op jit(solution)/shard_map/ppermute | solution.py:61
  62.2 9.4 %copy-start = (bf16[640,640]{1,0:T(8,128)(2,1)S(1)}, bf16[640,640]{1,0:T(8,128)(2,1)}, u32[]{:S(2)}) copy-start(bf16[640,640]{1,0:T(8,128)(2,1)} %refs_1_.1) | copy-start | bytes 2457604
  69.8 1.7 %collective-permute-start.17 = (bf16[688,256]{1,0:T(8,128)(2,1)S(1)}, bf16[688,256]{1,0:T(8,128)(2,1)S(1)}, u32[]{:S(2)}, u32[]{:S(2)}) collective-permute-start(bf16[688,256]{1,0:T(8,128)(2,1)S(1)} %get-tuple-element.49), channel_id=1, source_target_pairs={{1,0},{0,1},{3,2},{2,3},{5,4},{4,5},{7,6},{6,7},{9,8},{8,9},{11,10... | collective-permute-start | bytes 1056776 | tf_op jit(solution)/shard_map/ppermute | solution.py:66
  (3 other events, 11.5 us)

commit v4 on v3

--- a/solution.py
+++ b/solution.py
@@ -110,51 +110,60 @@
 
 
 def halo(cells):
+    core, cores = lax.axis_index("pcol"), lax.axis_size("pcol")
+    prow, rows = lax.axis_index("prow"), lax.axis_size("prow")
+    cells, left_core, right_core, upper, odd, second, third = lax.optimization_barrier((
+        cells, core == 0, core == 1, prow < 2, lax.rem(prow, 2) == 1, prow == 1, prow == 2
+    ))
     first, last, top, bottom = edges(cells)
-    core, cores = lax.axis_index("pcol"), lax.axis_size("pcol")
-    rows = lax.axis_size("prow")
     if cores == 2:
-        other = shifted(jnp.where(core == 0, last, first), "pcol", 1)
+        other = shifted(jnp.where(left_core, last, first), "pcol", 1)
         zero = jnp.zeros_like(other)
-        left = jnp.where(core == 1, other, zero)
-        right = jnp.where(core == 0, other, zero)
+        left = jnp.where(right_core, other, zero)
+        right = jnp.where(left_core, other, zero)
     else:
         left = lax.ppermute(last, "pcol", [(i, i + 1) for i in range(cores - 1)])
         right = lax.ppermute(first, "pcol", [(i + 1, i) for i in range(cores - 1)])
     low = jnp.concatenate([bottom, left[-1:], right[-1:]], axis=0)
     high = jnp.concatenate([top, left[:1], right[:1]], axis=0)
-    odd = lax.rem(lax.axis_index("prow"), 2) == 1
-    swaps = []
-    for first in range(2):
-        pairs = [(i, i + 1) for i in range(first, rows - 1, 2)]
-        block = jnp.where(odd, high, low) if first == 0 else jnp.where(odd, low, high)
-        swaps.append(lax.ppermute(block, "prow", pairs + [(j, i) for i, j in pairs]))
-    above = jnp.where(odd, swaps[0], swaps[1])
-    below = jnp.where(odd, swaps[1], swaps[0])
+    if rows != 4:
+        above = lax.ppermute(low, "prow", [(i, i + 1) for i in range(rows - 1)])
+        below = lax.ppermute(high, "prow", [(i + 1, i) for i in range(rows - 1)])
+        return left, right, above, below
+    near = exchange(jnp.concatenate([low, high], axis=0), "prow", 1)
+    low, high = near[:len(low)], near[len(low):]
+    far = exchange(jnp.where(upper, low, high), "prow", 2)
+    zero = jnp.zeros_like(far)
+    above = jnp.where(odd, low, jnp.where(third, far, zero))
+    below = jnp.where(odd, jnp.where(second, far, zero), high)
     return left, right, above, below
 
 
-def stage_kernel(in_ref, out_ref, sem):
-    copy = pltpu.make_async_copy(in_ref, out_ref, sem)
+def stage_kernel(row, in_ref, out_ref, sem):
+    copy = pltpu.make_async_copy(in_ref.at[row], out_ref, sem)
     copy.start()
     copy.wait()
 
 
-def stage(array):
-    return pl.pallas_call(
-        stage_kernel,
-        out_shape=shape(*array.shape),
+def stage(weights, row):
+    taps = weights[row]
+    return pl.pallas_call(
+        functools.partial(stage_kernel, row),
+        out_shape=shape(*taps.shape),
         in_specs=[ANY],
         out_specs=VMEM,
         scratch_shapes=[pltpu.SemaphoreType.DMA],
         compiler_params=grant(STAGE_MIB),
-        cost_estimate=cost(0, 2 * array.nbytes),
+        cost_estimate=cost(0, 2 * taps.nbytes),
         name="stage",
-    )(array)
-
-
-def conv_kernel(rows, cols, cores, x_ref, left_ref, right_ref, above_ref, below_ref, w_ref, *refs):
-    features_ref, *half_refs, shift0, shift1, shift2 = refs
+    )(weights)
+
+
+def conv_kernel(rows, cols, cores, x_ref, left_ref, right_ref, above_ref, below_ref, *refs):
+    taps, anchoring, refs = refs[:3], refs[3:6], refs[6:]
+    table_ref, features_ref, *half_refs, shift0, shift1, shift2 = refs
+
+    Table.fill(table_ref, *anchoring)
 
     def silu(v):
         v = v.astype(F32)
@@ -177,7 +186,7 @@
     for a in range(3):
         for b, shift in enumerate((shift0, shift1, shift2)):
             total = total + jnp.dot(
-                shift[a * cols:(a + rows) * cols], w_ref[a, b], preferred_element_type=F32
+                shift[a * cols:(a + rows) * cols], taps[a][b], preferred_element_type=F32
             )
     features = total.astype(BF16)
     features_ref[...] = features
@@ -196,19 +205,21 @@
                     ref[b * per:(b + 1) * per] = rows_of
 
 
-def conv_norm(cells, sides, conv_weight, cores):
+def conv_norm(cells, sides, taps, anchoring, cores):
     rows, cols, channels = cells.shape
     tokens = rows * cols
     return pl.pallas_call(
         functools.partial(conv_kernel, rows, cols, cores),
-        out_shape=(shape(tokens, channels),) + (shape(tokens // cores, channels),) * cores,
-        in_specs=[VMEM] * 6,
-        out_specs=(VMEM,) * (1 + cores),
+        out_shape=(
+            shape(anchoring[0].shape[0] * (2 + NSEL), dtype=jnp.int32), shape(tokens, channels),
+        ) + (shape(tokens // cores, channels),) * cores,
+        in_specs=[VMEM] * 8 + [SMEM] * 3,
+        out_specs=(SMEM,) + (VMEM,) * (1 + cores),
         scratch_shapes=[pltpu.VMEM(((rows + 2) * cols, channels), BF16)] * 3,
         compiler_params=grant(24),
         cost_estimate=cost(18 * tokens * channels**2, 18 * channels**2, tokens * channels),
         name="conv_norm",
-    )(cells.reshape(tokens, channels), *sides, conv_weight)
+    )(cells.reshape(tokens, channels), *sides, *taps, *anchoring)
 
 
 class Table:
@@ -217,8 +228,13 @@
         self.every_image = anchors == images
 
     @staticmethod
-    def build(anchor_index, block_count, order):
-        return jnp.concatenate([anchor_index, block_count, order.reshape(-1)])
+    def fill(ref, index_ref, count_ref, order_ref):
+        anchors = index_ref.shape[0]
+        for a in range(anchors):
+            ref[a] = index_ref[a]
+            ref[anchors + a] = count_ref[a]
+            for slot in range(NSEL):
+                ref[2 * anchors + a * NSEL + slot] = order_ref[a, slot]
 
     def anchor_at(self, image):
         found = jnp.int32(0)
@@ -584,10 +600,10 @@
     anchors = anchor_index.shape[0]
     per_patch = tile_rows * tile_cols // BLOCK
     info = (anchors, images, cores, prows, per_patch)
-    features, *parts = conv_norm(latent[0], halo(latent[0]), stage(conv_weight), cores)
-    parts, *anchoring = lax.optimization_barrier((parts, anchor_index, block_count, block_order))
-    anchor_index, block_count, block_order = anchoring
-    table = Table.build(anchor_index, block_count, block_order[:, :NSEL])
+    taps = [stage(conv_weight, row) for row in range(3)]
+    table, features, *parts = conv_norm(
+        latent[0], halo(latent[0]), taps, (anchor_index, block_count, block_order), cores
+    )
     keys, queries = [parts[0]], list(parts)
     for s in range(1, cores):
         theirs = [None] * cores

time: 73 us -> 77.3 us (1.059)
  Pallas kernels: 28.6 us -> 31.2 us
  waiting for transfers between devices: 20.1 us -> 21.5 us
    ppermute x2 -> x0, starting transfers between devices: 6.28 us -> none  [halo(): lax.ppermute(block, 'prow', pairs + [(j, i) for i, j in pairs])]
    ppermute x9 -> x11, starting transfers between devices: 11.5 us -> 16.7 us  [exchange(): lax.ppermute(block, axis, [(source_of(i, step, count), i) for i in range(...]
    pallas_call x1 -> x3, Pallas kernels: 3.1 us -> 5.15 us  [stage(): pl.pallas_call(functools.partial(stage_kernel, row), out_shape=shape(*tap...]
    ppermute x9 -> x11, waiting for transfers between devices: 11.5 us -> 13 us  [exchange(): lax.ppermute(block, axis, [(source_of(i, step, count), i) for i in range(...]
    ppermute x3, starting transfers between devices: 3 us -> 3.99 us  [hop(): lax.ppermute(rows, ('prow', 'pcol'), [((p ^ (entry if c % 2 == 0 else 3 -...]
  transfers between devices with their start and end apart: 18 -> 18, of which waited for: 7 -> 8; matrix products, arithmetic and copies ran while one was open for 0% -> 0% of each run, Pallas kernels for 22% -> 23%
where the time goes in v4:
time: 77.3 us; the launch traced here: 77.1 us
  Pallas kernels  31.2 us (40%)
  starting transfers between devices  21.9 us (28%)
  waiting for transfers between devices  21.5 us (28%)
  local copies, waits for them, and re-layouts  1.43 us (2%)
  between operations  0.94 us (1%)
    ppermute x11, starting transfers between devices, exchange(): lax.ppermute(block, axis, [(source_of(i, step, count), i) for i in range(...  16.7 us
    ppermute x11, waiting for transfers between devices, exchange(): lax.ppermute(block, axis, [(source_of(i, step, count), i) for i in range(...  13 us
    pallas_call x1, Pallas kernels, attend_anchors(): pl.pallas_call(functools.partial(anchor_kernel, info, len(keys), len(earl...  7.59 us
    pallas_call x1, Pallas kernels, attend_plane(): pl.pallas_call(functools.partial(plane_kernel, info, len(keys)), out_shap...  7.02 us
    ppermute x3, waiting for transfers between devices, hop(): lax.ppermute(rows, ('prow', 'pcol'), [((p ^ (entry if c % 2 == 0 else 3 -...  5.19 us
    pallas_call x3, Pallas kernels, stage(): pl.pallas_call(functools.partial(stage_kernel, row), out_shape=shape(*tap...  5.15 us
    pallas_call x1, Pallas kernels, conv_norm(): pl.pallas_call(functools.partial(conv_kernel, rows, cols, cores), out_sha...  4.52 us
    pallas_call x1, Pallas kernels, attend_own(): pl.pallas_call(functools.partial(own_kernel, info, len(parts)), out_shape...  4.21 us
  transfers between devices with their start and end apart: 18, of which 8 were waited for; matrix products, arithmetic and copies ran while one was open for 0% of the time, Pallas kernels for 23%

profile of v4, /device:TPU:0, one launch (start us, length us, event | category | flops | bytes accessed | tf_op | source)
XLA Modules:
  0.0 77.1 jit_solution(13492381514990222848)
XLA Ops:
  0.7 1.0 %copy-done.1 = bf16[1,8,32,640]{3,2,1,0:T(8,128)(2,1)S(1)} copy-done((bf16[1,8,32,640]{3,2,1,0:T(8,128)(2,1)S(1)}, bf16[1,8,32,640]{3,2,1,0:T(8,128)(2,1)}, u32[]{:S(2)}) %copy-start.1) | copy-done | bytes 327704
  2.2 0.8 %collective-permute-done = bf16[8,640]{1,0:T(8,128)(2,1)S(1)} collective-permute-done((bf16[8,640]{1,0:T(8,128)(2,1)S(1)}, bf16[8,640]{1,0:T(8,128)(2,1)S(1)}, u32[]{:S(2)}, u32[]{:S(2)}) %collective-permute-start) | collective-permute-done | bytes 10272 | tf_op jit(solution)/shard_map/ppermute | solution.py:66
  3.4 2.9 %collective-permute-start.1 = (bf16[68,640]{1,0:T(8,128)(2,1)S(1)}, bf16[68,640]{1,0:T(8,128)(2,1)S(1)}, u32[]{:S(2)}, u32[]{:S(2)}) collective-permute-start(bf16[68,640]{1,0:T(8,128)(2,1)S(1)} %concatenate.9), channel_id=1, source_target_pairs={{2,0},{0,2},{6,4},{4,6},{3,1},{1,3},{7,5},{5,7},{10,8},{8,10},{14,... | collective-permute-start | bytes 261128 | tf_op jit(solution)/shard_map/ppermute | solution.py:61
  6.3 3.0 %collective-permute-done.1 = bf16[68,640]{1,0:T(8,128)(2,1)S(1)} collective-permute-done((bf16[68,640]{1,0:T(8,128)(2,1)S(1)}, bf16[68,640]{1,0:T(8,128)(2,1)S(1)}, u32[]{:S(2)}, u32[]{:S(2)}) %collective-permute-start.1) | collective-permute-done | bytes 87072 | tf_op jit(solution)/shard_map/ppermute | solution.py:61
  9.3 1.8 %collective-permute-start.2 = (bf16[34,640]{1,0:T(8,128)(2,1)S(1)}, bf16[34,640]{1,0:T(8,128)(2,1)S(1)}, u32[]{:S(2)}, u32[]{:S(2)}) collective-permute-start(bf16[34,640]{1,0:T(8,128)(2,1)S(1)} %broadcast_select_fusion), channel_id=1, source_target_pairs={{4,0},{6,2},{0,4},{2,6},{5,1},{7,3},{1,5},{3,7},{12,8},{14,10},{8,... | collective-permute-start | bytes 130568 | tf_op jit(solution)/shard_map/ppermute | solution.py:61
  11.2 1.7 %stage.3.refs_0_ = bf16[3,640,640]{2,1,0:T(8,128)(2,1)S(1)} custom-call(bf16[3,3,640,640]{3,2,1,0:T(8,128)(2,1)} %in_ref.5), custom_call_target="tpu_custom_call" | custom-call | bytes 4915200 | tf_op jit(solution)/shard_map/stage/pallas_call | solution.py:150
  12.9 1.7 %stage.5.refs_2_ = bf16[3,640,640]{2,1,0:T(8,128)(2,1)S(1)} custom-call(bf16[3,3,640,640]{3,2,1,0:T(8,128)(2,1)} %in_ref.5), custom_call_target="tpu_custom_call" | custom-call | bytes 4915200 | tf_op jit(solution)/shard_map/stage/pallas_call | solution.py:150
  14.6 1.7 %stage.4.refs_1_ = bf16[3,640,640]{2,1,0:T(8,128)(2,1)S(1)} custom-call(bf16[3,3,640,640]{3,2,1,0:T(8,128)(2,1)} %in_ref.5), custom_call_target="tpu_custom_call" | custom-call | bytes 4915200 | tf_op jit(solution)/shard_map/stage/pallas_call | solution.py:150
  16.5 4.5 %conv_norm.1 = (s32[24]{0:T(128)S(1)}, bf16[256,640]{1,0:T(8,128)(2,1)}, bf16[128,640]{1,0:T(8,128)(2,1)S(1)}, bf16[128,640]{1,0:T(8,128)(2,1)S(1)}) custom-call(bf16[256,640]{1,0:T(8,128)(2,1)S(1)} %bitcast.5, bf16[8,640]{1,0:T(8,128)(2,1)S(1)} %get-tuple-element.63.left_ref, bf16[8,640]{1,0:T(8,128)(2,1)S(1)} %get-tuple-element.62.right_ref, ...), custom_call_target="tpu_custom_call" | custom-call | flops 1887436800 | bytes 7372800 | tf_op jit(solution)/shard_map/conv_norm/pallas_call | solution.py:211
  21.6 0.9 %collective-permute-done.4.refs_3_ = bf16[128,640]{1,0:T(8,128)(2,1)S(1)} collective-permute-done((bf16[128,640]{1,0:T(8,128)(2,1)S(1)}, bf16[128,640]{1,0:T(8,128)(2,1)S(1)}, u32[]{:S(2)}, u32[]{:S(2)}) %collective-permute-start.4) | collective-permute-done | bytes 163872 | tf_op jit(solution)/shard_map/ppermute | solution.py:66
  22.5 1.6 %collective-permute-start.14 = (bf16[256,640]{1,0:T(8,128)(2,1)S(1)}, bf16[256,640]{1,0:T(8,128)(2,1)S(1)}, u32[]{:S(2)}, u32[]{:S(2)}) collective-permute-start(bf16[256,640]{1,0:T(8,128)(2,1)S(1)} %constant_dynamic-update-slice_fusion.refs_4_.key_ref), channel_id=1, source_target_pairs={{2,0},{5,1},{0,2},{7,3},{6,4},{1,5},{4,6},{3,7},{10,8},{13,9},{8,1... | collective-permute-start | bytes 983048 | tf_op jit(solution)/shard_map/ppermute | solution.py:81
  25.5 2.7 %collective-permute-start.7 = (bf16[64,640]{1,0:T(8,128)(2,1)S(1)}, bf16[64,640]{1,0:T(8,128)(2,1)S(1)}, u32[]{:S(2)}, u32[]{:S(2)}) collective-permute-start(bf16[64,640]{1,0:T(8,128)(2,1)S(1)} %get-tuple-element.48), channel_id=1, source_target_pairs={{6,0},{4,2},{2,4},{0,6},{7,1},{5,3},{3,5},{1,7},{14,8},{12,10},{10... | collective-permute-start | bytes 245768 | tf_op jit(solution)/shard_map/ppermute | solution.py:61
  28.2 5.6 %collective-permute-done.5.refs_1_ = bf16[64,640]{1,0:T(8,128)(2,1)S(1)} collective-permute-done((bf16[64,640]{1,0:T(8,128)(2,1)S(1)}, bf16[64,640]{1,0:T(8,128)(2,1)S(1)}, u32[]{:S(2)}, u32[]{:S(2)}) %collective-permute-start.5) | collective-permute-done | bytes 81952 | tf_op jit(solution)/shard_map/ppermute | solution.py:61
  35.4 1.6 %collective-permute-start.8 = (bf16[64,640]{1,0:T(8,128)(2,1)S(1)}, bf16[64,640]{1,0:T(8,128)(2,1)S(1)}, u32[]{:S(2)}, u32[]{:S(2)}) collective-permute-start(bf16[64,640]{1,0:T(8,128)(2,1)S(1)} %accept.1), channel_id=1, source_target_pairs={{8,0},{0,8},{24,16},{16,24},{9,1},{1,9},{25,17},{17,25},{10,2},{2,... | collective-permute-start | bytes 245768 | tf_op jit(solution)/shard_map/ppermute | solution.py:61
  37.1 4.2 %attend_own.1 = (bf16[640,512]{1,0:T(8,128)(2,1)S(1)}, bf16[640,512]{1,0:T(8,128)(2,1)S(1)}, f32[10,8,512]{2,1,0:T(8,128)S(1)}) custom-call(s32[24]{0:T(128)S(1)} %get-tuple-element.41.table_ref, bf16[128,640]{1,0:T(8,128)(2,1)S(1)} %get-tuple-element.42.refs_0_, bf16[128,640]{1,0:T(8,128)(2,1)S(1)} %get-tuple-element.43.refs_1_, ...), custom_call_target="tpu_custom_call" | custom-call | flops 2181038080 | bytes 1638400 | tf_op jit(solution)/shard_map/attend_own/pallas_call | solution.py:351
  41.3 2.5 %collective-permute-start.10 = (bf16[64,640]{1,0:T(8,128)(2,1)S(1)}, bf16[64,640]{1,0:T(8,128)(2,1)S(1)}, u32[]{:S(2)}, u32[]{:S(2)}) collective-permute-start(bf16[64,640]{1,0:T(8,128)(2,1)S(1)} %accept.1), channel_id=1, source_target_pairs={{24,0},{16,8},{8,16},{0,24},{25,1},{17,9},{9,17},{1,25},{26,2},{18... | collective-permute-start | bytes 245768 | tf_op jit(solution)/shard_map/ppermute | solution.py:61
  44.1 2.4 %collective-permute-start.16 = (bf16[256,640]{1,0:T(8,128)(2,1)S(1)}, bf16[256,640]{1,0:T(8,128)(2,1)S(1)}, u32[]{:S(2)}, u32[]{:S(2)}) collective-permute-start(bf16[256,640]{1,0:T(8,128)(2,1)S(1)} %collective-permute-done.14.refs_0_), channel_id=1, source_target_pairs={{4,0},{3,1},{6,2},{1,3},{0,4},{7,5},{2,6},{5,7},{12,8},{11,9},{14,... | collective-permute-start | bytes 983048 | tf_op jit(solution)/shard_map/ppermute | solution.py:81
  46.5 3.6 %collective-permute-done.9 = bf16[64,640]{1,0:T(8,128)(2,1)S(1)} collective-permute-done((bf16[64,640]{1,0:T(8,128)(2,1)S(1)}, bf16[64,640]{1,0:T(8,128)(2,1)S(1)}, u32[]{:S(2)}, u32[]{:S(2)}) %collective-permute-start.9) | collective-permute-done | bytes 81952 | tf_op jit(solution)/shard_map/ppermute | solution.py:61
  50.1 3.4 %collective-permute-start.13 = (bf16[192,640]{1,0:T(8,128)(2,1)S(1)}, bf16[192,640]{1,0:T(8,128)(2,1)S(1)}, u32[]{:S(2)}, u32[]{:S(2)}) collective-permute-start(bf16[192,640]{1,0:T(8,128)(2,1)S(1)} %constant_dynamic-update-slice_fusion.2.refs_0_), channel_id=1, source_target_pairs={{6,0},{4,2},{2,4},{0,6},{7,1},{5,3},{3,5},{1,7},{14,8},{12,10},{10... | collective-permute-start | bytes 737288 | tf_op jit(solution)/shard_map/ppermute | solution.py:61
  54.2 5.2 %collective-permute-done.16.refs_2_ = bf16[256,640]{1,0:T(8,128)(2,1)S(1)} collective-permute-done((bf16[256,640]{1,0:T(8,128)(2,1)S(1)}, bf16[256,640]{1,0:T(8,128)(2,1)S(1)}, u32[]{:S(2)}, u32[]{:S(2)}) %collective-permute-start.16) | collective-permute-done | bytes 327712 | tf_op jit(solution)/shard_map/ppermute | solution.py:81
  59.4 7.0 %attend_plane.1 = (bf16[640,512]{1,0:T(8,128)(2,1)S(1)}, f32[10,8,512]{2,1,0:T(8,128)S(1)}) custom-call(s32[24]{0:T(128)S(1)} %get-tuple-element.41.table_ref, bf16[640,512]{1,0:T(8,128)(2,1)S(1)} %get-tuple-element.44.q_ref, bf16[256,640]{1,0:T(8,128)(2,1)S(1)} %collective-permute-done.14.refs_0_, bf16[256,640]{1,0:T(8,128)(2,1)S(1)} %collective-permute-done.15.refs_1_, ...), custom_call_target="tpu_custom_call" | custom-call | flops 5284823040 | bytes 2293760 | tf_op jit(solution)/shard_map/attend_plane/pallas_call | solution.py:383
  66.5 7.6 %attend_anchors.1 = (bf16[640,256]{1,0:T(8,128)(2,1)S(1)}, f32[16,256]{1,0:T(8,128)S(1)}, bf16[688,256]{1,0:T(8,128)(2,1)S(1)}) custom-call(s32[24]{0:T(128)S(1)} %get-tuple-element.41.table_ref, bf16[640,512]{1,0:T(8,128)(2,1)S(1)} %get-tuple-element.44.q_ref, bf16[192,640]{1,0:T(8,128)(2,1)S(1)} %constant_dynamic-update-slice_fusion.2.refs_0_, ...), custom_call_target="tpu_custom_call" | custom-call | flops 5284823040 | bytes 2293760 | tf_op jit(solution)/shard_map/attend_anchors/pallas_call | solution.py:460
  74.1 1.7 %collective-permute-done.17.refs_0_ = bf16[688,256]{1,0:T(8,128)(2,1)S(1)} collective-permute-done((bf16[688,256]{1,0:T(8,128)(2,1)S(1)}, bf16[688,256]{1,0:T(8,128)(2,1)S(1)}, u32[]{:S(2)}, u32[]{:S(2)}) %collective-permute-start.17) | collective-permute-done | bytes 352288 | tf_op jit(solution)/shard_map/ppermute | solution.py:66
  75.8 1.3 %finish.1 = bf16[256,640]{1,0:T(8,128)(2,1)} custom-call(bf16[640,256]{1,0:T(8,128)(2,1)S(1)} %get-tuple-element.53.own_ref, f32[16,256]{1,0:T(8,128)S(1)} %get-tuple-element.54.level_ref, bf16[688,256]{1,0:T(8,128)(2,1)S(1)} %collective-permute-done.17.refs_0_, bf16[640,640]{1,0:T(8,128)(2,1)S(1)} %copy-done), custom_call_target="tpu_custom_call" | custom-call | flops 209715200 | bytes 1802240 | tf_op jit(solution)/shard_map/finish/pallas_call | solution.py:510
  (52 shorter events, 5.6 us)
Async XLA Ops:
  1.7 1.4 %collective-permute-start = (bf16[8,640]{1,0:T(8,128)(2,1)S(1)}, bf16[8,640]{1,0:T(8,128)(2,1)S(1)}, u32[]{:S(2)}, u32[]{:S(2)}) collective-permute-start(bf16[8,640]{1,0:T(8,128)(2,1)S(1)} %broadcast_select_fusion.2), channel_id=1, source_target_pairs={{1,0},{0,1},{3,2},{2,3},{5,4},{4,5},{7,6},{6,7},{9,8},{8,9},{11,10... | collective-permute-start | bytes 30728 | tf_op jit(solution)/shard_map/ppermute | solution.py:66
  3.4 5.9 %collective-permute-start.1 = (bf16[68,640]{1,0:T(8,128)(2,1)S(1)}, bf16[68,640]{1,0:T(8,128)(2,1)S(1)}, u32[]{:S(2)}, u32[]{:S(2)}) collective-permute-start(bf16[68,640]{1,0:T(8,128)(2,1)S(1)} %concatenate.9), channel_id=1, source_target_pairs={{2,0},{0,2},{6,4},{4,6},{3,1},{1,3},{7,5},{5,7},{10,8},{8,10},{14,... | collective-permute-start | bytes 261128 | tf_op jit(solution)/shard_map/ppermute | solution.py:61
  9.3 7.1 %collective-permute-start.2 = (bf16[34,640]{1,0:T(8,128)(2,1)S(1)}, bf16[34,640]{1,0:T(8,128)(2,1)S(1)}, u32[]{:S(2)}, u32[]{:S(2)}) collective-permute-start(bf16[34,640]{1,0:T(8,128)(2,1)S(1)} %broadcast_select_fusion), channel_id=1, source_target_pairs={{4,0},{6,2},{0,4},{2,6},{5,1},{7,3},{1,5},{3,7},{12,8},{14,10},{8,... | collective-permute-start | bytes 130568 | tf_op jit(solution)/shard_map/ppermute | solution.py:61
  14.6 1.8 %copy-start.2 = (bf16[1,8,32,640]{3,2,1,0:T(8,128)(2,1)S(1)}, bf16[1,8,32,640]{3,2,1,0:T(8,128)(2,1)}, u32[]{:S(2)}) copy-start(bf16[1,8,32,640]{3,2,1,0:T(8,128)(2,1)} %param.9) | copy-start | bytes 983044
  14.6 1.8 %copy-start.3 = (s32[4,16]{1,0:T(4,128)S(1)}, s32[4,16]{1,0:T(4,128)}, u32[]{:S(2)}) copy-start(s32[4,16]{1,0:T(4,128)} %refs_5_.2) | copy-start | bytes 772
  16.5 20.6 %copy-start.6 = (bf16[640,640]{1,0:T(8,128)(2,1)S(1)}, bf16[640,640]{1,0:T(8,128)(2,1)}, u32[]{:S(2)}) copy-start(bf16[640,640]{1,0:T(8,128)(2,1)} %refs_5_.3) | copy-start | bytes 2457604
  16.5 20.6 %copy-start.7 = (bf16[640,640]{1,0:T(8,128)(2,1)S(1)}, bf16[640,640]{1,0:T(8,128)(2,1)}, u32[]{:S(2)}) copy-start(bf16[640,640]{1,0:T(8,128)(2,1)} %refs_8_.1) | copy-start | bytes 2457604
  16.5 20.6 %copy-start.8 = (bf16[640,640]{1,0:T(8,128)(2,1)S(1)}, bf16[640,640]{1,0:T(8,128)(2,1)}, u32[]{:S(2)}) copy-start(bf16[640,640]{1,0:T(8,128)(2,1)} %refs_9_.1) | copy-start | bytes 2457604
  21.0 1.5 %collective-permute-start.4 = (bf16[128,640]{1,0:T(8,128)(2,1)S(1)}, bf16[128,640]{1,0:T(8,128)(2,1)S(1)}, u32[]{:S(2)}, u32[]{:S(2)}) collective-permute-start(bf16[128,640]{1,0:T(8,128)(2,1)S(1)} %get-tuple-element.43.refs_1_), channel_id=1, source_target_pairs={{1,0},{0,1},{3,2},{2,3},{5,4},{4,5},{7,6},{6,7},{9,8},{8,9},{11,10... | collective-permute-start | bytes 491528 | tf_op jit(solution)/shard_map/ppermute | solution.py:66
  21.1 16.0 %collective-permute-start.3 = (bf16[128,640]{1,0:T(8,128)(2,1)S(1)}, bf16[128,640]{1,0:T(8,128)(2,1)S(1)}, u32[]{:S(2)}, u32[]{:S(2)}) collective-permute-start(bf16[128,640]{1,0:T(8,128)(2,1)S(1)} %get-tuple-element.42.refs_0_), channel_id=1, source_target_pairs={{1,0},{0,1},{3,2},{2,3},{5,4},{4,5},{7,6},{6,7},{9,8},{8,9},{11,10... | collective-permute-start | bytes 491528 | tf_op jit(solution)/shard_map/ppermute | solution.py:66
  22.5 21.5 %collective-permute-start.14 = (bf16[256,640]{1,0:T(8,128)(2,1)S(1)}, bf16[256,640]{1,0:T(8,128)(2,1)S(1)}, u32[]{:S(2)}, u32[]{:S(2)}) collective-permute-start(bf16[256,640]{1,0:T(8,128)(2,1)S(1)} %constant_dynamic-update-slice_fusion.refs_4_.key_ref), channel_id=1, source_target_pairs={{2,0},{5,1},{0,2},{7,3},{6,4},{1,5},{4,6},{3,7},{10,8},{13,9},{8,1... | collective-permute-start | bytes 983048 | tf_op jit(solution)/shard_map/ppermute | solution.py:81
  24.7 9.2 %collective-permute-start.5 = (bf16[64,640]{1,0:T(8,128)(2,1)S(1)}, bf16[64,640]{1,0:T(8,128)(2,1)S(1)}, u32[]{:S(2)}, u32[]{:S(2)}) collective-permute-start(bf16[64,640]{1,0:T(8,128)(2,1)S(1)} %get-tuple-element.46), channel_id=1, source_target_pairs={{2,0},{0,2},{6,4},{4,6},{3,1},{1,3},{7,5},{5,7},{10,8},{8,10},{14,... | collective-permute-start | bytes 245768 | tf_op jit(solution)/shard_map/ppermute | solution.py:61
  25.3 8.6 %collective-permute-start.6 = (bf16[64,640]{1,0:T(8,128)(2,1)S(1)}, bf16[64,640]{1,0:T(8,128)(2,1)S(1)}, u32[]{:S(2)}, u32[]{:S(2)}) collective-permute-start(bf16[64,640]{1,0:T(8,128)(2,1)S(1)} %get-tuple-element.47), channel_id=1, source_target_pairs={{4,0},{6,2},{0,4},{2,6},{5,1},{7,3},{1,5},{3,7},{12,8},{14,10},{8,... | collective-permute-start | bytes 245768 | tf_op jit(solution)/shard_map/ppermute | solution.py:61
  25.5 9.1 %collective-permute-start.7 = (bf16[64,640]{1,0:T(8,128)(2,1)S(1)}, bf16[64,640]{1,0:T(8,128)(2,1)S(1)}, u32[]{:S(2)}, u32[]{:S(2)}) collective-permute-start(bf16[64,640]{1,0:T(8,128)(2,1)S(1)} %get-tuple-element.48), channel_id=1, source_target_pairs={{6,0},{4,2},{2,4},{0,6},{7,1},{5,3},{3,5},{1,7},{14,8},{12,10},{10... | collective-permute-start | bytes 245768 | tf_op jit(solution)/shard_map/ppermute | solution.py:61
  33.9 20.3 %collective-permute-start.15 = (bf16[256,640]{1,0:T(8,128)(2,1)S(1)}, bf16[256,640]{1,0:T(8,128)(2,1)S(1)}, u32[]{:S(2)}, u32[]{:S(2)}) collective-permute-start(bf16[256,640]{1,0:T(8,128)(2,1)S(1)} %constant_dynamic-update-slice_fusion.refs_4_.key_ref), channel_id=1, source_target_pairs={{4,0},{3,1},{6,2},{1,3},{0,4},{7,5},{2,6},{5,7},{12,8},{11,9},{14,... | collective-permute-start | bytes 983048 | tf_op jit(solution)/shard_map/ppermute | solution.py:81
  35.4 11.1 %collective-permute-start.8 = (bf16[64,640]{1,0:T(8,128)(2,1)S(1)}, bf16[64,640]{1,0:T(8,128)(2,1)S(1)}, u32[]{:S(2)}, u32[]{:S(2)}) collective-permute-start(bf16[64,640]{1,0:T(8,128)(2,1)S(1)} %accept.1), channel_id=1, source_target_pairs={{8,0},{0,8},{24,16},{16,24},{9,1},{1,9},{25,17},{17,25},{10,2},{2,... | collective-permute-start | bytes 245768 | tf_op jit(solution)/shard_map/ppermute | solution.py:61
  41.3 8.8 %collective-permute-start.10 = (bf16[64,640]{1,0:T(8,128)(2,1)S(1)}, bf16[64,640]{1,0:T(8,128)(2,1)S(1)}, u32[]{:S(2)}, u32[]{:S(2)}) collective-permute-start(bf16[64,640]{1,0:T(8,128)(2,1)S(1)} %accept.1), channel_id=1, source_target_pairs={{24,0},{16,8},{8,16},{0,24},{25,1},{17,9},{9,17},{1,25},{26,2},{18... | collective-permute-start | bytes 245768 | tf_op jit(solution)/shard_map/ppermute | solution.py:61
  43.8 6.2 %collective-permute-start.9 = (bf16[64,640]{1,0:T(8,128)(2,1)S(1)}, bf16[64,640]{1,0:T(8,128)(2,1)S(1)}, u32[]{:S(2)}, u32[]{:S(2)}) collective-permute-start(bf16[64,640]{1,0:T(8,128)(2,1)S(1)} %accept.1), channel_id=1, source_target_pairs={{16,0},{24,8},{0,16},{8,24},{17,1},{25,9},{1,17},{9,25},{18,2},{26... | collective-permute-start | bytes 245768 | tf_op jit(solution)/shard_map/ppermute | solution.py:61
  44.1 15.3 %collective-permute-start.16 = (bf16[256,640]{1,0:T(8,128)(2,1)S(1)}, bf16[256,640]{1,0:T(8,128)(2,1)S(1)}, u32[]{:S(2)}, u32[]{:S(2)}) collective-permute-start(bf16[256,640]{1,0:T(8,128)(2,1)S(1)} %collective-permute-done.14.refs_0_), channel_id=1, source_target_pairs={{4,0},{3,1},{6,2},{1,3},{0,4},{7,5},{2,6},{5,7},{12,8},{11,9},{14,... | collective-permute-start | bytes 983048 | tf_op jit(solution)/shard_map/ppermute | solution.py:81
  50.1 16.3 %collective-permute-start.13 = (bf16[192,640]{1,0:T(8,128)(2,1)S(1)}, bf16[192,640]{1,0:T(8,128)(2,1)S(1)}, u32[]{:S(2)}, u32[]{:S(2)}) collective-permute-start(bf16[192,640]{1,0:T(8,128)(2,1)S(1)} %constant_dynamic-update-slice_fusion.2.refs_0_), channel_id=1, source_target_pairs={{6,0},{4,2},{2,4},{0,6},{7,1},{5,3},{3,5},{1,7},{14,8},{12,10},{10... | collective-permute-start | bytes 737288 | tf_op jit(solution)/shard_map/ppermute | solution.py:61
  53.6 12.9 %collective-permute-start.12 = (bf16[192,640]{1,0:T(8,128)(2,1)S(1)}, bf16[192,640]{1,0:T(8,128)(2,1)S(1)}, u32[]{:S(2)}, u32[]{:S(2)}) collective-permute-start(bf16[192,640]{1,0:T(8,128)(2,1)S(1)} %constant_dynamic-update-slice_fusion.2.refs_0_), channel_id=1, source_target_pairs={{4,0},{6,2},{0,4},{2,6},{5,1},{7,3},{1,5},{3,7},{12,8},{14,10},{8,... | collective-permute-start | bytes 737288 | tf_op jit(solution)/shard_map/ppermute | solution.py:61
  53.6 12.9 %collective-permute-start.11 = (bf16[192,640]{1,0:T(8,128)(2,1)S(1)}, bf16[192,640]{1,0:T(8,128)(2,1)S(1)}, u32[]{:S(2)}, u32[]{:S(2)}) collective-permute-start(bf16[192,640]{1,0:T(8,128)(2,1)S(1)} %constant_dynamic-update-slice_fusion.2.refs_0_), channel_id=1, source_target_pairs={{2,0},{0,2},{6,4},{4,6},{3,1},{1,3},{7,5},{5,7},{10,8},{8,10},{14,... | collective-permute-start | bytes 737288 | tf_op jit(solution)/shard_map/ppermute | solution.py:61
  66.5 9.3 %copy-start = (bf16[640,640]{1,0:T(8,128)(2,1)S(1)}, bf16[640,640]{1,0:T(8,128)(2,1)}, u32[]{:S(2)}) copy-start(bf16[640,640]{1,0:T(8,128)(2,1)} %refs_1_.1) | copy-start | bytes 2457604
  74.1 1.7 %collective-permute-start.17 = (bf16[688,256]{1,0:T(8,128)(2,1)S(1)}, bf16[688,256]{1,0:T(8,128)(2,1)S(1)}, u32[]{:S(2)}, u32[]{:S(2)}) collective-permute-start(bf16[688,256]{1,0:T(8,128)(2,1)S(1)} %get-tuple-element.55), channel_id=1, source_target_pairs={{1,0},{0,1},{3,2},{2,3},{5,4},{4,5},{7,6},{6,7},{9,8},{8,9},{11,10... | collective-permute-start | bytes 1056776 | tf_op jit(solution)/shard_map/ppermute | solution.py:66
  (3 other events, 4.7 us)

commit v5 on v3

--- a/solution.py
+++ b/solution.py
@@ -271,12 +271,12 @@
         v_scr[head, HEAD_DIM:] = ones
 
 
-def attend_heads(q_ref, k_scr, v_scr, out_ref, level_ref, width):
+def attend_heads(q_ref, k_scr, v_scr, out_ref, level_ref, width, span=None):
     zeros = jnp.zeros((HEAD_DIM, width), BF16)
     items = [
         (head, slice(at, at + width))
         for head in range(q_ref.shape[0] // HEAD_DIM)
-        for at in range(0, q_ref.shape[1], width)
+        for at in range(*(span or (0, q_ref.shape[1])), width)
     ]
 
     def scores_of(head, cols):
@@ -394,9 +394,8 @@
     anchors, images, _, prows, _ = info
     key_refs, refs = refs[:tiles], refs[tiles:]
     early_refs, refs = refs[:2 * earlier], refs[2 * earlier:]
-    wk_ref, wv_ref, *out_refs = refs[:2 + groups + 1]
-    out_scr, level_scr, k_scr, v_scr = refs[3 + groups:]
-    own_ref, own_level_ref, *sent_refs = out_refs
+    wk_ref, wv_ref, k_ref, v_ref = refs[:4]
+    sent_refs, (out_scr, level_scr) = refs[4:-2], refs[-2:]
     table = Table(table_ref, anchors, images)
     if table.every_image:
         each = NSEL // prows
@@ -407,53 +406,84 @@
     else:
         times = [table.anchor_times(t, slot) for t in range(tiles) for slot in range(NSEL)]
     normed = jnp.concatenate([ref[...] for ref in key_refs], axis=0)
-    project(normed, times, wk_ref, wv_ref, k_scr, v_scr)
+    project(normed, times, wk_ref, wv_ref, k_ref, v_ref)
     channels = q_ref.shape[0]
     width = q_ref.shape[1] // groups
-    attend_heads(q_ref, k_scr, v_scr, out_scr, level_scr, width)
-    pairs = list(zip(early_refs[::2], early_refs[1::2])) + [(out_scr, level_scr)]
+    if groups > 1:
+        attend_heads(q_ref, k_ref, v_ref, out_scr, level_scr, width, (width, groups * width))
+    for n in range(1, groups):
+        ref, cols = sent_refs[n - 1], slice(n * width, (n + 1) * width)
+        levels = merge_all(list(early_refs) + [out_scr, level_scr], ref, cols)
+        for term in range(3):
+            high = levels.astype(BF16)
+            at = channels + term * 2 * SUBLANES
+            ref[at:at + 2 * SUBLANES] = high
+            levels = levels - high.astype(F32)
+
+
+def merge_all(refs, out_ref, cols):
     parts = [
-        (ref, lambda head, cols, level=level: level[head, 0:1, cols]) for ref, level in pairs
+        (ref, lambda head, at, level=level: level[head, 0:1, at])
+        for ref, level in zip(refs[::2], refs[1::2])
     ]
-    heads = channels // HEAD_DIM
+    width = cols.stop - cols.start
     row = lax.broadcasted_iota(jnp.int32, (2 * SUBLANES, width), 0)
-    for n in range(groups):
-        cols = slice(n * width, (n + 1) * width)
-        ref = own_ref if n == 0 else sent_refs[n - 1]
-        levels = jnp.zeros((2 * SUBLANES, width), F32)
-        for head in range(heads):
-            value, level = merge_head(parts, head, cols)
-            ref[head * HEAD_DIM:(head + 1) * HEAD_DIM] = value.astype(BF16)
-            levels = jnp.where(row == head, level, levels)
-        if n == 0:
-            own_level_ref[...] = levels
-        else:
-            for term in range(3):
-                high = levels.astype(BF16)
-                at = channels + term * 2 * SUBLANES
-                ref[at:at + 2 * SUBLANES] = high
-                levels = levels - high.astype(F32)
+    levels = jnp.zeros((2 * SUBLANES, width), F32)
+    for head in range(refs[0].shape[0] // HEAD_DIM):
+        value, level = merge_head(parts, head, cols)
+        out_ref[head * HEAD_DIM:(head + 1) * HEAD_DIM] = value.astype(BF16)
+        levels = jnp.where(row == head, level, levels)
+    return levels
+
+
+def result_scratch(channels, rows):
+    return [
+        pltpu.VMEM((channels, rows), BF16),
+        pltpu.VMEM((channels // HEAD_DIM, SUBLANES, rows), F32),
+    ]
 
 
 def attend_anchors(info, table, queries, keys, earlier, w_key, w_value, groups):
     size, channels = keys[0].shape
     rows = queries.shape[1]
+    count = size * len(keys)
+    flat = [leaf for part in earlier for leaf in part]
+    return pl.pallas_call(
+        functools.partial(anchor_kernel, info, len(keys), len(earlier), groups),
+        out_shape=(
+            shape(channels // LANES, count, LANES),
+            shape(channels // HEAD_DIM, HEAD_DIM + ONES, count),
+        ) + (shape(channels + 6 * SUBLANES, rows // groups),) * (groups - 1),
+        in_specs=[SMEM] + [VMEM] * (len(keys) + len(flat) + 3),
+        out_specs=(VMEM,) * (1 + groups),
+        scratch_shapes=result_scratch(channels, rows),
+        compiler_params=grant(24),
+        cost_estimate=attend_cost(rows, count, channels),
+        name="attend_anchors",
+    )(table, queries, *keys, *flat, w_key, w_value)
+
+
+def own_anchor_kernel(groups, q_ref, k_ref, v_ref, *refs):
+    *early_refs, own_ref, level_ref, out_scr, level_scr = refs
+    width = q_ref.shape[1] // groups
+    attend_heads(q_ref, k_ref, v_ref, out_scr, level_scr, width, (0, width))
+    level_ref[...] = merge_all(early_refs + [out_scr, level_scr], own_ref, slice(0, width))
+
+
+def attend_anchors_own(queries, k, v, earlier, groups):
+    channels, rows = queries.shape
     width = rows // groups
     flat = [leaf for part in earlier for leaf in part]
-    heads = channels // HEAD_DIM
-    return pl.pallas_call(
-        functools.partial(anchor_kernel, info, len(keys), len(earlier), groups),
-        out_shape=(shape(channels, width), shape(2 * SUBLANES, width, dtype=F32))
-        + (shape(channels + 6 * SUBLANES, width),) * (groups - 1),
-        in_specs=[SMEM] + [VMEM] * (len(keys) + len(flat) + 3),
-        out_specs=(VMEM,) * (1 + groups),
-        scratch_shapes=[
-            pltpu.VMEM((channels, rows), BF16), pltpu.VMEM((heads, SUBLANES, rows), F32),
-        ] + key_scratch(size * len(keys), channels),
+    return pl.pallas_call(
+        functools.partial(own_anchor_kernel, groups),
+        out_shape=(shape(channels, width), shape(2 * SUBLANES, width, dtype=F32)),
+        in_specs=[VMEM] * (3 + len(flat)),
+        out_specs=(VMEM,) * 2,
+        scratch_shapes=result_scratch(channels, width),
         compiler_params=grant(24),
-        cost_estimate=attend_cost(rows, size * len(keys), channels),
-        name="attend_anchors",
-    )(table, queries, *keys, *flat, w_key, w_value)
+        cost_estimate=attend_cost(width, k.shape[1], channels),
+        name="attend_anchors_own",
+    )(queries, k, v, *flat)
 
 
 def finish_kernel(cores, own_ref, level_ref, *refs):
@@ -619,8 +649,11 @@
         sources = [joined[anchor] for anchor in range(anchors)]
     if plane:
         done.append(attend_plane(info, table, q, plane, w_key, w_value))
-    own, level, *sent = attend_anchors(info, table, q, sources, done, w_key, w_value, cores)
-    received = [shifted(block, "pcol", cores - s) for s, block in enumerate(sent, 1)]
+    k, v, *sent = attend_anchors(info, table, q, sources, done, w_key, w_value, cores)
+    received = []
+    for s, block in enumerate(sent, 1):
+        received.append(shifted(block, "pcol", cores - s))
+    own, level = attend_anchors_own(q, k, v, done, cores)
     attended = finish(own, level, received, w_out, cores)
     return features.reshape(latent.shape), attended.reshape(latent.shape)
 

time: 73 us -> 72 us (0.986)
  waiting for transfers between devices: 20.1 us -> 18.4 us
    pallas_call x0 -> x1, Pallas kernels: none -> 2.87 us  [attend_anchors_own(): pl.pallas_call(functools.partial(own_anchor_kernel, groups), out_shape=(s...]
    pallas_call x1, Pallas kernels: 7.61 us -> 5.44 us  [attend_anchors(): pl.pallas_call(functools.partial(anchor_kernel, info, len(keys), len(earl...]
    ppermute x4, waiting for transfers between devices: 3.26 us -> 1.62 us  [shifted(): lax.ppermute(block, axis, [((i + step) % count, i) for i in range(count)])]
  transfers between devices with their start and end apart: 18 -> 18, of which waited for: 7 -> 6; matrix products, arithmetic and copies ran while one was open for 0% -> 0% of each run, Pallas kernels for 22% -> 26%
where the time goes in v5:
time: 72 us; the launch traced here: 71.8 us
  Pallas kernels  29.2 us (41%)
  starting transfers between devices  21.9 us (30%)
  waiting for transfers between devices  18.4 us (26%)
  local copies, waits for them, and re-layouts  1.19 us (2%)
  between operations  0.92 us (1%)
    ppermute x9, starting transfers between devices, exchange(): lax.ppermute(block, axis, [(source_of(i, step, count), i) for i in range(...  11.5 us
    ppermute x9, waiting for transfers between devices, exchange(): lax.ppermute(block, axis, [(source_of(i, step, count), i) for i in range(...  11.5 us
    pallas_call x1, Pallas kernels, attend_plane(): pl.pallas_call(functools.partial(plane_kernel, info, len(keys)), out_shap...  7.02 us
    ppermute x2, starting transfers between devices, halo(): lax.ppermute(block, 'prow', pairs + [(j, i) for i, j in pairs])  6.28 us
    pallas_call x1, Pallas kernels, attend_anchors(): pl.pallas_call(functools.partial(anchor_kernel, info, len(keys), len(earl...  5.44 us
    ppermute x3, waiting for transfers between devices, hop(): lax.ppermute(rows, ('prow', 'pcol'), [((p ^ (entry if c % 2 == 0 else 3 -...  5.36 us
    pallas_call x1, Pallas kernels, attend_own(): pl.pallas_call(functools.partial(own_kernel, info, len(parts)), out_shape...  4.2 us
    pallas_call x1, Pallas kernels, conv_norm(): pl.pallas_call(functools.partial(conv_kernel, rows, cols, cores), out_sha...  3.93 us
  transfers between devices with their start and end apart: 18, of which 6 were waited for; matrix products, arithmetic and copies ran while one was open for 0% of the time, Pallas kernels for 26%

profile of v5, /device:TPU:0, one launch (start us, length us, event | category | flops | bytes accessed | tf_op | source)
XLA Modules:
  0.0 71.8 jit_solution(13116624507299536389)
XLA Ops:
  0.6 1.0 %copy-done.1 = bf16[1,8,32,640]{3,2,1,0:T(8,128)(2,1)S(1)} copy-done((bf16[1,8,32,640]{3,2,1,0:T(8,128)(2,1)S(1)}, bf16[1,8,32,640]{3,2,1,0:T(8,128)(2,1)}, u32[]{:S(2)}) %copy-start.1) | copy-done | bytes 327704
  2.2 0.8 %collective-permute-done = bf16[8,640]{1,0:T(8,128)(2,1)S(1)} collective-permute-done((bf16[8,640]{1,0:T(8,128)(2,1)S(1)}, bf16[8,640]{1,0:T(8,128)(2,1)S(1)}, u32[]{:S(2)}, u32[]{:S(2)}) %collective-permute-start) | collective-permute-done | bytes 10272 | tf_op jit(solution)/shard_map/ppermute | solution.py:66
  3.8 5.6 %collective-permute-start.1 = (bf16[34,640]{1,0:T(8,128)(2,1)S(1)}, bf16[34,640]{1,0:T(8,128)(2,1)S(1)}, u32[]{:S(2)}, u32[]{:S(2)}) collective-permute-start(bf16[34,640]{1,0:T(8,128)(2,1)S(1)} %get-tuple-element.57), channel_id=1, source_target_pairs={{0,2},{4,6},{2,0},{6,4},{1,3},{5,7},{3,1},{7,5},{8,10},{12,14},{10... | collective-permute-start | bytes 130568 | tf_op jit(solution)/shard_map/ppermute | solution.py:131
  9.4 3.1 %stage.1.w_ref = bf16[3,3,640,640]{3,2,1,0:T(8,128)(2,1)S(1)} custom-call(bf16[3,3,640,640]{3,2,1,0:T(8,128)(2,1)} %in_ref.1), custom_call_target="tpu_custom_call" | custom-call | bytes 14745600 | tf_op jit(solution)/shard_map/stage/pallas_call | solution.py:144
  12.7 3.9 %conv_norm.1 = (bf16[256,640]{1,0:T(8,128)(2,1)}, bf16[128,640]{1,0:T(8,128)(2,1)S(1)}, bf16[128,640]{1,0:T(8,128)(2,1)S(1)}) custom-call(bf16[256,640]{1,0:T(8,128)(2,1)S(1)} %bitcast.6, bf16[8,640]{1,0:T(8,128)(2,1)S(1)} %get-tuple-element.63.left_ref, bf16[8,640]{1,0:T(8,128)(2,1)S(1)} %get-tuple-element.62.right_ref, ...), custom_call_target="tpu_custom_call" | custom-call | flops 1887436800 | bytes 7372800 | tf_op jit(solution)/shard_map/conv_norm/pallas_call | solution.py:202
  17.2 0.8 %collective-permute-done.4.refs_3_ = bf16[128,640]{1,0:T(8,128)(2,1)S(1)} collective-permute-done((bf16[128,640]{1,0:T(8,128)(2,1)S(1)}, bf16[128,640]{1,0:T(8,128)(2,1)S(1)}, u32[]{:S(2)}, u32[]{:S(2)}) %collective-permute-start.4) | collective-permute-done | bytes 163872 | tf_op jit(solution)/shard_map/ppermute | solution.py:66
  18.0 1.0 %collective-permute-start.14 = (bf16[256,640]{1,0:T(8,128)(2,1)S(1)}, bf16[256,640]{1,0:T(8,128)(2,1)S(1)}, u32[]{:S(2)}, u32[]{:S(2)}) collective-permute-start(bf16[256,640]{1,0:T(8,128)(2,1)S(1)} %constant_dynamic-update-slice_fusion.refs_4_.key_ref), channel_id=1, source_target_pairs={{2,0},{5,1},{0,2},{7,3},{6,4},{1,5},{4,6},{3,7},{10,8},{13,9},{8,1... | collective-permute-start | bytes 983048 | tf_op jit(solution)/shard_map/ppermute | solution.py:81
  19.7 1.2 %collective-permute-start.5 = (bf16[64,640]{1,0:T(8,128)(2,1)S(1)}, bf16[64,640]{1,0:T(8,128)(2,1)S(1)}, u32[]{:S(2)}, u32[]{:S(2)}) collective-permute-start(bf16[64,640]{1,0:T(8,128)(2,1)S(1)} %get-tuple-element.42), channel_id=1, source_target_pairs={{2,0},{0,2},{6,4},{4,6},{3,1},{1,3},{7,5},{5,7},{10,8},{8,10},{14,... | collective-permute-start | bytes 245768 | tf_op jit(solution)/shard_map/ppermute | solution.py:61
  20.9 0.9 %collective-permute-start.6 = (bf16[64,640]{1,0:T(8,128)(2,1)S(1)}, bf16[64,640]{1,0:T(8,128)(2,1)S(1)}, u32[]{:S(2)}, u32[]{:S(2)}) collective-permute-start(bf16[64,640]{1,0:T(8,128)(2,1)S(1)} %get-tuple-element.43), channel_id=1, source_target_pairs={{4,0},{6,2},{0,4},{2,6},{5,1},{7,3},{1,5},{3,7},{12,8},{14,10},{8,... | collective-permute-start | bytes 245768 | tf_op jit(solution)/shard_map/ppermute | solution.py:61
  21.8 1.5 %collective-permute-start.7 = (bf16[64,640]{1,0:T(8,128)(2,1)S(1)}, bf16[64,640]{1,0:T(8,128)(2,1)S(1)}, u32[]{:S(2)}, u32[]{:S(2)}) collective-permute-start(bf16[64,640]{1,0:T(8,128)(2,1)S(1)} %get-tuple-element.44), channel_id=1, source_target_pairs={{6,0},{4,2},{2,4},{0,6},{7,1},{5,3},{3,5},{1,7},{14,8},{12,10},{10... | collective-permute-start | bytes 245768 | tf_op jit(solution)/shard_map/ppermute | solution.py:61
  23.2 5.7 %collective-permute-done.5.refs_1_ = bf16[64,640]{1,0:T(8,128)(2,1)S(1)} collective-permute-done((bf16[64,640]{1,0:T(8,128)(2,1)S(1)}, bf16[64,640]{1,0:T(8,128)(2,1)S(1)}, u32[]{:S(2)}, u32[]{:S(2)}) %collective-permute-start.5) | collective-permute-done | bytes 81952 | tf_op jit(solution)/shard_map/ppermute | solution.py:61
  29.5 1.2 %collective-permute-done.7.refs_3_ = bf16[64,640]{1,0:T(8,128)(2,1)S(1)} collective-permute-done((bf16[64,640]{1,0:T(8,128)(2,1)S(1)}, bf16[64,640]{1,0:T(8,128)(2,1)S(1)}, u32[]{:S(2)}, u32[]{:S(2)}) %collective-permute-start.7) | collective-permute-done | bytes 81952 | tf_op jit(solution)/shard_map/ppermute | solution.py:61
  31.5 1.6 %collective-permute-start.8 = (bf16[64,640]{1,0:T(8,128)(2,1)S(1)}, bf16[64,640]{1,0:T(8,128)(2,1)S(1)}, u32[]{:S(2)}, u32[]{:S(2)}) collective-permute-start(bf16[64,640]{1,0:T(8,128)(2,1)S(1)} %accept.1), channel_id=1, source_target_pairs={{8,0},{0,8},{24,16},{16,24},{9,1},{1,9},{25,17},{17,25},{10,2},{2,... | collective-permute-start | bytes 245768 | tf_op jit(solution)/shard_map/ppermute | solution.py:61
  33.2 4.2 %attend_own.1 = (bf16[640,512]{1,0:T(8,128)(2,1)S(1)}, bf16[640,512]{1,0:T(8,128)(2,1)S(1)}, f32[10,8,512]{2,1,0:T(8,128)S(1)}) custom-call(s32[24]{0:T(128)S(1)} %pad_add_fusion.table_ref, bf16[128,640]{1,0:T(8,128)(2,1)S(1)} %get-tuple-element.38.refs_0_, bf16[128,640]{1,0:T(8,128)(2,1)S(1)} %get-tuple-element.39.refs_1_, ...), custom_call_target="tpu_custom_call" | custom-call | flops 2181038080 | bytes 1638400 | tf_op jit(solution)/shard_map/attend_own/pallas_call | solution.py:335
  37.4 2.5 %collective-permute-start.10 = (bf16[64,640]{1,0:T(8,128)(2,1)S(1)}, bf16[64,640]{1,0:T(8,128)(2,1)S(1)}, u32[]{:S(2)}, u32[]{:S(2)}) collective-permute-start(bf16[64,640]{1,0:T(8,128)(2,1)S(1)} %accept.1), channel_id=1, source_target_pairs={{24,0},{16,8},{8,16},{0,24},{25,1},{17,9},{9,17},{1,25},{26,2},{18... | collective-permute-start | bytes 245768 | tf_op jit(solution)/shard_map/ppermute | solution.py:61
  40.1 1.4 %collective-permute-start.16 = (bf16[256,640]{1,0:T(8,128)(2,1)S(1)}, bf16[256,640]{1,0:T(8,128)(2,1)S(1)}, u32[]{:S(2)}, u32[]{:S(2)}) collective-permute-start(bf16[256,640]{1,0:T(8,128)(2,1)S(1)} %collective-permute-done.14.refs_0_), channel_id=1, source_target_pairs={{4,0},{3,1},{6,2},{1,3},{0,4},{7,5},{2,6},{5,7},{12,8},{11,9},{14,... | collective-permute-start | bytes 983048 | tf_op jit(solution)/shard_map/ppermute | solution.py:81
  41.6 4.6 %collective-permute-done.9 = bf16[64,640]{1,0:T(8,128)(2,1)S(1)} collective-permute-done((bf16[64,640]{1,0:T(8,128)(2,1)S(1)}, bf16[64,640]{1,0:T(8,128)(2,1)S(1)}, u32[]{:S(2)}, u32[]{:S(2)}) %collective-permute-start.9) | collective-permute-done | bytes 81952 | tf_op jit(solution)/shard_map/ppermute | solution.py:61
  46.2 1.6 %collective-permute-start.13 = (bf16[192,640]{1,0:T(8,128)(2,1)S(1)}, bf16[192,640]{1,0:T(8,128)(2,1)S(1)}, u32[]{:S(2)}, u32[]{:S(2)}) collective-permute-start(bf16[192,640]{1,0:T(8,128)(2,1)S(1)} %constant_dynamic-update-slice_fusion.2.refs_0_), channel_id=1, source_target_pairs={{6,0},{4,2},{2,4},{0,6},{7,1},{5,3},{3,5},{1,7},{14,8},{12,10},{10... | collective-permute-start | bytes 737288 | tf_op jit(solution)/shard_map/ppermute | solution.py:61
  47.8 1.3 %collective-permute-start.12 = (bf16[192,640]{1,0:T(8,128)(2,1)S(1)}, bf16[192,640]{1,0:T(8,128)(2,1)S(1)}, u32[]{:S(2)}, u32[]{:S(2)}) collective-permute-start(bf16[192,640]{1,0:T(8,128)(2,1)S(1)} %constant_dynamic-update-slice_fusion.2.refs_0_), channel_id=1, source_target_pairs={{4,0},{6,2},{0,4},{2,6},{5,1},{7,3},{1,5},{3,7},{12,8},{14,10},{8,... | collective-permute-start | bytes 737288 | tf_op jit(solution)/shard_map/ppermute | solution.py:61
  49.7 5.4 %collective-permute-done.16.refs_2_ = bf16[256,640]{1,0:T(8,128)(2,1)S(1)} collective-permute-done((bf16[256,640]{1,0:T(8,128)(2,1)S(1)}, bf16[256,640]{1,0:T(8,128)(2,1)S(1)}, u32[]{:S(2)}, u32[]{:S(2)}) %collective-permute-start.16) | collective-permute-done | bytes 327712 | tf_op jit(solution)/shard_map/ppermute | solution.py:81
  55.1 7.0 %attend_plane.1 = (bf16[640,512]{1,0:T(8,128)(2,1)S(1)}, f32[10,8,512]{2,1,0:T(8,128)S(1)}) custom-call(s32[24]{0:T(128)S(1)} %pad_add_fusion.table_ref, bf16[640,512]{1,0:T(8,128)(2,1)S(1)} %get-tuple-element.40.q_ref, bf16[256,640]{1,0:T(8,128)(2,1)S(1)} %collective-permute-done.14.refs_0_, bf16[256,640]{1,0:T(8,128)(2,1)S(1)} %collective-permute-done.15.refs_1_, ...), custom_call_target="tpu_custom_call" | custom-call | flops 5284823040 | bytes 2293760 | tf_op jit(solution)/shard_map/attend_plane/pallas_call | solution.py:367
  62.2 5.4 %attend_anchors.1 = (bf16[5,768,128]{2,1,0:T(8,128)(2,1)S(1)}, bf16[10,80,768]{2,1,0:T(8,128)(2,1)S(1)}, bf16[688,256]{1,0:T(8,128)(2,1)S(1)}) custom-call(s32[24]{0:T(128)S(1)} %pad_add_fusion.table_ref, bf16[640,512]{1,0:T(8,128)(2,1)S(1)} %get-tuple-element.40.q_ref, bf16[192,640]{1,0:T(8,128)(2,1)S(1)} %constant_dynamic-update-slice_fusion.2.refs_0_, ...), custom_call_target="tpu_custom_call" | custom-call | flops 5284823040 | bytes 2293760 | tf_op jit(solution)/shard_map/attend_anchors/pallas_call | solution.py:451
  67.7 2.9 %attend_anchors_own.1 = (bf16[640,256]{1,0:T(8,128)(2,1)S(1)}, f32[16,256]{1,0:T(8,128)S(1)}) custom-call(bf16[640,512]{1,0:T(8,128)(2,1)S(1)} %get-tuple-element.40.q_ref, bf16[5,768,128]{2,1,0:T(8,128)(2,1)S(1)} %get-tuple-element.49.k_ref, bf16[10,80,768]{2,1,0:T(8,128)(2,1)S(1)} %get-tuple-element.50.v_ref, ...), custom_call_target="tpu_custom_call" | custom-call | flops 3271557120 | bytes 1638400 | tf_op jit(solution)/shard_map/attend_anchors_own/pallas_call | solution.py:477
  70.6 1.3 %finish.1 = bf16[256,640]{1,0:T(8,128)(2,1)} custom-call(bf16[640,256]{1,0:T(8,128)(2,1)S(1)} %get-tuple-element.51.own_ref, f32[16,256]{1,0:T(8,128)S(1)} %get-tuple-element.52.level_ref, bf16[688,256]{1,0:T(8,128)(2,1)S(1)} %collective-permute-done.17.refs_0_, bf16[640,640]{1,0:T(8,128)(2,1)S(1)} %copy-done), custom_call_target="tpu_custom_call" | custom-call | flops 209715200 | bytes 1802240 | tf_op jit(solution)/shard_map/finish/pallas_call | solution.py:524
  (52 shorter events, 5.1 us)
Async XLA Ops:
  1.7 1.4 %collective-permute-start = (bf16[8,640]{1,0:T(8,128)(2,1)S(1)}, bf16[8,640]{1,0:T(8,128)(2,1)S(1)}, u32[]{:S(2)}, u32[]{:S(2)}) collective-permute-start(bf16[8,640]{1,0:T(8,128)(2,1)S(1)} %broadcast_select_fusion.5), channel_id=1, source_target_pairs={{1,0},{0,1},{3,2},{2,3},{5,4},{4,5},{7,6},{6,7},{9,8},{8,9},{11,10... | collective-permute-start | bytes 30728 | tf_op jit(solution)/shard_map/ppermute | solution.py:66
  3.1 9.5 %collective-permute-start.2 = (bf16[34,640]{1,0:T(8,128)(2,1)S(1)}, bf16[34,640]{1,0:T(8,128)(2,1)S(1)}, u32[]{:S(2)}, u32[]{:S(2)}) collective-permute-start(bf16[34,640]{1,0:T(8,128)(2,1)S(1)} %get-tuple-element.56), channel_id=1, source_target_pairs={{2,4},{4,2},{3,5},{5,3},{10,12},{12,10},{11,13},{13,11},{18,20},{2... | collective-permute-start | bytes 130568 | tf_op jit(solution)/shard_map/ppermute | solution.py:131
  3.8 8.9 %copy-start.2 = (bf16[1,8,32,640]{3,2,1,0:T(8,128)(2,1)S(1)}, bf16[1,8,32,640]{3,2,1,0:T(8,128)(2,1)}, u32[]{:S(2)}) copy-start(bf16[1,8,32,640]{3,2,1,0:T(8,128)(2,1)} %param.9) | copy-start | bytes 983044
  3.8 8.8 %collective-permute-start.1 = (bf16[34,640]{1,0:T(8,128)(2,1)S(1)}, bf16[34,640]{1,0:T(8,128)(2,1)S(1)}, u32[]{:S(2)}, u32[]{:S(2)}) collective-permute-start(bf16[34,640]{1,0:T(8,128)(2,1)S(1)} %get-tuple-element.57), channel_id=1, source_target_pairs={{0,2},{4,6},{2,0},{6,4},{1,3},{5,7},{3,1},{7,5},{8,10},{12,14},{10... | collective-permute-start | bytes 130568 | tf_op jit(solution)/shard_map/ppermute | solution.py:131
  12.6 6.4 %copy-start.7 = (s32[4]{0:T(128)S(1)}, s32[4]{0:T(128)}, u32[]{:S(2)}) copy-start(s32[4]{0:T(128)} %param.17) | copy-start | bytes 52
  12.6 6.4 %copy-start.8 = (s32[4]{0:T(128)S(1)}, s32[4]{0:T(128)}, u32[]{:S(2)}) copy-start(s32[4]{0:T(128)} %param.15) | copy-start | bytes 52
  12.6 20.6 %copy-start.3 = (bf16[640,640]{1,0:T(8,128)(2,1)S(1)}, bf16[640,640]{1,0:T(8,128)(2,1)}, u32[]{:S(2)}) copy-start(bf16[640,640]{1,0:T(8,128)(2,1)} %refs_5_.1) | copy-start | bytes 2457604
  12.6 20.6 %copy-start.4 = (bf16[640,640]{1,0:T(8,128)(2,1)S(1)}, bf16[640,640]{1,0:T(8,128)(2,1)}, u32[]{:S(2)}) copy-start(bf16[640,640]{1,0:T(8,128)(2,1)} %refs_8_.1) | copy-start | bytes 2457604
  12.6 20.6 %copy-start.5 = (bf16[640,640]{1,0:T(8,128)(2,1)S(1)}, bf16[640,640]{1,0:T(8,128)(2,1)}, u32[]{:S(2)}) copy-start(bf16[640,640]{1,0:T(8,128)(2,1)} %refs_9_.1) | copy-start | bytes 2457604
  16.6 1.4 %collective-permute-start.4 = (bf16[128,640]{1,0:T(8,128)(2,1)S(1)}, bf16[128,640]{1,0:T(8,128)(2,1)S(1)}, u32[]{:S(2)}, u32[]{:S(2)}) collective-permute-start(bf16[128,640]{1,0:T(8,128)(2,1)S(1)} %get-tuple-element.39.refs_1_), channel_id=1, source_target_pairs={{1,0},{0,1},{3,2},{2,3},{5,4},{4,5},{7,6},{6,7},{9,8},{8,9},{11,10... | collective-permute-start | bytes 491528 | tf_op jit(solution)/shard_map/ppermute | solution.py:66
  16.7 16.5 %collective-permute-start.3 = (bf16[128,640]{1,0:T(8,128)(2,1)S(1)}, bf16[128,640]{1,0:T(8,128)(2,1)S(1)}, u32[]{:S(2)}, u32[]{:S(2)}) collective-permute-start(bf16[128,640]{1,0:T(8,128)(2,1)S(1)} %get-tuple-element.38.refs_0_), channel_id=1, source_target_pairs={{1,0},{0,1},{3,2},{2,3},{5,4},{4,5},{7,6},{6,7},{9,8},{8,9},{11,10... | collective-permute-start | bytes 491528 | tf_op jit(solution)/shard_map/ppermute | solution.py:66
  18.0 22.1 %collective-permute-start.14 = (bf16[256,640]{1,0:T(8,128)(2,1)S(1)}, bf16[256,640]{1,0:T(8,128)(2,1)S(1)}, u32[]{:S(2)}, u32[]{:S(2)}) collective-permute-start(bf16[256,640]{1,0:T(8,128)(2,1)S(1)} %constant_dynamic-update-slice_fusion.refs_4_.key_ref), channel_id=1, source_target_pairs={{2,0},{5,1},{0,2},{7,3},{6,4},{1,5},{4,6},{3,7},{10,8},{13,9},{8,1... | collective-permute-start | bytes 983048 | tf_op jit(solution)/shard_map/ppermute | solution.py:81
  19.7 9.3 %collective-permute-start.5 = (bf16[64,640]{1,0:T(8,128)(2,1)S(1)}, bf16[64,640]{1,0:T(8,128)(2,1)S(1)}, u32[]{:S(2)}, u32[]{:S(2)}) collective-permute-start(bf16[64,640]{1,0:T(8,128)(2,1)S(1)} %get-tuple-element.42), channel_id=1, source_target_pairs={{2,0},{0,2},{6,4},{4,6},{3,1},{1,3},{7,5},{5,7},{10,8},{8,10},{14,... | collective-permute-start | bytes 245768 | tf_op jit(solution)/shard_map/ppermute | solution.py:61
  20.9 8.7 %collective-permute-start.6 = (bf16[64,640]{1,0:T(8,128)(2,1)S(1)}, bf16[64,640]{1,0:T(8,128)(2,1)S(1)}, u32[]{:S(2)}, u32[]{:S(2)}) collective-permute-start(bf16[64,640]{1,0:T(8,128)(2,1)S(1)} %get-tuple-element.43), channel_id=1, source_target_pairs={{4,0},{6,2},{0,4},{2,6},{5,1},{7,3},{1,5},{3,7},{12,8},{14,10},{8,... | collective-permute-start | bytes 245768 | tf_op jit(solution)/shard_map/ppermute | solution.py:61
  21.8 9.0 %collective-permute-start.7 = (bf16[64,640]{1,0:T(8,128)(2,1)S(1)}, bf16[64,640]{1,0:T(8,128)(2,1)S(1)}, u32[]{:S(2)}, u32[]{:S(2)}) collective-permute-start(bf16[64,640]{1,0:T(8,128)(2,1)S(1)} %get-tuple-element.44), channel_id=1, source_target_pairs={{6,0},{4,2},{2,4},{0,6},{7,1},{5,3},{3,5},{1,7},{14,8},{12,10},{10... | collective-permute-start | bytes 245768 | tf_op jit(solution)/shard_map/ppermute | solution.py:61
  28.9 20.8 %collective-permute-start.15 = (bf16[256,640]{1,0:T(8,128)(2,1)S(1)}, bf16[256,640]{1,0:T(8,128)(2,1)S(1)}, u32[]{:S(2)}, u32[]{:S(2)}) collective-permute-start(bf16[256,640]{1,0:T(8,128)(2,1)S(1)} %constant_dynamic-update-slice_fusion.refs_4_.key_ref), channel_id=1, source_target_pairs={{4,0},{3,1},{6,2},{1,3},{0,4},{7,5},{2,6},{5,7},{12,8},{11,9},{14,... | collective-permute-start | bytes 983048 | tf_op jit(solution)/shard_map/ppermute | solution.py:81
  31.5 10.0 %collective-permute-start.8 = (bf16[64,640]{1,0:T(8,128)(2,1)S(1)}, bf16[64,640]{1,0:T(8,128)(2,1)S(1)}, u32[]{:S(2)}, u32[]{:S(2)}) collective-permute-start(bf16[64,640]{1,0:T(8,128)(2,1)S(1)} %accept.1), channel_id=1, source_target_pairs={{8,0},{0,8},{24,16},{16,24},{9,1},{1,9},{25,17},{17,25},{10,2},{2,... | collective-permute-start | bytes 245768 | tf_op jit(solution)/shard_map/ppermute | solution.py:61
  37.4 8.8 %collective-permute-start.10 = (bf16[64,640]{1,0:T(8,128)(2,1)S(1)}, bf16[64,640]{1,0:T(8,128)(2,1)S(1)}, u32[]{:S(2)}, u32[]{:S(2)}) collective-permute-start(bf16[64,640]{1,0:T(8,128)(2,1)S(1)} %accept.1), channel_id=1, source_target_pairs={{24,0},{16,8},{8,16},{0,24},{25,1},{17,9},{9,17},{1,25},{26,2},{18... | collective-permute-start | bytes 245768 | tf_op jit(solution)/shard_map/ppermute | solution.py:61
  39.9 6.2 %collective-permute-start.9 = (bf16[64,640]{1,0:T(8,128)(2,1)S(1)}, bf16[64,640]{1,0:T(8,128)(2,1)S(1)}, u32[]{:S(2)}, u32[]{:S(2)}) collective-permute-start(bf16[64,640]{1,0:T(8,128)(2,1)S(1)} %accept.1), channel_id=1, source_target_pairs={{16,0},{24,8},{0,16},{8,24},{17,1},{25,9},{1,17},{9,25},{18,2},{26... | collective-permute-start | bytes 245768 | tf_op jit(solution)/shard_map/ppermute | solution.py:61
  40.1 15.0 %collective-permute-start.16 = (bf16[256,640]{1,0:T(8,128)(2,1)S(1)}, bf16[256,640]{1,0:T(8,128)(2,1)S(1)}, u32[]{:S(2)}, u32[]{:S(2)}) collective-permute-start(bf16[256,640]{1,0:T(8,128)(2,1)S(1)} %collective-permute-done.14.refs_0_), channel_id=1, source_target_pairs={{4,0},{3,1},{6,2},{1,3},{0,4},{7,5},{2,6},{5,7},{12,8},{11,9},{14,... | collective-permute-start | bytes 983048 | tf_op jit(solution)/shard_map/ppermute | solution.py:81
  46.2 15.9 %collective-permute-start.13 = (bf16[192,640]{1,0:T(8,128)(2,1)S(1)}, bf16[192,640]{1,0:T(8,128)(2,1)S(1)}, u32[]{:S(2)}, u32[]{:S(2)}) collective-permute-start(bf16[192,640]{1,0:T(8,128)(2,1)S(1)} %constant_dynamic-update-slice_fusion.2.refs_0_), channel_id=1, source_target_pairs={{6,0},{4,2},{2,4},{0,6},{7,1},{5,3},{3,5},{1,7},{14,8},{12,10},{10... | collective-permute-start | bytes 737288 | tf_op jit(solution)/shard_map/ppermute | solution.py:61
  47.8 14.3 %collective-permute-start.12 = (bf16[192,640]{1,0:T(8,128)(2,1)S(1)}, bf16[192,640]{1,0:T(8,128)(2,1)S(1)}, u32[]{:S(2)}, u32[]{:S(2)}) collective-permute-start(bf16[192,640]{1,0:T(8,128)(2,1)S(1)} %constant_dynamic-update-slice_fusion.2.refs_0_), channel_id=1, source_target_pairs={{4,0},{6,2},{0,4},{2,6},{5,1},{7,3},{1,5},{3,7},{12,8},{14,10},{8,... | collective-permute-start | bytes 737288 | tf_op jit(solution)/shard_map/ppermute | solution.py:61
  49.1 13.1 %collective-permute-start.11 = (bf16[192,640]{1,0:T(8,128)(2,1)S(1)}, bf16[192,640]{1,0:T(8,128)(2,1)S(1)}, u32[]{:S(2)}, u32[]{:S(2)}) collective-permute-start(bf16[192,640]{1,0:T(8,128)(2,1)S(1)} %constant_dynamic-update-slice_fusion.2.refs_0_), channel_id=1, source_target_pairs={{2,0},{0,2},{6,4},{4,6},{3,1},{1,3},{7,5},{5,7},{10,8},{8,10},{14,... | collective-permute-start | bytes 737288 | tf_op jit(solution)/shard_map/ppermute | solution.py:61
  67.6 3.0 %collective-permute-start.17 = (bf16[688,256]{1,0:T(8,128)(2,1)S(1)}, bf16[688,256]{1,0:T(8,128)(2,1)S(1)}, u32[]{:S(2)}, u32[]{:S(2)}) collective-permute-start(bf16[688,256]{1,0:T(8,128)(2,1)S(1)} %get-tuple-element.53), channel_id=1, source_target_pairs={{1,0},{0,1},{3,2},{2,3},{5,4},{4,5},{7,6},{6,7},{9,8},{8,9},{11,10... | collective-permute-start | bytes 1056776 | tf_op jit(solution)/shard_map/ppermute | solution.py:66
  (3 other events, 8.0 us)

commit v6 on v5

--- a/solution.py
+++ b/solution.py
@@ -13,7 +13,8 @@
 LANES = 128
 SUBLANES = 8
 ONES = 16
-AHEAD = 2
+AHEAD = 3
+EDGE_MIB = 60
 EDGE_FLOPS = 4 * 10**9
 STAGE_MIB = 46
 F32 = jnp.float32
@@ -87,13 +88,24 @@
     return [near, side, hop(near, 2)]
 
 
-def edges_kernel(x_ref, first_ref, last_ref, top_ref, bottom_ref):
+def edges_kernel(x_ref, first_ref, last_ref, top_ref, bottom_ref, strips, sem):
     rows, cols, _ = x_ref.shape
-    part = 2 * SUBLANES
-    first_ref[...] = x_ref[:, :part].astype(F32)[:, 0].astype(BF16)
-    last_ref[...] = x_ref[:, cols - part:].astype(F32)[:, part - 1].astype(BF16)
-    top_ref[...] = x_ref[0]
-    bottom_ref[...] = x_ref[rows - 1]
+    part = strips.shape[2]
+    copies = [
+        pltpu.make_async_copy(source, target, sem.at[n])
+        for n, (source, target) in enumerate((
+            (x_ref.at[:, :part], strips.at[0]),
+            (x_ref.at[:, cols - part:], strips.at[1]),
+            (x_ref.at[0], top_ref),
+            (x_ref.at[rows - 1], bottom_ref),
+        ))
+    ]
+    for copy in copies:
+        copy.start()
+    for copy in copies:
+        copy.wait()
+    first_ref[...] = strips[0].astype(F32)[:, 0].astype(BF16)
+    last_ref[...] = strips[1].astype(F32)[:, part - 1].astype(BF16)
 
 
 def edges(cells):
@@ -101,9 +113,12 @@
     return pl.pallas_call(
         edges_kernel,
         out_shape=(shape(rows, channels),) * 2 + (shape(cols, channels),) * 2,
-        in_specs=[VMEM],
+        in_specs=[ANY],
         out_specs=(VMEM,) * 4,
-        compiler_params=grant(8),
+        scratch_shapes=[
+            pltpu.VMEM((2, rows, 2 * SUBLANES, channels), BF16), pltpu.SemaphoreType.DMA((4,)),
+        ],
+        compiler_params=grant(EDGE_MIB),
         cost_estimate=cost(EDGE_FLOPS, cells.nbytes),
         name="edges",
     )(cells)

time: 72 us -> 73.2 us (1.017)
  other arithmetic: 0.14 us -> 1.65 us
  local copies, waits for them, and re-layouts: 1.19 us -> 0.22 us
    pallas_call x1, Pallas kernels: 0.04 us -> 1.68 us  [edges(): pl.pallas_call(edges_kernel, out_shape=(shape(rows, channels),) * 2 + (sh...]
    unnamed x21 -> x19, local copies, waits for them, and re-layouts: 1.05 us -> 0.09 us
    select_n x1, other arithmetic: 0.04 us -> 0.84 us  [halo(): jnp.where(odd, low, high)]
  transfers between devices with their start and end apart: 18 -> 18, of which waited for: 6 -> 6; matrix products, arithmetic and copies ran while one was open for 0% -> 0% of each run, Pallas kernels for 26% -> 24%
where the time goes in v6:
time: 73.2 us; the launch traced here: 72.9 us
  Pallas kernels  29.9 us (41%)
  starting transfers between devices  21.8 us (30%)
  waiting for transfers between devices  18.4 us (25%)
  other arithmetic  1.65 us (2%)
  between operations  0.9 us (1%)
    ppermute x9, starting transfers between devices, exchange(): lax.ppermute(block, axis, [(source_of(i, step, count), i) for i in range(...  11.5 us
    ppermute x9, waiting for transfers between devices, exchange(): lax.ppermute(block, axis, [(source_of(i, step, count), i) for i in range(...  11.5 us
    pallas_call x1, Pallas kernels, attend_plane(): pl.pallas_call(functools.partial(plane_kernel, info, len(keys)), out_shap...  6.75 us
    ppermute x2, starting transfers between devices, halo(): lax.ppermute(block, 'prow', pairs + [(j, i) for i, j in pairs])  6.28 us
    pallas_call x1, Pallas kernels, attend_anchors(): pl.pallas_call(functools.partial(anchor_kernel, info, len(keys), len(earl...  5.32 us
    ppermute x3, waiting for transfers between devices, hop(): lax.ppermute(rows, ('prow', 'pcol'), [((p ^ (entry if c % 2 == 0 else 3 -...  5.3 us
    pallas_call x1, Pallas kernels, conv_norm(): pl.pallas_call(functools.partial(conv_kernel, rows, cols, cores), out_sha...  3.93 us
    pallas_call x1, Pallas kernels, attend_own(): pl.pallas_call(functools.partial(own_kernel, info, len(parts)), out_shape...  3.66 us
  transfers between devices with their start and end apart: 18, of which 6 were waited for; matrix products, arithmetic and copies ran while one was open for 0% of the time, Pallas kernels for 24%

profile of v6, /device:TPU:0, one launch (start us, length us, event | category | flops | bytes accessed | tf_op | source)
XLA Modules:
  0.0 72.9 jit_solution(10518286507896131667)
XLA Ops:
  0.6 1.7 %edges.1 = (bf16[8,640]{1,0:T(8,128)(2,1)}, bf16[8,640]{1,0:T(8,128)(2,1)}, bf16[32,640]{1,0:T(8,128)(2,1)}, bf16[32,640]{1,0:T(8,128)(2,1)}) custom-call(bf16[8,32,640]{2,1,0:T(8,128)(2,1)} %bitcast.5), custom_call_target="tpu_custom_call" | custom-call | flops 4000000000 | bytes 327680 | tf_op jit(solution)/shard_map/edges/pallas_call | solution.py:113
  3.5 0.8 %collective-permute-done = bf16[8,640]{1,0:T(8,128)(2,1)S(1)} collective-permute-done((bf16[8,640]{1,0:T(8,128)(2,1)S(1)}, bf16[8,640]{1,0:T(8,128)(2,1)S(1)}, u32[]{:S(2)}, u32[]{:S(2)}) %collective-permute-start) | collective-permute-done | bytes 10272 | tf_op jit(solution)/shard_map/ppermute | solution.py:67
  4.4 0.8 %broadcast_select_fusion.2 = (bf16[34,640]{1,0:T(8,128)(2,1)S(1)}, bf16[34,640]{1,0:T(8,128)(2,1)S(1)}) fusion(pred[]{:T(512)S(6)} %eq.12, bf16[1,640]{1,0:T(2,128)(2,1)S(1)} %get-tuple-element.64, bf16[1,640]{1,0:T(2,128)(2,1)S(1)} %get-tuple-element.59, bf16[32,640]{1,0:T(8,128)(2,1)} %get-tuple-element.31, bf16[1,640]{1,0:T(2,128)(2,1)S(1)} %get-tuple-element.65, ...), kind=kLoop, calls=%fused_computation.4 | loop fusion | flops 304640 | bytes 174081 | tf_op jit(solution)/shard_map/jit(_where)/select_n | solution.py:145
  5.9 5.6 %collective-permute-start.1 = (bf16[34,640]{1,0:T(8,128)(2,1)S(1)}, bf16[34,640]{1,0:T(8,128)(2,1)S(1)}, u32[]{:S(2)}, u32[]{:S(2)}) collective-permute-start(bf16[34,640]{1,0:T(8,128)(2,1)S(1)} %get-tuple-element.57), channel_id=1, source_target_pairs={{0,2},{4,6},{2,0},{6,4},{1,3},{5,7},{3,1},{7,5},{8,10},{12,14},{10... | collective-permute-start | bytes 130568 | tf_op jit(solution)/shard_map/ppermute | solution.py:146
  11.5 3.1 %stage.1.w_ref = bf16[3,3,640,640]{3,2,1,0:T(8,128)(2,1)S(1)} custom-call(bf16[3,3,640,640]{3,2,1,0:T(8,128)(2,1)} %in_ref.1), custom_call_target="tpu_custom_call" | custom-call | bytes 14745600 | tf_op jit(solution)/shard_map/stage/pallas_call | solution.py:159
  14.8 3.9 %conv_norm.1 = (bf16[256,640]{1,0:T(8,128)(2,1)}, bf16[128,640]{1,0:T(8,128)(2,1)S(1)}, bf16[128,640]{1,0:T(8,128)(2,1)S(1)}) custom-call(bf16[256,640]{1,0:T(8,128)(2,1)S(1)} %bitcast.6, bf16[8,640]{1,0:T(8,128)(2,1)S(1)} %get-tuple-element.63.left_ref, bf16[8,640]{1,0:T(8,128)(2,1)S(1)} %get-tuple-element.62.right_ref, ...), custom_call_target="tpu_custom_call" | custom-call | flops 1887436800 | bytes 7372800 | tf_op jit(solution)/shard_map/conv_norm/pallas_call | solution.py:217
  20.1 1.0 %collective-permute-start.14 = (bf16[256,640]{1,0:T(8,128)(2,1)S(1)}, bf16[256,640]{1,0:T(8,128)(2,1)S(1)}, u32[]{:S(2)}, u32[]{:S(2)}) collective-permute-start(bf16[256,640]{1,0:T(8,128)(2,1)S(1)} %constant_dynamic-update-slice_fusion.refs_4_.key_ref), channel_id=1, source_target_pairs={{2,0},{5,1},{0,2},{7,3},{6,4},{1,5},{4,6},{3,7},{10,8},{13,9},{8,1... | collective-permute-start | bytes 983048 | tf_op jit(solution)/shard_map/ppermute | solution.py:82
  21.8 1.2 %collective-permute-start.5 = (bf16[64,640]{1,0:T(8,128)(2,1)S(1)}, bf16[64,640]{1,0:T(8,128)(2,1)S(1)}, u32[]{:S(2)}, u32[]{:S(2)}) collective-permute-start(bf16[64,640]{1,0:T(8,128)(2,1)S(1)} %get-tuple-element.42), channel_id=1, source_target_pairs={{2,0},{0,2},{6,4},{4,6},{3,1},{1,3},{7,5},{5,7},{10,8},{8,10},{14,... | collective-permute-start | bytes 245768 | tf_op jit(solution)/shard_map/ppermute | solution.py:62
  23.0 0.9 %collective-permute-start.6 = (bf16[64,640]{1,0:T(8,128)(2,1)S(1)}, bf16[64,640]{1,0:T(8,128)(2,1)S(1)}, u32[]{:S(2)}, u32[]{:S(2)}) collective-permute-start(bf16[64,640]{1,0:T(8,128)(2,1)S(1)} %get-tuple-element.43), channel_id=1, source_target_pairs={{4,0},{6,2},{0,4},{2,6},{5,1},{7,3},{1,5},{3,7},{12,8},{14,10},{8,... | collective-permute-start | bytes 245768 | tf_op jit(solution)/shard_map/ppermute | solution.py:62
  23.8 1.5 %collective-permute-start.7 = (bf16[64,640]{1,0:T(8,128)(2,1)S(1)}, bf16[64,640]{1,0:T(8,128)(2,1)S(1)}, u32[]{:S(2)}, u32[]{:S(2)}) collective-permute-start(bf16[64,640]{1,0:T(8,128)(2,1)S(1)} %get-tuple-element.44), channel_id=1, source_target_pairs={{6,0},{4,2},{2,4},{0,6},{7,1},{5,3},{3,5},{1,7},{14,8},{12,10},{10... | collective-permute-start | bytes 245768 | tf_op jit(solution)/shard_map/ppermute | solution.py:62
  25.3 5.7 %collective-permute-done.5.refs_1_ = bf16[64,640]{1,0:T(8,128)(2,1)S(1)} collective-permute-done((bf16[64,640]{1,0:T(8,128)(2,1)S(1)}, bf16[64,640]{1,0:T(8,128)(2,1)S(1)}, u32[]{:S(2)}, u32[]{:S(2)}) %collective-permute-start.5) | collective-permute-done | bytes 81952 | tf_op jit(solution)/shard_map/ppermute | solution.py:62
  31.6 1.2 %collective-permute-done.7.refs_3_ = bf16[64,640]{1,0:T(8,128)(2,1)S(1)} collective-permute-done((bf16[64,640]{1,0:T(8,128)(2,1)S(1)}, bf16[64,640]{1,0:T(8,128)(2,1)S(1)}, u32[]{:S(2)}, u32[]{:S(2)}) %collective-permute-start.7) | collective-permute-done | bytes 81952 | tf_op jit(solution)/shard_map/ppermute | solution.py:62
  33.6 1.6 %collective-permute-start.8 = (bf16[64,640]{1,0:T(8,128)(2,1)S(1)}, bf16[64,640]{1,0:T(8,128)(2,1)S(1)}, u32[]{:S(2)}, u32[]{:S(2)}) collective-permute-start(bf16[64,640]{1,0:T(8,128)(2,1)S(1)} %accept.1), channel_id=1, source_target_pairs={{8,0},{0,8},{24,16},{16,24},{9,1},{1,9},{25,17},{17,25},{10,2},{2,... | collective-permute-start | bytes 245768 | tf_op jit(solution)/shard_map/ppermute | solution.py:62
  35.3 3.7 %attend_own.1 = (bf16[640,512]{1,0:T(8,128)(2,1)S(1)}, bf16[640,512]{1,0:T(8,128)(2,1)S(1)}, f32[10,8,512]{2,1,0:T(8,128)S(1)}) custom-call(s32[24]{0:T(128)S(1)} %pad_add_fusion.table_ref, bf16[128,640]{1,0:T(8,128)(2,1)S(1)} %get-tuple-element.38.refs_0_, bf16[128,640]{1,0:T(8,128)(2,1)S(1)} %get-tuple-element.39.refs_1_, ...), custom_call_target="tpu_custom_call" | custom-call | flops 2181038080 | bytes 1638400 | tf_op jit(solution)/shard_map/attend_own/pallas_call | solution.py:350
  38.9 2.5 %collective-permute-start.10 = (bf16[64,640]{1,0:T(8,128)(2,1)S(1)}, bf16[64,640]{1,0:T(8,128)(2,1)S(1)}, u32[]{:S(2)}, u32[]{:S(2)}) collective-permute-start(bf16[64,640]{1,0:T(8,128)(2,1)S(1)} %accept.1), channel_id=1, source_target_pairs={{24,0},{16,8},{8,16},{0,24},{25,1},{17,9},{9,17},{1,25},{26,2},{18... | collective-permute-start | bytes 245768 | tf_op jit(solution)/shard_map/ppermute | solution.py:62
  41.7 1.4 %collective-permute-start.16 = (bf16[256,640]{1,0:T(8,128)(2,1)S(1)}, bf16[256,640]{1,0:T(8,128)(2,1)S(1)}, u32[]{:S(2)}, u32[]{:S(2)}) collective-permute-start(bf16[256,640]{1,0:T(8,128)(2,1)S(1)} %collective-permute-done.14.refs_0_), channel_id=1, source_target_pairs={{4,0},{3,1},{6,2},{1,3},{0,4},{7,5},{2,6},{5,7},{12,8},{11,9},{14,... | collective-permute-start | bytes 983048 | tf_op jit(solution)/shard_map/ppermute | solution.py:82
  43.1 4.6 %collective-permute-done.9 = bf16[64,640]{1,0:T(8,128)(2,1)S(1)} collective-permute-done((bf16[64,640]{1,0:T(8,128)(2,1)S(1)}, bf16[64,640]{1,0:T(8,128)(2,1)S(1)}, u32[]{:S(2)}, u32[]{:S(2)}) %collective-permute-start.9) | collective-permute-done | bytes 81952 | tf_op jit(solution)/shard_map/ppermute | solution.py:62
  47.7 1.6 %collective-permute-start.13 = (bf16[192,640]{1,0:T(8,128)(2,1)S(1)}, bf16[192,640]{1,0:T(8,128)(2,1)S(1)}, u32[]{:S(2)}, u32[]{:S(2)}) collective-permute-start(bf16[192,640]{1,0:T(8,128)(2,1)S(1)} %constant_dynamic-update-slice_fusion.2.refs_0_), channel_id=1, source_target_pairs={{6,0},{4,2},{2,4},{0,6},{7,1},{5,3},{3,5},{1,7},{14,8},{12,10},{10... | collective-permute-start | bytes 737288 | tf_op jit(solution)/shard_map/ppermute | solution.py:62
  49.4 1.3 %collective-permute-start.12 = (bf16[192,640]{1,0:T(8,128)(2,1)S(1)}, bf16[192,640]{1,0:T(8,128)(2,1)S(1)}, u32[]{:S(2)}, u32[]{:S(2)}) collective-permute-start(bf16[192,640]{1,0:T(8,128)(2,1)S(1)} %constant_dynamic-update-slice_fusion.2.refs_0_), channel_id=1, source_target_pairs={{4,0},{6,2},{0,4},{2,6},{5,1},{7,3},{1,5},{3,7},{12,8},{14,10},{8,... | collective-permute-start | bytes 737288 | tf_op jit(solution)/shard_map/ppermute | solution.py:62
  51.3 5.3 %collective-permute-done.16.refs_2_ = bf16[256,640]{1,0:T(8,128)(2,1)S(1)} collective-permute-done((bf16[256,640]{1,0:T(8,128)(2,1)S(1)}, bf16[256,640]{1,0:T(8,128)(2,1)S(1)}, u32[]{:S(2)}, u32[]{:S(2)}) %collective-permute-start.16) | collective-permute-done | bytes 327712 | tf_op jit(solution)/shard_map/ppermute | solution.py:82
  56.6 6.7 %attend_plane.1 = (bf16[640,512]{1,0:T(8,128)(2,1)S(1)}, f32[10,8,512]{2,1,0:T(8,128)S(1)}) custom-call(s32[24]{0:T(128)S(1)} %pad_add_fusion.table_ref, bf16[640,512]{1,0:T(8,128)(2,1)S(1)} %get-tuple-element.40.q_ref, bf16[256,640]{1,0:T(8,128)(2,1)S(1)} %collective-permute-done.14.refs_0_, bf16[256,640]{1,0:T(8,128)(2,1)S(1)} %collective-permute-done.15.refs_1_, ...), custom_call_target="tpu_custom_call" | custom-call | flops 5284823040 | bytes 2293760 | tf_op jit(solution)/shard_map/attend_plane/pallas_call | solution.py:382
  63.4 5.3 %attend_anchors.1 = (bf16[5,768,128]{2,1,0:T(8,128)(2,1)S(1)}, bf16[10,80,768]{2,1,0:T(8,128)(2,1)S(1)}, bf16[688,256]{1,0:T(8,128)(2,1)S(1)}) custom-call(s32[24]{0:T(128)S(1)} %pad_add_fusion.table_ref, bf16[640,512]{1,0:T(8,128)(2,1)S(1)} %get-tuple-element.40.q_ref, bf16[192,640]{1,0:T(8,128)(2,1)S(1)} %constant_dynamic-update-slice_fusion.2.refs_0_, ...), custom_call_target="tpu_custom_call" | custom-call | flops 5284823040 | bytes 2293760 | tf_op jit(solution)/shard_map/attend_anchors/pallas_call | solution.py:466
  68.8 2.8 %attend_anchors_own.1 = (bf16[640,256]{1,0:T(8,128)(2,1)S(1)}, f32[16,256]{1,0:T(8,128)S(1)}) custom-call(bf16[640,512]{1,0:T(8,128)(2,1)S(1)} %get-tuple-element.40.q_ref, bf16[5,768,128]{2,1,0:T(8,128)(2,1)S(1)} %get-tuple-element.49.k_ref, bf16[10,80,768]{2,1,0:T(8,128)(2,1)S(1)} %get-tuple-element.50.v_ref, ...), custom_call_target="tpu_custom_call" | custom-call | flops 3271557120 | bytes 1638400 | tf_op jit(solution)/shard_map/attend_anchors_own/pallas_call | solution.py:492
  71.6 1.3 %finish.1 = bf16[256,640]{1,0:T(8,128)(2,1)} custom-call(bf16[640,256]{1,0:T(8,128)(2,1)S(1)} %get-tuple-element.51.own_ref, f32[16,256]{1,0:T(8,128)S(1)} %get-tuple-element.52.level_ref, bf16[688,256]{1,0:T(8,128)(2,1)S(1)} %collective-permute-done.17.refs_0_, bf16[640,640]{1,0:T(8,128)(2,1)S(1)} %copy-done), custom_call_target="tpu_custom_call" | custom-call | flops 209715200 | bytes 1802240 | tf_op jit(solution)/shard_map/finish/pallas_call | solution.py:539
  (50 shorter events, 6.4 us)
Async XLA Ops:
  3.0 1.3 %collective-permute-start = (bf16[8,640]{1,0:T(8,128)(2,1)S(1)}, bf16[8,640]{1,0:T(8,128)(2,1)S(1)}, u32[]{:S(2)}, u32[]{:S(2)}) collective-permute-start(bf16[8,640]{1,0:T(8,128)(2,1)S(1)} %broadcast_select_fusion.5), channel_id=1, source_target_pairs={{1,0},{0,1},{3,2},{2,3},{5,4},{4,5},{7,6},{6,7},{9,8},{8,9},{11,10... | collective-permute-start | bytes 30728 | tf_op jit(solution)/shard_map/ppermute | solution.py:67
  5.2 9.5 %collective-permute-start.2 = (bf16[34,640]{1,0:T(8,128)(2,1)S(1)}, bf16[34,640]{1,0:T(8,128)(2,1)S(1)}, u32[]{:S(2)}, u32[]{:S(2)}) collective-permute-start(bf16[34,640]{1,0:T(8,128)(2,1)S(1)} %get-tuple-element.56), channel_id=1, source_target_pairs={{2,4},{4,2},{3,5},{5,3},{10,12},{12,10},{11,13},{13,11},{18,20},{2... | collective-permute-start | bytes 130568 | tf_op jit(solution)/shard_map/ppermute | solution.py:146
  5.9 8.9 %copy-start.1 = (bf16[1,8,32,640]{3,2,1,0:T(8,128)(2,1)S(1)}, bf16[1,8,32,640]{3,2,1,0:T(8,128)(2,1)}, u32[]{:S(2)}) copy-start(bf16[1,8,32,640]{3,2,1,0:T(8,128)(2,1)} %param.9) | copy-start | bytes 983044
  5.9 8.8 %collective-permute-start.1 = (bf16[34,640]{1,0:T(8,128)(2,1)S(1)}, bf16[34,640]{1,0:T(8,128)(2,1)S(1)}, u32[]{:S(2)}, u32[]{:S(2)}) collective-permute-start(bf16[34,640]{1,0:T(8,128)(2,1)S(1)} %get-tuple-element.57), channel_id=1, source_target_pairs={{0,2},{4,6},{2,0},{6,4},{1,3},{5,7},{3,1},{7,5},{8,10},{12,14},{10... | collective-permute-start | bytes 130568 | tf_op jit(solution)/shard_map/ppermute | solution.py:146
  14.7 6.4 %copy-start.6 = (s32[4]{0:T(128)S(1)}, s32[4]{0:T(128)}, u32[]{:S(2)}) copy-start(s32[4]{0:T(128)} %param.17) | copy-start | bytes 52
  14.7 6.4 %copy-start.7 = (s32[4]{0:T(128)S(1)}, s32[4]{0:T(128)}, u32[]{:S(2)}) copy-start(s32[4]{0:T(128)} %param.15) | copy-start | bytes 52
  14.7 20.6 %copy-start.2 = (bf16[640,640]{1,0:T(8,128)(2,1)S(1)}, bf16[640,640]{1,0:T(8,128)(2,1)}, u32[]{:S(2)}) copy-start(bf16[640,640]{1,0:T(8,128)(2,1)} %refs_5_.1) | copy-start | bytes 2457604
  14.7 20.6 %copy-start.3 = (bf16[640,640]{1,0:T(8,128)(2,1)S(1)}, bf16[640,640]{1,0:T(8,128)(2,1)}, u32[]{:S(2)}) copy-start(bf16[640,640]{1,0:T(8,128)(2,1)} %refs_8_.1) | copy-start | bytes 2457604
  14.7 20.6 %copy-start.4 = (bf16[640,640]{1,0:T(8,128)(2,1)S(1)}, bf16[640,640]{1,0:T(8,128)(2,1)}, u32[]{:S(2)}) copy-start(bf16[640,640]{1,0:T(8,128)(2,1)} %refs_9_.1) | copy-start | bytes 2457604
  18.7 1.4 %collective-permute-start.4 = (bf16[128,640]{1,0:T(8,128)(2,1)S(1)}, bf16[128,640]{1,0:T(8,128)(2,1)S(1)}, u32[]{:S(2)}, u32[]{:S(2)}) collective-permute-start(bf16[128,640]{1,0:T(8,128)(2,1)S(1)} %get-tuple-element.39.refs_1_), channel_id=1, source_target_pairs={{1,0},{0,1},{3,2},{2,3},{5,4},{4,5},{7,6},{6,7},{9,8},{8,9},{11,10... | collective-permute-start | bytes 491528 | tf_op jit(solution)/shard_map/ppermute | solution.py:67
  18.8 16.5 %collective-permute-start.3 = (bf16[128,640]{1,0:T(8,128)(2,1)S(1)}, bf16[128,640]{1,0:T(8,128)(2,1)S(1)}, u32[]{:S(2)}, u32[]{:S(2)}) collective-permute-start(bf16[128,640]{1,0:T(8,128)(2,1)S(1)} %get-tuple-element.38.refs_0_), channel_id=1, source_target_pairs={{1,0},{0,1},{3,2},{2,3},{5,4},{4,5},{7,6},{6,7},{9,8},{8,9},{11,10... | collective-permute-start | bytes 491528 | tf_op jit(solution)/shard_map/ppermute | solution.py:67
  20.1 21.6 %collective-permute-start.14 = (bf16[256,640]{1,0:T(8,128)(2,1)S(1)}, bf16[256,640]{1,0:T(8,128)(2,1)S(1)}, u32[]{:S(2)}, u32[]{:S(2)}) collective-permute-start(bf16[256,640]{1,0:T(8,128)(2,1)S(1)} %constant_dynamic-update-slice_fusion.refs_4_.key_ref), channel_id=1, source_target_pairs={{2,0},{5,1},{0,2},{7,3},{6,4},{1,5},{4,6},{3,7},{10,8},{13,9},{8,1... | collective-permute-start | bytes 983048 | tf_op jit(solution)/shard_map/ppermute | solution.py:82
  21.8 9.3 %collective-permute-start.5 = (bf16[64,640]{1,0:T(8,128)(2,1)S(1)}, bf16[64,640]{1,0:T(8,128)(2,1)S(1)}, u32[]{:S(2)}, u32[]{:S(2)}) collective-permute-start(bf16[64,640]{1,0:T(8,128)(2,1)S(1)} %get-tuple-element.42), channel_id=1, source_target_pairs={{2,0},{0,2},{6,4},{4,6},{3,1},{1,3},{7,5},{5,7},{10,8},{8,10},{14,... | collective-permute-start | bytes 245768 | tf_op jit(solution)/shard_map/ppermute | solution.py:62
  23.0 8.7 %collective-permute-start.6 = (bf16[64,640]{1,0:T(8,128)(2,1)S(1)}, bf16[64,640]{1,0:T(8,128)(2,1)S(1)}, u32[]{:S(2)}, u32[]{:S(2)}) collective-permute-start(bf16[64,640]{1,0:T(8,128)(2,1)S(1)} %get-tuple-element.43), channel_id=1, source_target_pairs={{4,0},{6,2},{0,4},{2,6},{5,1},{7,3},{1,5},{3,7},{12,8},{14,10},{8,... | collective-permute-start | bytes 245768 | tf_op jit(solution)/shard_map/ppermute | solution.py:62
  23.8 9.0 %collective-permute-start.7 = (bf16[64,640]{1,0:T(8,128)(2,1)S(1)}, bf16[64,640]{1,0:T(8,128)(2,1)S(1)}, u32[]{:S(2)}, u32[]{:S(2)}) collective-permute-start(bf16[64,640]{1,0:T(8,128)(2,1)S(1)} %get-tuple-element.44), channel_id=1, source_target_pairs={{6,0},{4,2},{2,4},{0,6},{7,1},{5,3},{3,5},{1,7},{14,8},{12,10},{10... | collective-permute-start | bytes 245768 | tf_op jit(solution)/shard_map/ppermute | solution.py:62
  31.0 20.3 %collective-permute-start.15 = (bf16[256,640]{1,0:T(8,128)(2,1)S(1)}, bf16[256,640]{1,0:T(8,128)(2,1)S(1)}, u32[]{:S(2)}, u32[]{:S(2)}) collective-permute-start(bf16[256,640]{1,0:T(8,128)(2,1)S(1)} %constant_dynamic-update-slice_fusion.refs_4_.key_ref), channel_id=1, source_target_pairs={{4,0},{3,1},{6,2},{1,3},{0,4},{7,5},{2,6},{5,7},{12,8},{11,9},{14,... | collective-permute-start | bytes 983048 | tf_op jit(solution)/shard_map/ppermute | solution.py:82
  33.6 9.5 %collective-permute-start.8 = (bf16[64,640]{1,0:T(8,128)(2,1)S(1)}, bf16[64,640]{1,0:T(8,128)(2,1)S(1)}, u32[]{:S(2)}, u32[]{:S(2)}) collective-permute-start(bf16[64,640]{1,0:T(8,128)(2,1)S(1)} %accept.1), channel_id=1, source_target_pairs={{8,0},{0,8},{24,16},{16,24},{9,1},{1,9},{25,17},{17,25},{10,2},{2,... | collective-permute-start | bytes 245768 | tf_op jit(solution)/shard_map/ppermute | solution.py:62
  38.9 8.8 %collective-permute-start.10 = (bf16[64,640]{1,0:T(8,128)(2,1)S(1)}, bf16[64,640]{1,0:T(8,128)(2,1)S(1)}, u32[]{:S(2)}, u32[]{:S(2)}) collective-permute-start(bf16[64,640]{1,0:T(8,128)(2,1)S(1)} %accept.1), channel_id=1, source_target_pairs={{24,0},{16,8},{8,16},{0,24},{25,1},{17,9},{9,17},{1,25},{26,2},{18... | collective-permute-start | bytes 245768 | tf_op jit(solution)/shard_map/ppermute | solution.py:62
  41.5 6.2 %collective-permute-start.9 = (bf16[64,640]{1,0:T(8,128)(2,1)S(1)}, bf16[64,640]{1,0:T(8,128)(2,1)S(1)}, u32[]{:S(2)}, u32[]{:S(2)}) collective-permute-start(bf16[64,640]{1,0:T(8,128)(2,1)S(1)} %accept.1), channel_id=1, source_target_pairs={{16,0},{24,8},{0,16},{8,24},{17,1},{25,9},{1,17},{9,25},{18,2},{26... | collective-permute-start | bytes 245768 | tf_op jit(solution)/shard_map/ppermute | solution.py:62
  41.7 14.9 %collective-permute-start.16 = (bf16[256,640]{1,0:T(8,128)(2,1)S(1)}, bf16[256,640]{1,0:T(8,128)(2,1)S(1)}, u32[]{:S(2)}, u32[]{:S(2)}) collective-permute-start(bf16[256,640]{1,0:T(8,128)(2,1)S(1)} %collective-permute-done.14.refs_0_), channel_id=1, source_target_pairs={{4,0},{3,1},{6,2},{1,3},{0,4},{7,5},{2,6},{5,7},{12,8},{11,9},{14,... | collective-permute-start | bytes 983048 | tf_op jit(solution)/shard_map/ppermute | solution.py:82
  47.7 15.6 %collective-permute-start.13 = (bf16[192,640]{1,0:T(8,128)(2,1)S(1)}, bf16[192,640]{1,0:T(8,128)(2,1)S(1)}, u32[]{:S(2)}, u32[]{:S(2)}) collective-permute-start(bf16[192,640]{1,0:T(8,128)(2,1)S(1)} %constant_dynamic-update-slice_fusion.2.refs_0_), channel_id=1, source_target_pairs={{6,0},{4,2},{2,4},{0,6},{7,1},{5,3},{3,5},{1,7},{14,8},{12,10},{10... | collective-permute-start | bytes 737288 | tf_op jit(solution)/shard_map/ppermute | solution.py:62
  49.4 14.0 %collective-permute-start.12 = (bf16[192,640]{1,0:T(8,128)(2,1)S(1)}, bf16[192,640]{1,0:T(8,128)(2,1)S(1)}, u32[]{:S(2)}, u32[]{:S(2)}) collective-permute-start(bf16[192,640]{1,0:T(8,128)(2,1)S(1)} %constant_dynamic-update-slice_fusion.2.refs_0_), channel_id=1, source_target_pairs={{4,0},{6,2},{0,4},{2,6},{5,1},{7,3},{1,5},{3,7},{12,8},{14,10},{8,... | collective-permute-start | bytes 737288 | tf_op jit(solution)/shard_map/ppermute | solution.py:62
  50.6 12.8 %collective-permute-start.11 = (bf16[192,640]{1,0:T(8,128)(2,1)S(1)}, bf16[192,640]{1,0:T(8,128)(2,1)S(1)}, u32[]{:S(2)}, u32[]{:S(2)}) collective-permute-start(bf16[192,640]{1,0:T(8,128)(2,1)S(1)} %constant_dynamic-update-slice_fusion.2.refs_0_), channel_id=1, source_target_pairs={{2,0},{0,2},{6,4},{4,6},{3,1},{1,3},{7,5},{5,7},{10,8},{8,10},{14,... | collective-permute-start | bytes 737288 | tf_op jit(solution)/shard_map/ppermute | solution.py:62
  68.7 2.9 %collective-permute-start.17 = (bf16[688,256]{1,0:T(8,128)(2,1)S(1)}, bf16[688,256]{1,0:T(8,128)(2,1)S(1)}, u32[]{:S(2)}, u32[]{:S(2)}) collective-permute-start(bf16[688,256]{1,0:T(8,128)(2,1)S(1)} %get-tuple-element.53), channel_id=1, source_target_pairs={{1,0},{0,1},{3,2},{2,3},{5,4},{4,5},{7,6},{6,7},{9,8},{8,9},{11,10... | collective-permute-start | bytes 1056776 | tf_op jit(solution)/shard_map/ppermute | solution.py:67
  (2 other events, 7.0 us)
